TPU v7x, 32 devices: a whole 2x2x4 slice. The times are simulated.
32 devices in a mesh: dp: 8 (over z, x), tensor: 4 (over y, core).
Axes of the slice: x: 2, y: 2, z: 4, core: 2. Of those that a mesh axis runs over, the one named last changes fastest.
Arguments:
- layer_in: bfloat16 [1024, 8, 1024], P('tensor', 'dp'), may hold values from -6 to 6
- out_grad: bfloat16 [1024, 8, 1024], P('tensor', 'dp'), may hold values from -6 to 6
- lengths: int32 [8], P('dp'), may hold values from 512 to 1024, as said below
- mamba_x: float32 [1024, 1536], P('dp', 'tensor'), may hold values from -0.1875 to 0.1875
- mamba_z: float32 [1024, 1536], P('dp', 'tensor'), may hold values from -0.1875 to 0.1875
- mamba_step: float32 [1024, 24], P('dp', 'tensor'), may hold values from -0.1875 to 0.1875
- query_proj: float32 [1024, 512], P('dp', 'tensor'), may hold values from -0.25 to 0.25
- key_proj: float32 [1024, 256], P('dp', 'tensor'), may hold values from -0.25 to 0.25
- value_proj: float32 [1024, 256], P('dp', 'tensor'), may hold values from -0.1875 to 0.1875
- mamba_out: float32 [1536, 1024], P('tensor', 'dp'), may hold values from -0.15625 to 0.15625
- attend_out: float32 [512, 1024], P('tensor', 'dp'), may hold values from -3 to 3
- mlp_gate: float32 [1024, 2048], P('dp', 'tensor'), may hold values from -0.1875 to 0.1875
- mlp_up: float32 [1024, 2048], P('dp', 'tensor'), may hold values from -0.1875 to 0.1875
- mlp_down: float32 [2048, 1024], P('tensor', 'dp'), may hold values from -0.125 to 0.125
- state_proj: float32 [1024, 256], P(('dp', 'tensor')), may hold values from -0.1875 to 0.1875
- conv_state: float32 [5, 256], P(None, ('dp', 'tensor')), may hold values from -3 to 3
- norm_gains: float32 [2, 1024], P(None, ('dp', 'tensor')), may hold values from 0.5 to 1.5
- conv_mamba: float32 [5, 1536], P(None, 'tensor'), may hold values from -3 to 3
- step_bias: float32 [24], P('tensor'), may hold values from -3 to -0.5
- decay_log: float32 [24], P('tensor'), may hold values from -4 to 1
- skip_gain: float32 [24], P('tensor'), may hold values from 0.5 to 1.5
Outputs:
- layer_out: bfloat16 [1024, 8, 1024], P('tensor', 'dp')
- in_grad: bfloat16 [1024, 8, 1024], P('tensor', 'dp')
- mamba_x_grad: float32 [1024, 1536], P('dp', 'tensor')
- mamba_z_grad: float32 [1024, 1536], P('dp', 'tensor')
- mamba_step_grad: float32 [1024, 24], P('dp', 'tensor')
- query_proj_grad: float32 [1024, 512], P('dp', 'tensor')
- key_proj_grad: float32 [1024, 256], P('dp', 'tensor')
- value_proj_grad: float32 [1024, 256], P('dp', 'tensor')
- mamba_out_grad: float32 [1536, 1024], P('tensor', 'dp')
- attend_out_grad: float32 [512, 1024], P('tensor', 'dp')
- mlp_gate_grad: float32 [1024, 2048], P('dp', 'tensor')
- mlp_up_grad: float32 [1024, 2048], P('dp', 'tensor')
- mlp_down_grad: float32 [2048, 1024], P('tensor', 'dp')
- state_proj_grad: float32 [1024, 256], P(('dp', 'tensor'))
- conv_state_grad: float32 [5, 256], P(None, ('dp', 'tensor'))
- norm_gains_grad: float32 [2, 1024], P(None, ('dp', 'tensor'))
- conv_mamba_grad: float32 [5, 1536], P(None, 'tensor')
- step_bias_grad: float32 [24], P('tensor')
- decay_log_grad: float32 [24], P('tensor')
- skip_gain_grad: float32 [24], P('tensor')
Inputs may be any that keep to these rules, and one draw needn't show every extreme that they name: `lengths`: the valid tokens of a sequence are its first ones; in every draw one sequence has exactly 1024 and another exactly half of 1024.
All inputs are finite; a program needn't handle non-finite values.
Results may differ from a plain program's by a relative error of at most 0.019.
Values may be sent and summed in bfloat16 or wider, within the bound.
No kernel may reach another device: no remote copies, remote signals or barrier semaphores. Data moves between devices by JAX's collectives and lax.ppermute only.
A program may use at most 128 MiB of HBM per device.

v0:
```python
import functools

import jax
import jax.numpy as jnp
from jax import lax
from jax.experimental import pallas as pl
from jax.experimental.pallas import tpu as pltpu
from jax.sharding import PartitionSpec as P

epsilon = 1e-05
rotary_base = 100000000000.0
HIGHEST = lax.Precision.HIGHEST
bf16 = jnp.bfloat16
f32 = jnp.float32


def flip(value, axis, mask):
    size = lax.axis_size(axis)
    return lax.ppermute(value, axis, [(i, i ^ mask) for i in range(size)])


def bits_of(size):
    bits = size.bit_length() - 1
    assert size == 1 << bits
    return bits


def relative_order(size):
    order = [0]
    for bit in reversed(range(bits_of(size))):
        order = order + [k | (1 << bit) for k in order]
    return order


def join_quarters(quarters):
    count = quarters[0][0].shape[0]
    return jnp.concatenate(
        [item[k * count : (k + 1) * count] for item, k in quarters], axis=0
    )


def quarter_specs(quarters):
    count, cols = quarters[0][0].shape
    return [
        pl.BlockSpec((count, cols), lambda i, r, block=block: (block, 0)) for _, block in quarters
    ]


def arrays_of(quarters):
    return [array for array, _ in quarters]


class Gather:
    def __init__(self, own, axis, swap, split=False):
        self.axis, self.swap, self.split = axis, swap, split
        order = list(reversed(range(bits_of(lax.axis_size(axis)))))
        if swap:
            order[-2:] = [0, 1]
        self.order, self.held = order, own
        self.send()

    def send(self):
        self.got = flip(self.held, self.axis, 1 << self.order[0])
        if self.split and len(self.order) == 2:
            self.cross = flip(self.held, self.axis, 1 << self.order[1])

    def advance(self, *others):
        got = after(self.got, *others) if others else self.got
        left = len(self.order)
        self.order = self.order[1:]
        if left > 2:
            self.held = jnp.concatenate([self.held, got], axis=0)
            self.send()
            return self.held
        if left == 2:
            self.near = got
            sent = got if self.split else jnp.concatenate([self.held, got], axis=0)
            self.got = flip(sent, self.axis, 1 << self.order[0])
            return sent
        cross, last = ((self.cross, 0), (got, 0)) if self.split else ((got, 0), (got, 1))
        one, two = (cross, (self.near, 0)) if self.swap else ((self.near, 0), cross)
        return [(self.held, 0), one, two, last]

    def until(self, left, *others):
        while len(self.order) > left:
            both = self.advance(*others)
        return both


class Sum:
    def __init__(self, kept, sent, axis, swap):
        order = list(range(bits_of(lax.axis_size(axis))))
        if swap:
            order[:2] = [1, 0]
        self.order, self.kept, self.axis = order, kept, axis
        self.got = flip(sent, axis, 1 << order[0])

    def advance(self, *others):
        got = after(self.got, *others) if others else self.got
        self.order = self.order[1:]
        if not self.order:
            return self.kept + got.astype(f32)
        half = got.shape[0] // 2
        sent = (self.kept[half:] + got[half:].astype(f32)).astype(bf16)
        self.kept = self.kept[:half] + got[:half].astype(f32)
        self.got = flip(sent, self.axis, 1 << self.order[0])
        return sent

    def finish(self, *others):
        while self.order:
            total = self.advance(*others)
        return total


def product_kernel(groups, rank, *refs):
    kept, sent = refs[-2:]
    step = pl.program_id(0)
    first, at = 0, 0
    for pairs, widths in groups:
        per = 1 + len(widths)
        for j, width in enumerate(widths):
            total = 0.0
            for p in range(pairs):
                left, right = refs[first + p * per], refs[first + p * per + 1 + j]
                total = total + dot_tn(left[...], right[...])
            cols = slice(at, at + width)
            at += width

            @pl.when(step < 2)
            def _(total=total, cols=cols):
                sent[:, cols] = total.astype(bf16)

            @pl.when(step >= 2)
            def _(total=total, cols=cols):
                kept[:, cols] = total

        first += pairs * per


def product(token, groups, swap):
    width = groups[0][0][0].shape[1]
    quarter = width // 4

    def place(i):
        return (2 * i + 1) % 5 if swap else (i + 2) % 4

    specs, operands, shapes, total, flops = [], [], [], 0, 0
    for pairs in groups:
        widths = [array.shape[1] for array, _ in pairs[0][1]]
        shapes.append((len(pairs), widths))
        total += sum(widths)
        for left, rights in pairs:
            lines = left.shape[0]
            flops += 2 * lines * width * sum(widths)
            specs.append(pl.BlockSpec((lines, quarter), lambda i, r: (0, place(i))))
            operands.append(left)
            for array, block in rights:
                specs.append(
                    pl.BlockSpec((lines, array.shape[1]), lambda i, r, block=block: (block, 0))
                )
                operands.append(array)
    return pl.pallas_call(
        functools.partial(product_kernel, shapes),
        grid_spec=pltpu.PrefetchScalarGridSpec(
            num_scalar_prefetch=1,
            grid=(4,),
            in_specs=specs,
            out_specs=[
                pl.BlockSpec((quarter, total), lambda i, r: (jnp.maximum(i - 2, 0), 0)),
                pl.BlockSpec((quarter, total), lambda i, r: (jnp.minimum(i, 1), 0)),
            ],
        ),
        out_shape=[
            jax.ShapeDtypeStruct((2 * quarter, total), f32),
            jax.ShapeDtypeStruct((2 * quarter, total), bf16),
        ],
        cost_estimate=cost(flops, 8 * width * total, 0),
        name="weight_product",
    )(token, *operands)


def pack_kernel(chans, x, step, z, q, k, v, pack_x, pack_z):
    pack_x[:, :chans] = x[...].astype(bf16)
    pack_x[:, chans:] = jnp.zeros((x.shape[0], 128), bf16)
    pack_x[:, chans : chans + step.shape[1]] = step[...].astype(bf16)
    pack_z[:, :chans] = z[...].astype(bf16)
    pack_z[:, chans : chans + q.shape[1]] = q[...].astype(bf16)
    both = jnp.concatenate([k[...], v[...]], axis=1)
    pack_z[:, chans + q.shape[1] :] = both.astype(bf16)


def pack_early(x, step, z, q, k, v):
    lines, chans = x.shape
    cols = chans + q.shape[1] + k.shape[1] + v.shape[1]
    return pl.pallas_call(
        functools.partial(pack_kernel, chans),
        out_shape=[
            jax.ShapeDtypeStruct((lines, chans + 128), bf16),
            jax.ShapeDtypeStruct((lines, cols), bf16),
        ],
        cost_estimate=cost(0, lines * 7000, 0),
        name="pack_weights",
    )(x, step, z, q, k, v)


def move_kernel(back, order, me, source, target):
    width = source.shape[1] // len(order)
    for p, k in enumerate(order):
        there = pl.ds(pl.multiple_of((me[0] ^ k) * width, width), width)
        here = slice(p * width, (p + 1) * width)
        if back:
            target[:, there] = source[:, here]
        else:
            target[:, here] = source[:, there]


def final_kernel(order, me, u_own, u_other, gain, source, g_r1, target):
    width = source.shape[1] // len(order)
    step = 32
    for i in range(source.shape[0] // step):
        rows = slice(i * step, (i + 1) * step)
        x = source[rows].astype(f32)
        e = (u_own[rows].astype(f32) + u_other[rows].astype(f32)) * gain[...]
        rho = lax.rsqrt(jnp.mean(x * x, axis=1, keepdims=True) + epsilon)
        n = x * rho
        inner = jnp.mean(e * n, axis=1, keepdims=True)
        out = (g_r1[rows] + rho * (e - n * inner)).astype(bf16)
        for p, k in enumerate(order):
            there = pl.ds(pl.multiple_of((me[0] ^ k) * width, width), width)
            target[rows, there] = out[:, p * width : (p + 1) * width]


def final_gradient(member, size, u02, u_other, gain, x02, g_r1):
    shape = u_other.shape
    moved = shape[1] // size % 128 == 0
    result = pl.pallas_call(
        functools.partial(final_kernel, relative_order(size) if moved else [0]),
        grid_spec=pltpu.PrefetchScalarGridSpec(
            num_scalar_prefetch=1,
            grid=(1,),
            in_specs=[whole(shape), whole(shape), whole((1, shape[1])), whole(shape), whole(shape)],
            out_specs=whole(shape),
        ),
        out_shape=jax.ShapeDtypeStruct(shape, bf16),
        cost_estimate=cost(10**7, 10**7, 0),
        name="input_gradient",
    )(
        member.reshape(1) if moved else jnp.zeros((1,), jnp.int32),
        u02, u_other, gain.reshape(1, -1), x02, g_r1,
    )
    return result if moved else take_blocks(result, member, size, True)


def move_blocks(value, member, size, back):
    width = value.shape[1] // size
    if width % 128 == 0:
        return pl.pallas_call(
            functools.partial(move_kernel, back, relative_order(size)),
            grid_spec=pltpu.PrefetchScalarGridSpec(
                num_scalar_prefetch=1,
                grid=(1,),
                in_specs=[whole(value.shape)],
                out_specs=whole(value.shape),
            ),
            out_shape=jax.ShapeDtypeStruct(value.shape, value.dtype),
            cost_estimate=cost(0, 2 * value.size * value.dtype.itemsize, 0),
            name="move_blocks",
        )(member.reshape(1), value)
    return take_blocks(value, member, size, back)


def take_blocks(value, member, size, back):
    order = relative_order(size)
    where = [0] * size
    for p, k in enumerate(order):
        where[k] = p
    if back:
        index = jnp.array(where, jnp.int32)[member ^ jnp.arange(size, dtype=jnp.int32)]
    else:
        index = member ^ jnp.array(order, jnp.int32)
    cut = value.reshape(value.shape[0], size, -1)
    return jnp.take(cut, index, axis=1).reshape(value.shape)


def pick(bit, one, zero):
    return jnp.where(bit == 1, one, zero)


def after(value, *others):
    return lax.optimization_barrier((value,) + others)[0]


def flip_core(value):
    return flip(value, "tensor", 1)


def flip_y(value):
    return flip(value, "tensor", 2)


def in_rank_order(own, y, core):
    other = flip_y(own)
    pair = jnp.stack([pick(y, other, own), pick(y, own, other)])
    other = flip_core(pair)
    both = jnp.stack([pick(core, other, pair), pick(core, pair, other)], axis=1)
    return both.reshape((4,) + own.shape)


def add_low(kept, got):
    return lax.optimization_barrier((kept.astype(f32) + got.astype(f32)).astype(bf16))


def core_sum(kept, sent):
    return add_low(kept, flip_core(sent.astype(bf16)))


def y_sum(kept, sent):
    return kept.astype(f32) + flip_y(sent).astype(f32)


CHUNK = 128
HEAD = 64
TAPS = 4


def dot_nn(a, b):
    return lax.dot_general(a, b, (((1,), (0,)), ((), ())), preferred_element_type=f32)


def dot_nt(a, b):
    return lax.dot_general(a, b, (((1,), (1,)), ((), ())), preferred_element_type=f32)


def dot_tn(a, b):
    return lax.dot_general(a, b, (((0,), (0,)), ((), ())), preferred_element_type=f32)


def dot_exact(a, b):
    return lax.dot_general(
        a, b, (((1,), (0,)), ((), ())), precision=HIGHEST, preferred_element_type=f32
    )


def iota(shape, axis):
    return lax.broadcasted_iota(jnp.int32, shape, axis)


def earlier(tail, block, back):
    if back == 0:
        return block
    return pltpu.roll(jnp.concatenate([tail, block], axis=0), back, 0)[8:]


def later(block, head, ahead):
    if ahead == 0:
        return block
    both = jnp.concatenate([block, head], axis=0)
    return pltpu.roll(both, both.shape[0] - ahead, 0)[: block.shape[0]]


def conv_rows(tail, block, taps):
    total = block * taps[TAPS - 1 : TAPS] + taps[TAPS : TAPS + 1]
    for j in range(TAPS - 1):
        total = total + earlier(tail, block, TAPS - 1 - j) * taps[j : j + 1]
    return total


def conv_rows_back(grad, head, taps):
    total = grad * taps[TAPS - 1 : TAPS]
    for j in range(TAPS - 1):
        total = total + later(grad, head, TAPS - 1 - j) * taps[j : j + 1]
    return total


def conv_taps_back(tail, block, grad):
    rows = [
        jnp.sum(earlier(tail, block, TAPS - 1 - j) * grad, axis=0, keepdims=True)
        for j in range(TAPS)
    ]
    rows.append(jnp.sum(grad, axis=0, keepdims=True))
    rows.append(jnp.zeros((8 - len(rows), grad.shape[1]), f32))
    return jnp.concatenate(rows, axis=0)


def head_columns(columns, heads):
    rows = columns.shape[0]
    low = iota((rows, 2 * HEAD), 1) < HEAD
    return jnp.concatenate(
        [
            jnp.where(low, columns[:, h : h + 1], columns[:, h + 1 : h + 2])
            for h in range(0, heads, 2)
        ],
        axis=1,
    )


def head_sums(values, heads):
    rows = values.shape[0]
    low = iota((rows, 2 * HEAD), 1) < HEAD
    sums = []
    for pair in range(heads // 2):
        part = values[:, pair * 2 * HEAD : (pair + 1) * 2 * HEAD]
        sums.append(jnp.sum(jnp.where(low, part, 0.0), axis=1, keepdims=True))
        sums.append(jnp.sum(jnp.where(low, 0.0, part), axis=1, keepdims=True))
    return sums


def softplus(value):
    return jnp.maximum(value, 0.0) + jnp.log1p(jnp.exp(-jnp.abs(value)))


def step_rows(pdt, vec):
    size = pdt.shape[1]
    raw = pdt + vec[:, 0:1]
    dt = softplus(raw)
    rate = -jnp.exp(vec[:, 1:2])
    upper = (iota((size, size), 0) <= iota((size, size), 1)).astype(f32)
    logs = dot_exact(dt * rate, upper)
    last = logs[:, size - 1 : size]
    return raw, dt, rate, logs, jnp.exp(logs), jnp.exp(last - logs), jnp.exp(last)


def mamba_fwd_kernel(
    heads,
    rank,
    px,
    px_tail,
    pz,
    pbc,
    pbc_tail,
    pdt,
    taps,
    shared_taps,
    vec,
    om,
    kept,
    states,
    state,
):
    step = pl.program_id(0)

    @pl.when(step == 0)
    def _():
        state[...] = jnp.zeros_like(state)

    started = jnp.where(step == 0, 0.0, 1.0)
    u = conv_rows(px_tail[...] * started, px[...], taps[...])
    u = u * jax.nn.sigmoid(u)
    bc = conv_rows(pbc_tail[...] * started, pbc[...], shared_taps[...])
    bc = (bc * jax.nn.sigmoid(bc)).astype(bf16)
    half = bc.shape[1] // 2
    b_in, c_out = bc[:, :half], bc[:, half:]
    _, dt, _, logs, grow, fade, last = step_rows(pdt[...], vec[...])
    columns = jnp.transpose(jnp.concatenate([logs, grow, fade * dt, dt], axis=0))
    size = u.shape[0]
    causal = iota((size, size), 0) >= iota((size, size), 1)
    mixing = dot_nt(c_out, b_in)
    u_low = u.astype(bf16)
    low = iota((size, 2 * HEAD), 1) < HEAD
    local = []
    for pair in range(heads // 2):
        piece = u_low[:, pair * 2 * HEAD : (pair + 1) * 2 * HEAD]
        outs = []
        for h in (2 * pair, 2 * pair + 1):
            spread = jnp.where(causal, columns[:, h : h + 1] - logs[h : h + 1], -1e30)
            matrix = (mixing * jnp.exp(spread) * dt[h : h + 1]).astype(bf16)
            outs.append(dot_nn(matrix, piece))
        local.append(jnp.where(low, outs[0], outs[1]))
    before = state[...]
    states[0] = before
    carried = dot_nn(c_out, before.astype(bf16)) * head_columns(columns[:, 8:16], heads)
    skip = head_columns(jnp.transpose(jnp.broadcast_to(vec[:, 2:3], (8, size))), heads)
    total = jnp.concatenate(local, axis=1) + carried + skip * u
    z = pz[...]
    om[...] = (total * (z * jax.nn.sigmoid(z))).astype(bf16)
    kept[...] = total.astype(bf16)
    fed = (u * head_columns(columns[:, 16:24], heads)).astype(bf16)
    end = head_columns(jnp.transpose(jnp.broadcast_to(last, (8, 128))), heads)[:1]
    state[...] = before * end + dot_tn(b_in, fed)


def mamba_bwd_kernel(
    heads,
    rank,
    px,
    px_tail,
    pz,
    pbc,
    pbc_tail,
    pdt,
    taps,
    shared_taps,
    vec,
    states,
    gym,
    g_pxs,
    g_pbc,
    g_taps,
    g_shared,
    g_vec,
    g_skip,
    d_state,
    next_px,
    next_bc,
):
    step = pl.program_id(0)
    steps = pl.num_programs(0)

    @pl.when(step == 0)
    def _():
        d_state[...] = jnp.zeros_like(d_state)
        next_px[...] = jnp.zeros_like(next_px)
        next_bc[...] = jnp.zeros_like(next_bc)
        g_taps[...] = jnp.zeros_like(g_taps)
        g_shared[...] = jnp.zeros_like(g_shared)
        g_vec[...] = jnp.zeros_like(g_vec)
        g_skip[...] = jnp.zeros_like(g_skip)

    started = jnp.where(step == steps - 1, 0.0, 1.0)
    size = px.shape[0]
    tail_x = px_tail[...] * started
    block_x = px[...]
    pre_u = conv_rows(tail_x, block_x, taps[...])
    sig_u = jax.nn.sigmoid(pre_u)
    u = pre_u * sig_u
    tail_bc = pbc_tail[...] * started
    block_bc = pbc[...]
    pre_bc = conv_rows(tail_bc, block_bc, shared_taps[...])
    sig_bc = jax.nn.sigmoid(pre_bc)
    bc = (pre_bc * sig_bc).astype(bf16)
    half = bc.shape[1] // 2
    b_in, c_out = bc[:, :half], bc[:, half:]
    raw, dt, rate, logs, grow, fade, last = step_rows(pdt[...], vec[...])
    columns = jnp.transpose(jnp.concatenate([logs, grow, fade, dt], axis=0))
    z = pz[...]
    sig_z = jax.nn.sigmoid(z)
    g = gym[...]
    dy = g * (z * sig_z)
    dy_low = dy.astype(bf16)
    u_low = u.astype(bf16)
    before = states[0]
    before_low = before.astype(bf16)
    d_after = d_state[...]
    d_after_low = d_after.astype(bf16)
    causal = iota((size, size), 0) <= iota((size, size), 1)
    mixing = dot_nt(b_in, c_out)
    low = iota((size, 2 * HEAD), 1) < HEAD
    d_mixing = jnp.zeros((size, size), f32)
    du_local, col_sums, row_sums = [], [], []
    for pair in range(heads // 2):
        lanes = slice(pair * 2 * HEAD, (pair + 1) * 2 * HEAD)
        u_piece, dy_piece = u_low[:, lanes], dy_low[:, lanes]
        outs = []
        for h in (2 * pair, 2 * pair + 1):
            dt_col = columns[:, 24 + h : 25 + h]
            spread = jnp.where(causal, logs[h : h + 1] - columns[:, h : h + 1], -1e30)
            decay = jnp.exp(spread)
            keep = low if h % 2 == 0 else jnp.logical_not(low)
            masked = jnp.where(keep, u_piece, jnp.zeros_like(u_piece))
            product = dot_nt(masked, dy_piece) * decay
            d_mixing = d_mixing + product * dt_col
            product = product * mixing
            col_sums.append(jnp.sum(product, axis=1, keepdims=True))
            row_sums.append(jnp.sum(product * dt_col, axis=0, keepdims=True))
            outs.append(dot_nn((mixing * decay).astype(bf16), dy_piece))
        du_local.append(jnp.where(low, outs[0], outs[1]))
    grow_all = head_columns(columns[:, 8:16], heads)
    fade_all = head_columns(columns[:, 16:24], heads)
    dt_all = head_columns(columns[:, 24:32], heads)
    dy_grown = dy * grow_all
    dy_grown_low = dy_grown.astype(bf16)
    fed_low = (u * fade_all * dt_all).astype(bf16)
    back = dot_nn(b_in, d_after_low) * fade_all
    inter = head_sums(dy_grown * dot_nn(c_out, before_low), heads)
    tails = head_sums(u * back, heads)
    skip = head_columns(jnp.transpose(jnp.broadcast_to(vec[:, 2:3], (8, size))), heads)
    du = (jnp.concatenate(du_local, axis=1) + back) * dt_all + skip * dy
    d_mixing_low = d_mixing.astype(bf16)
    db = dot_nn(d_mixing_low, c_out) + dot_nt(fed_low, d_after_low)
    dc = dot_tn(d_mixing_low, b_in) + dot_nt(dy_grown_low, before_low)
    end = head_columns(jnp.transpose(jnp.broadcast_to(last, (8, 128))), heads)[:1]
    ended = d_after * end
    ends = head_sums(jnp.sum(ended * before, axis=0, keepdims=True), heads)
    d_state[...] = ended + dot_tn(c_out, dy_grown_low)
    lane = iota((size, 128), 1)
    gathered = jnp.zeros((size, 128), f32)
    for h in range(heads):
        gathered = jnp.where(lane == h, col_sums[h] + tails[h], gathered)
        gathered = jnp.where(lane == 8 + h, tails[h], gathered)
        gathered = jnp.where(lane == 16 + h, inter[h], gathered)
    turned = jnp.transpose(gathered)
    direct, tail_row, inter_row = turned[0:8], turned[8:16], turned[16:24]
    pad = [jnp.zeros((1, size), f32)] * (8 - heads)
    row_sum = jnp.concatenate(row_sums + pad, axis=0)
    zero = jnp.zeros((1, 1), f32)
    end_col = jnp.concatenate(ends + [zero] * (8 - heads), axis=0)
    d_logs = row_sum + inter_row - dt * direct
    at_last = end_col + jnp.sum(dt * tail_row, axis=1, keepdims=True)
    lower = (iota((size, size), 0) >= iota((size, size), 1)).astype(f32)
    d_rate = dot_exact(d_logs, lower) + at_last
    d_dt = direct + rate * d_rate
    d_raw = d_dt * jax.nn.sigmoid(raw)
    spread_rows = jnp.concatenate([d_raw, jnp.zeros((120, size), f32)], axis=0)
    g_pxs[:, u.shape[1] :] = jnp.transpose(spread_rows).astype(bf16)
    g_vec[0:8] += d_raw
    g_vec[8:16] += rate * dt * d_rate
    g_skip[...] += jnp.sum((dy * u).reshape(size // 8, 8, u.shape[1]), axis=0)
    d_pre = du * (sig_u * (1.0 + pre_u * (1.0 - sig_u)))
    g_pxs[:, : u.shape[1]] = conv_rows_back(d_pre, next_px[...], taps[...]).astype(bf16)
    g_taps[...] += conv_taps_back(tail_x, block_x, d_pre)
    next_px[...] = d_pre[:8]
    d_bc = jnp.concatenate([db, dc], axis=1) * (sig_bc * (1.0 + pre_bc * (1.0 - sig_bc)))
    g_pbc[...] = conv_rows_back(d_bc, next_bc[...], shared_taps[...]).astype(bf16)
    g_shared[...] += conv_taps_back(tail_bc, block_bc, d_bc)
    next_bc[...] = d_bc[:8]


def pad_rows(value):
    return jnp.pad(value, ((0, -value.shape[0] % 8), (0, 0)))


def vec_of(step_bias, decay_log, skip_gain):
    table = jnp.stack([step_bias, decay_log, skip_gain], axis=1)
    return jnp.pad(table, ((0, 8 - table.shape[0]), (0, 128 - table.shape[1])))


def whole(shape):
    return pl.BlockSpec(shape, lambda i, r: tuple(0 for _ in shape))


def cost(flops, moved, exps):
    return pl.CostEstimate(flops=flops, bytes_accessed=moved, transcendentals=exps)


def chunk_specs(length, ranks, order):
    per_block = length // ranks // CHUNK
    per = CHUNK // 8

    def place(i, r):
        c = order(i)
        return ((c // per_block) ^ r[0]) * per_block + c % per_block

    def at(cols):
        return pl.BlockSpec((CHUNK, cols), lambda i, r: (place(i, r), 0))

    def tail(cols):
        def index(i, r):
            c = jnp.maximum(order(i) - 1, 0)
            return ((((c // per_block) ^ r[0]) * per_block + c % per_block) * per + per - 1, 0)

        return pl.BlockSpec((8, cols), index)

    row = pl.BlockSpec((8, CHUNK), lambda i, r: (0, place(i, r)))
    return at, tail, row


def mamba_fwd(rank, px, pz, pbc, pdt, taps, shared_taps, vec, heads, ranks):
    length, chans = px.shape
    wide = pbc.shape[1]
    steps = length // CHUNK
    at, tail, row = chunk_specs(length, ranks, lambda i: i)
    return pl.pallas_call(
        functools.partial(mamba_fwd_kernel, heads),
        grid_spec=pltpu.PrefetchScalarGridSpec(
            num_scalar_prefetch=1,
            grid=(steps,),
            in_specs=[
                at(chans),
                tail(chans),
                at(chans),
                at(wide),
                tail(wide),
                row,
                whole((8, chans)),
                whole((8, wide)),
                whole((8, 128)),
            ],
            out_specs=[
                at(chans),
                at(chans),
                pl.BlockSpec((1, wide // 2, chans), lambda i, r: (i, 0, 0)),
            ],
            scratch_shapes=[pltpu.VMEM((wide // 2, chans), f32)],
        ),
        out_shape=[
            jax.ShapeDtypeStruct((length, chans), bf16),
            jax.ShapeDtypeStruct((length, chans), bf16),
            jax.ShapeDtypeStruct((steps, wide // 2, chans), f32),
        ],
        cost_estimate=cost(4 * 10**9, 8 * 10**6, 10**6),
        name="mamba_forward",
    )(rank, px, px, pz, pbc, pbc, pdt, taps, shared_taps, vec)


def mamba_bwd(rank, px, pz, pbc, pdt, taps, shared_taps, vec, states, gym, heads, ranks):
    length, chans = px.shape
    wide = pbc.shape[1]
    steps = length // CHUNK
    at, tail, row = chunk_specs(length, ranks, lambda i: steps - 1 - i)
    return pl.pallas_call(
        functools.partial(mamba_bwd_kernel, heads),
        grid_spec=pltpu.PrefetchScalarGridSpec(
            num_scalar_prefetch=1,
            grid=(steps,),
            in_specs=[
                at(chans),
                tail(chans),
                at(chans),
                at(wide),
                tail(wide),
                row,
                whole((8, chans)),
                whole((8, wide)),
                whole((8, 128)),
                pl.BlockSpec((1, wide // 2, chans), lambda i, r: (steps - 1 - i, 0, 0)),
                at(chans),
            ],
            out_specs=[
                at(chans + 128),
                at(wide),
                whole((8, chans)),
                whole((8, wide)),
                whole((16, 128)),
                whole((8, chans)),
            ],
            scratch_shapes=[
                pltpu.VMEM((wide // 2, chans), f32),
                pltpu.VMEM((8, chans), f32),
                pltpu.VMEM((8, wide), f32),
            ],
        ),
        out_shape=[
            jax.ShapeDtypeStruct((length, chans + 128), bf16),
            jax.ShapeDtypeStruct((length, wide), bf16),
            jax.ShapeDtypeStruct((8, chans), f32),
            jax.ShapeDtypeStruct((8, wide), f32),
            jax.ShapeDtypeStruct((16, 128), f32),
            jax.ShapeDtypeStruct((8, chans), f32),
        ],
        cost_estimate=cost(9 * 10**9, 10**7, 10**6),
        name="mamba_backward",
    )(rank, px, px, pz, pbc, pbc, pdt, taps, shared_taps, vec, states, gym)


ROWS = 256


def turn(pre, cosine, sine):
    inner = iota(pre.shape, 1) % HEAD < HEAD // 2
    lanes = pre.shape[1]
    other = jnp.where(
        inner, pltpu.roll(pre, lanes - HEAD // 2, 1), pltpu.roll(pre, HEAD // 2, 1)
    )
    return pre * cosine + other * sine


def attend_fwd_kernel(scale, rank, qkv, cosine, sine, out, q, k, v):
    length, wide = out.shape
    blocks = length // ROWS
    low = iota((ROWS, 2 * HEAD), 1) < HEAD
    load_qkv(rank, qkv, cosine, sine, q, k, v)
    for i in range(blocks):
        seen = (i + 1) * ROWS
        block = q[i * ROWS : (i + 1) * ROWS]
        keys, values = k[:seen], v[:seen]
        allowed = iota((ROWS, seen), 1) <= iota((ROWS, seen), 0) + i * ROWS
        outs = []
        for h in range(2):
            keep = low if h == 0 else jnp.logical_not(low)
            part = jnp.where(keep, block, jnp.zeros_like(block))
            scores = jnp.where(allowed, dot_nt(part, keys) * scale, -1e30)
            expo = jnp.exp(scores - jnp.max(scores, axis=1, keepdims=True))
            chance = expo * (1.0 / jnp.sum(expo, axis=1, keepdims=True))
            outs.append(dot_nn(chance.astype(bf16), values))
        out[relative_rows(rank, i)] = jnp.where(low, outs[0], outs[1]).astype(bf16)


def relative_rows(rank, i):
    return pl.ds(pl.multiple_of((i ^ rank[0]) * ROWS, ROWS), ROWS)


def load_qkv(rank, qkv, cosine, sine, q, k, v):
    wide = q.shape[1]
    for i in range(q.shape[0] // ROWS):
        rows = slice(i * ROWS, (i + 1) * ROWS)
        piece = qkv[relative_rows(rank, i)]
        q[rows] = turn(piece[:, :wide], cosine[rows], sine[rows]).astype(bf16)
        both = piece[:, wide:]
        turned = pltpu.roll(both, HEAD, 1)
        low = iota(both.shape, 1) < HEAD
        k[rows] = turn(jnp.where(low, both, turned), cosine[rows], sine[rows]).astype(bf16)
        v[rows] = jnp.where(low, turned, both).astype(bf16)


def attend_bwd_kernel(scale, rank, qkv, cosine, sine, go, g_qkv, q, k, v, dk, dv):
    length, wide = dk.shape
    blocks = length // ROWS
    low = iota((ROWS, 2 * HEAD), 1) < HEAD
    load_qkv(rank, qkv, cosine, sine, q, k, v)
    dk[...] = jnp.zeros_like(dk)
    dv[...] = jnp.zeros_like(dv)
    for i in range(blocks):
        seen = (i + 1) * ROWS
        rows = slice(i * ROWS, (i + 1) * ROWS)
        block, grads = q[rows], go[relative_rows(rank, i)]
        keys, values = k[:seen], v[:seen]
        allowed = iota((seen, ROWS), 0) <= iota((seen, ROWS), 1) + i * ROWS
        dqs, dks, dvs = [], [], []
        for h in range(2):
            keep = low if h == 0 else jnp.logical_not(low)
            part = jnp.where(keep, block, jnp.zeros_like(block))
            part_g = jnp.where(keep, grads, jnp.zeros_like(grads))
            scores = jnp.where(allowed, dot_nt(keys, part) * scale, -1e30)
            expo = jnp.exp(scores - jnp.max(scores, axis=0, keepdims=True))
            chance = expo * (1.0 / jnp.sum(expo, axis=0, keepdims=True))
            g_chance = dot_nt(values, part_g)
            center = jnp.sum(chance * g_chance, axis=0, keepdims=True)
            g_scores = (chance * (g_chance - center)).astype(bf16)
            dqs.append(dot_tn(g_scores, keys))
            dks.append(dot_nn(g_scores, part))
            dvs.append(dot_nn(chance.astype(bf16), part_g))
        dq = jnp.where(low, dqs[0], dqs[1]) * scale
        g_qkv[relative_rows(rank, i), :wide] = turn(dq, cosine[rows], -sine[rows]).astype(bf16)
        dk[:seen] += (dks[0] + dks[1]) * scale
        dv[:seen] += dvs[0] + dvs[1]
    for i in range(blocks):
        rows = slice(i * ROWS, (i + 1) * ROWS)
        g_k, g_v = dk[rows], dv[rows]
        g_k = turn(g_k + pltpu.roll(g_k, HEAD, 1), cosine[rows], -sine[rows])
        g_v = g_v + pltpu.roll(g_v, HEAD, 1)
        g_qkv[relative_rows(rank, i), wide:] = jnp.where(low, g_k, g_v).astype(bf16)


def attend_specs(length, wide):
    return [
        whole((length, 2 * wide)),
        whole((length, wide)),
        whole((length, wide)),
    ], [pltpu.VMEM((length, wide), bf16)] * 3


def attend_fwd(rank, qkv, cosine, sine):
    length, wide = cosine.shape
    ins, scratch = attend_specs(length, wide)
    return pl.pallas_call(
        functools.partial(attend_fwd_kernel, HEAD**-0.5),
        grid_spec=pltpu.PrefetchScalarGridSpec(
            num_scalar_prefetch=1,
            grid=(1,),
            in_specs=ins,
            out_specs=whole((length, wide)),
            scratch_shapes=scratch,
        ),
        out_shape=jax.ShapeDtypeStruct((length, wide), bf16),
        cost_estimate=cost(2 * 10**9, 4 * 10**6, 10**6),
        name="attend_forward",
    )(rank, qkv, cosine, sine)


def attend_bwd(rank, qkv, cosine, sine, g_oa):
    length, wide = cosine.shape
    ins, scratch = attend_specs(length, wide)
    return pl.pallas_call(
        functools.partial(attend_bwd_kernel, HEAD**-0.5),
        grid_spec=pltpu.PrefetchScalarGridSpec(
            num_scalar_prefetch=1,
            grid=(1,),
            in_specs=ins + [whole((length, wide))],
            out_specs=whole((length, 2 * wide)),
            scratch_shapes=scratch + [pltpu.VMEM((length, wide), f32)] * 2,
        ),
        out_shape=jax.ShapeDtypeStruct((length, 2 * wide), bf16),
        cost_estimate=cost(4 * 10**9, 6 * 10**6, 10**6),
        name="attend_backward",
    )(rank, qkv, cosine, sine, g_oa)


def project_kernel(order, chans, scalars, even, odd, gain, *refs):
    w_x, w_z, w_bc, outs = refs[:4], refs[4:8], refs[8], refs[9:]
    a1, kept, px, pz, pbc, pdt, qkv = outs
    rows, width = even.shape
    block = width // len(order)
    is_even = pl.program_id(0) % 2 == 0
    step = 32

    def norm(source, keep):
        for i in range(rows // step):
            own = slice(i * step, (i + 1) * step)
            value = source[own].astype(f32)
            rho = lax.rsqrt(jnp.mean(value * value, axis=1, keepdims=True) + epsilon)
            for p, k in enumerate(order):
                there = pl.ds(pl.multiple_of((scalars[0] ^ k) * block, block), block)
                here = slice(p * block, (p + 1) * block)
                piece = source[own, there]
                a1[own, here] = (piece.astype(f32) * rho * gain[:, here]).astype(bf16)
                if keep:
                    kept[own, here] = piece

    @pl.when(is_even)
    def _():
        norm(even, True)

    @pl.when(jnp.logical_not(is_even))
    def _():
        norm(odd, False)

    quarter = width // 4
    parts = [a1[:, q * quarter : (q + 1) * quarter] for q in range(4)]
    px[...] = sum(dot_nn(part, w[:, :chans]) for part, w in zip(parts, w_x))
    steps = sum(
        lax.dot_general(
            w[:, chans:], part, (((0,), (1,)), ((), ())), preferred_element_type=f32
        )
        for part, w in zip(parts, w_x)
    )
    pdt[...] = steps[:8]
    pz[...] = sum(dot_nn(part, w[:, :chans]) for part, w in zip(parts, w_z))
    pbc[...] = dot_nn(a1[...], w_bc[...])
    qkv[...] = sum(dot_nn(part, w[:, chans:]) for part, w in zip(parts, w_z))


def project(scalars, even, odd, gain, w_x, w_z, w_bc, chans, size):
    rows, width = even.shape[0] // 2, even.shape[1]
    length = 4 * rows
    if width // size % 128:
        member = scalars[0]
        even = take_blocks(even, member, size, False)
        odd = take_blocks(odd, member, size, False)
        order = [0]
    else:
        order = relative_order(size)
    if len(order) == 1:
        scalars = jnp.zeros_like(scalars)

    def at(cols):
        return pl.BlockSpec((rows, cols), lambda i, r: (i, 0))

    def half(cols):
        return pl.BlockSpec((rows, cols), lambda i, r: (i // 2, 0))

    def shape(cols, kind, count=length):
        return jax.ShapeDtypeStruct((count, cols), kind)

    n2, low = w_bc.shape[1], w_z[0][0].shape[1] - chans
    return pl.pallas_call(
        functools.partial(project_kernel, order, chans),
        grid_spec=pltpu.PrefetchScalarGridSpec(
            num_scalar_prefetch=1,
            grid=(4,),
            in_specs=[half(width), half(width), whole((1, width))]
            + quarter_specs(w_x)
            + quarter_specs(w_z)
            + [whole(w_bc.shape)],
            out_specs=[
                at(width),
                half(width),
                at(chans),
                at(chans),
                at(n2),
                pl.BlockSpec((8, rows), lambda i, r: (0, i)),
                at(low),
            ],
        ),
        out_shape=[
            shape(width, bf16),
            shape(width, bf16, 2 * rows),
            shape(chans, f32),
            shape(chans, f32),
            shape(n2, f32),
            shape(length, f32, 8),
            shape(low, f32),
        ],
        cost_estimate=cost(3 * 10**9, 14 * 10**6, length),
        name="norm_project",
    )(scalars, even, odd, gain.reshape(1, -1), *arrays_of(w_x), *arrays_of(w_z), w_bc)


def mixer_kernel(chans, rank, om, oa, *refs):
    w_o, (kept, sent) = refs[:4], refs[4:]
    total = jnp.concatenate(
        [dot_nt(om[...], w[:, :chans]) + dot_nt(oa[...], w[:, chans:]) for w in w_o], axis=1
    )

    @pl.when(pl.program_id(0) % 2 == 0)
    def _():
        kept[...] = total

    @pl.when(pl.program_id(0) % 2 == 1)
    def _():
        sent[...] = total.astype(bf16)


def mixer_out(token, om, oa, w_o):
    rows, width = om.shape[0] // 4, 4 * w_o[0][0].shape[0]

    def at(cols):
        return pl.BlockSpec((rows, cols), lambda i, r: (i, 0))

    half = pl.BlockSpec((rows, width), lambda i, r: (i // 2, 0))
    return pl.pallas_call(
        functools.partial(mixer_kernel, om.shape[1]),
        grid_spec=pltpu.PrefetchScalarGridSpec(
            num_scalar_prefetch=1,
            grid=(4,),
            in_specs=[at(om.shape[1]), at(oa.shape[1])] + quarter_specs(w_o),
            out_specs=[half, half],
        ),
        out_shape=[
            jax.ShapeDtypeStruct((2 * rows, width), f32),
            jax.ShapeDtypeStruct((2 * rows, width), bf16),
        ],
        cost_estimate=cost(10**9, 7 * 10**6, 0),
        name="mixer_out",
    )(token, om, oa, *arrays_of(w_o))


def mixer_back_kernel(chans, rank, g0, g1, g2, g3, *refs):
    w_o = refs[:4]
    pz, kept, g_ym, g_oa, g_pz, total = refs[4:]
    quarter = g0.shape[1] // 4
    for k, piece in enumerate((g0, g1, g2, g3)):

        @pl.when(pl.program_id(0) == k)
        def _(piece=piece):
            total[...] = sum(
                dot_nn(piece[:, q * quarter : (q + 1) * quarter], w_o[q][...]) for q in range(4)
            )

    back = total[:, :chans]
    g_ym[...] = back
    g_oa[...] = total[:, chans:].astype(bf16)
    z = pz[...]
    sig = jax.nn.sigmoid(z)
    g_pz[...] = (back * kept[...].astype(f32) * (sig * (1.0 + z * (1.0 - sig)))).astype(bf16)


def mixer_back(token, g_m, w_o, pz, kept):
    rows, width = g_m[0].shape
    length, chans = pz.shape
    cols_o = w_o[0][0].shape[1]
    other = cols_o - chans

    def at(cols):
        return pl.BlockSpec((rows, cols), lambda i, r: (i, 0))

    return pl.pallas_call(
        functools.partial(mixer_back_kernel, chans),
        grid_spec=pltpu.PrefetchScalarGridSpec(
            num_scalar_prefetch=1,
            grid=(4,),
            in_specs=[whole((rows, width))] * 4 + quarter_specs(w_o) + [at(chans)] * 2,
            out_specs=[at(chans), at(other), at(chans)],
            scratch_shapes=[pltpu.VMEM((rows, cols_o), f32)],
        ),
        out_shape=[
            jax.ShapeDtypeStruct((length, chans), f32),
            jax.ShapeDtypeStruct((length, other), bf16),
            jax.ShapeDtypeStruct((length, chans), bf16),
        ],
        cost_estimate=cost(10**9, 9 * 10**6, 10**6),
        name="mixer_back",
    )(token, *g_m, *arrays_of(w_o), pz, kept)


def project_back_kernel(chans, rank, a1, g_pz, g_qkv, g_pxs, g_bc, *refs):
    w_x, w_z, w_bc = refs[:4], refs[4:8], refs[8]
    kept, sent, sums = refs[9:]
    step = pl.program_id(0)
    total = jnp.concatenate(
        [
            dot_nt(g_pz[...], wz[:, :chans])
            + dot_nt(g_qkv[...], wz[:, chans:])
            + dot_nt(g_pxs[...], wx[...])
            for wx, wz in zip(w_x, w_z)
        ],
        axis=1,
    ) + dot_nt(g_bc[...], w_bc[...])

    @pl.when(step == 0)
    def _():
        sums[...] = jnp.zeros_like(sums)

    rows, width = total.shape
    weighed = total * a1[...].astype(f32)
    sums[...] += jnp.sum(weighed.reshape(rows // 8, 8, width), axis=0)

    @pl.when(step % 2 == 0)
    def _():
        kept[...] = total

    @pl.when(step % 2 == 1)
    def _():
        sent[...] = total.astype(bf16)


def project_back(token, a1, g_pz, g_qkv, g_pxs, g_bc, w_x, w_z, w_bc):
    length, width = a1.shape
    chans = g_pz.shape[1]
    rows = length // 4

    def at(cols):
        return pl.BlockSpec((rows, cols), lambda i, r: (i, 0))

    half = pl.BlockSpec((rows, width), lambda i, r: (i // 2, 0))
    parts = (a1, g_pz, g_qkv, g_pxs, g_bc)
    return pl.pallas_call(
        functools.partial(project_back_kernel, chans),
        grid_spec=pltpu.PrefetchScalarGridSpec(
            num_scalar_prefetch=1,
            grid=(4,),
            in_specs=[at(item.shape[1]) for item in parts]
            + quarter_specs(w_x)
            + quarter_specs(w_z)
            + [whole(w_bc.shape)],
            out_specs=[half, half, whole((8, width))],
        ),
        out_shape=[
            jax.ShapeDtypeStruct((2 * rows, width), f32),
            jax.ShapeDtypeStruct((2 * rows, width), bf16),
            jax.ShapeDtypeStruct((8, width), f32),
        ],
        cost_estimate=cost(3 * 10**9, 11 * 10**6, 0),
        name="project_back",
    )(token, *parts, *arrays_of(w_x), *arrays_of(w_z), w_bc)


def rotary_tables(length):
    half = HEAD // 2
    frequency = rotary_base ** (-2.0 * jnp.arange(half, dtype=f32) / HEAD)
    angles = jnp.arange(length, dtype=f32)[:, None] * frequency[None, :]
    cosine, sine = jnp.cos(angles), jnp.sin(angles)
    return (
        jnp.concatenate([cosine] * 4, axis=1),
        jnp.concatenate([-sine, sine, -sine, sine], axis=1),
    )


def swiglu(gate_part, up_part):
    return jax.nn.silu(gate_part) * up_part


def mm(a, b):
    return jnp.dot(a, b, preferred_element_type=f32)


def mm_t(a, b):
    return lax.dot_general(a, b, (((1,), (1,)), ((), ())), preferred_element_type=f32)


def t_mm(a, b):
    return lax.dot_general(a, b, (((0,), (0,)), ((), ())), preferred_element_type=f32)


def body(
    layer_in,
    out_grad,
    lengths,
    mamba_x,
    mamba_z,
    mamba_step,
    query_proj,
    key_proj,
    value_proj,
    mamba_out,
    attend_out,
    mlp_gate,
    mlp_up,
    mlp_down,
    state_proj,
    conv_state,
    norm_gains,
    conv_mamba,
    step_bias,
    decay_log,
    skip_gain,
):
    ranks = lax.axis_size("tensor")
    assert ranks == 4 and layer_in.shape[1] == 1
    rank = lax.axis_index("tensor")
    y, core = rank // 2, rank % 2
    rank_ref = rank.reshape(1)
    peers = lax.axis_size("dp")
    me = lax.axis_index("dp")
    rows, _, width = layer_in.shape
    length = rows * ranks
    chans = mamba_x.shape[1]
    heads = step_bias.shape[0]
    q_cols, k_cols = query_proj.shape[1], key_proj.shape[1]
    ff = mlp_gate.shape[1]
    own_rows, n2 = state_proj.shape

    raw_0 = layer_in[:, 0]
    raw_even = jnp.concatenate([raw_0, flip_y(raw_0)], axis=0)
    raw_odd = flip_core(raw_even)

    pack_x, pack_z = pack_early(
        mamba_x, mamba_step, mamba_z, query_proj, key_proj, value_proj
    )
    first = Gather(pack_x, "dp", False)
    second = Gather(pack_z, "dp", True)
    small = jnp.concatenate([conv_state.reshape(-1), norm_gains.reshape(-1)])
    parts = []
    rest = small
    for _ in range(3):
        parts.append(lax.reduce_precision(rest, 8, 7))
        rest = rest - parts[-1]
    parts = jnp.concatenate(parts)
    small_rows = -(-parts.shape[0] // n2)
    parts = jnp.pad(parts, (0, small_rows * n2 - parts.shape[0])).reshape(small_rows, n2)
    pack_s = jnp.concatenate([state_proj, parts], axis=0).astype(bf16)
    pack_o = jnp.concatenate([mamba_out.T.astype(bf16), attend_out.T.astype(bf16)], axis=1)
    pack_m = jnp.concatenate(
        [mlp_gate.astype(bf16), mlp_up.astype(bf16), mlp_down.T.astype(bf16)], axis=1
    )
    ranked = in_rank_order(pack_s, y, core)
    third = Gather(ranked.reshape(-1, n2), "dp", False)
    sent_x = first.until(2)
    sent_z = second.until(2)
    third.until(2, sent_x, sent_z)
    far_x = first.advance()
    far_z = second.advance()
    third.advance(far_x, far_z)
    gather_m = Gather(after(pack_m, far_x, far_z), "dp", False, True)
    w_x = first.advance()
    gather_o = Gather(after(pack_o, arrays_of(w_x)[2]), "dp", True)
    w_z = second.advance()
    all_s = join_quarters(third.advance()).reshape(peers, ranks, own_rows + small_rows, n2)
    w_bc = all_s[:, :, :own_rows].reshape(width, n2)
    parts = all_s[:, :, own_rows:].reshape(peers, ranks, -1).astype(f32)
    count = small.shape[0]
    small = parts[..., :count] + parts[..., count : 2 * count] + parts[..., 2 * count : 3 * count]
    cut = conv_state.size
    taps_own = conv_state.shape[1]
    gains_own = norm_gains.shape[1]
    taps_rel = small[..., :cut].reshape(peers, ranks, conv_state.shape[0], taps_own)
    taps_rel = jnp.transpose(taps_rel, (2, 0, 1, 3)).reshape(conv_state.shape[0], -1)
    conv_shared = take_blocks(taps_rel, me, peers, True)
    gain_pair = jnp.transpose(
        small[..., cut:].reshape(peers, ranks, 2, gains_own), (2, 0, 1, 3)
    ).reshape(2, width)

    def rho_of(values):
        return lax.rsqrt(jnp.mean(values * values, axis=-1, keepdims=True) + epsilon)

    a1, x02, px, pz, pbc, pdt, qkv = project(
        me.reshape(1), raw_even, raw_odd, gain_pair[0], w_x, w_z, w_bc, chans, peers
    )
    x0, x2 = x02[:rows], x02[rows:]

    limit = lengths[0]

    def masked(block, k):
        place = (rank ^ k) * rows + jnp.arange(rows, dtype=jnp.int32)
        return jnp.where((place < limit)[:, None], block, jnp.zeros_like(block))

    gf0 = masked(move_blocks(after(out_grad, far_x, far_z)[:, 0], me, peers, False), 0)
    gf2 = flip_y(after(gf0, raw_even))

    sent_m = gather_m.until(2, pdt)
    sent_o = gather_o.until(2, pdt)
    cosine, sine = rotary_tables(length)
    oa = attend_fwd(after(rank_ref, sent_o, sent_m), qkv, cosine, sine)
    gf_odd = flip_core(jnp.concatenate([gf0, after(gf2, pdt)], axis=0))
    sent_o = gather_o.advance(oa)
    vec = vec_of(step_bias, decay_log, skip_gain)
    taps, shared_taps = pad_rows(conv_mamba), pad_rows(conv_shared)
    gf_odd = after(gf_odd, oa)
    om, kept, states = mamba_fwd(
        after(rank_ref, sent_o, gf_odd), px, pz, pbc, pdt, taps, shared_taps, vec, heads, ranks
    )
    w_o = gather_o.advance(om)
    gf1, gf3 = gf_odd[:rows], gf_odd[rows:]
    gf_a = jnp.concatenate([gf0, gf1], axis=0)
    gf_b = jnp.concatenate([gf2, gf3], axis=0)
    sent_m = gather_m.advance(om)
    m_kept, m_sent = mixer_out(after(rank_ref, sent_m, gather_m.cross), om, oa, w_o)
    s02 = add_low(m_kept, flip_core(m_sent))
    s0, s2 = s02[:rows], s02[rows:]
    w_m = gather_m.advance()
    m_got = after(flip_y(s2), *arrays_of(w_m))
    w_m = join_quarters(w_m)
    w_gu, w_dn = w_m[:, : 2 * ff], w_m[:, 2 * ff :]

    def second_norm(low_x, m):
        r1 = low_x.astype(f32) + m
        rho = rho_of(r1)
        return r1, rho, (r1 * rho * gain_pair[1]).astype(bf16)

    r1_0, rho_0, a2_0 = second_norm(x0, s0.astype(f32) + m_got.astype(f32))
    a2_1 = flip_core(a2_0)
    a2_a = jnp.concatenate([a2_0, a2_1], axis=0)
    r1_2, rho_2, a2_2 = second_norm(x2, y_sum(s2, s0))
    a2_3 = flip_core(a2_2)
    a2_b = jnp.concatenate([a2_2, a2_3], axis=0)

    def feed(a2, gf, *others):
        gate_up = mm(a2, w_gu)
        gate, up = gate_up[:, :ff], gate_up[:, ff:]
        hidden, glu_back = jax.vjp(swiglu, gate, up)
        hid = hidden.astype(bf16)
        gate_grad, up_grad = glu_back(mm(gf, w_dn))
        g_gu = jnp.concatenate([gate_grad.astype(bf16), up_grad.astype(bf16)], axis=1)
        if others:
            g_gu = after(g_gu, *others)
        return hid, g_gu, mm_t(g_gu, w_gu)

    hid_a, g_gu_a, g_a2_a = feed(a2_a, gf_a)
    t0 = core_sum(g_a2_a[:rows], g_a2_a[rows:])
    hid_b, g_gu_b, g_a2_b = feed(a2_b, gf_b, t0)
    t2 = core_sum(g_a2_b[:rows], g_a2_b[rows:])

    halves = ((0, 0), (0, 1), (1, 0), (1, 1))
    dn_kept, dn_sent = product(
        after(rank_ref, g_a2_b),
        [[(left, [((hid_a, hid_b)[p], b)]) for left, (p, b) in zip((gf0, gf1, gf2, gf3), halves)]],
        True,
    )
    dn = Sum(dn_kept, dn_sent, "dp", True)
    gu_kept, gu_sent = product(
        after(rank_ref, dn_sent),
        [
            [
                (left, [((g_gu_a, g_gu_b)[p], b)])
                for left, (p, b) in zip((a2_0, a2_1, a2_2, a2_3), halves)
            ]
        ],
        False,
    )
    gu = Sum(gu_kept, gu_sent, "dp", False)

    def second_back(g_a2, r1, rho, gf):
        n_two = r1 * rho
        e_two = g_a2 * gain_pair[1]
        inner = jnp.mean(e_two * n_two, axis=-1, keepdims=True)
        return gf.astype(f32) + rho * (e_two - n_two * inner)

    t0_got, t2_got = flip_y(t0), flip_y(t2)
    g_a2_2 = t2.astype(f32) + after(t0_got, t2, gu_sent).astype(f32)
    g_r1_2 = second_back(g_a2_2, r1_2, rho_2, gf2)
    g_m_2 = g_r1_2.astype(bf16)
    g_a2_0 = t0.astype(f32) + after(t2_got, gu_sent).astype(f32)
    g_r1_0 = second_back(g_a2_0, r1_0, rho_0, gf0)
    g_m_0 = g_r1_0.astype(bf16)
    gain_two_grad = jnp.sum(g_a2_0 * (r1_0 * rho_0), axis=0)
    g_m_3, g_m_1 = flip_core(g_m_2), flip_core(g_m_0)
    g_m = (g_m_0, g_m_1, g_m_2, g_m_3)
    g_ym, g_oa, g_pz = mixer_back(after(rank_ref, dn_sent, gu_sent), g_m, w_o, pz, kept)

    sent_dn = dn.advance(g_oa)
    hid_a, hid_b = lax.optimization_barrier((hid_a, hid_b, g_m_0))[:2]
    f_a, f_b = mm_t(hid_a, w_dn), mm_t(hid_b, w_dn)
    f_sent = jnp.concatenate([f_a[rows:], f_b[rows:]], axis=0).astype(bf16)
    f_got = flip_core(f_sent)
    g_qkv = attend_bwd(after(rank_ref, sent_dn, f_sent), qkv, cosine, sine, g_oa)
    sent_dn = dn.advance(g_qkv)
    sent_gu = gu.advance(g_qkv)
    f_kept = jnp.concatenate([f_a[:rows], f_b[:rows]], axis=0)
    f02 = add_low(f_kept, after(f_got, g_qkv))
    f_other = flip_y(f02[rows:])
    z_kept, z_sent = product(
        after(rank_ref, sent_dn, sent_gu, f02),
        [[(g_m[k], [(om, k), (oa, k)]) for k in range(4)], [(a1, [(g_pz, 0), (g_qkv, 0)])]],
        False,
    )
    z = Sum(z_kept, z_sent, "dp", False)
    sent_gu = gu.advance(z_sent)

    g_pxs, g_bc, g_taps, g_shared, g_vec, g_skip = mamba_bwd(
        after(rank_ref, z_sent, sent_gu),
        px, pz, pbc, pdt, taps, shared_taps, vec, states, g_ym, heads, ranks,
    )
    dn_sum, gu_sum = dn.finish(g_pxs), gu.finish(g_pxs)
    x_kept, x_sent = product(
        after(rank_ref, dn_sum, gu_sum), [[(a1, [(g_pxs, 0)])]], False
    )
    x = Sum(x_kept, x_sent, "dp", False)
    sent_z = z.advance(x_sent)
    g_kept, g_sent, g_sums = project_back(
        after(rank_ref, x_sent, sent_z), a1, g_pz, g_qkv, g_pxs, g_bc, w_x, w_z, w_bc
    )
    g_got = flip_core(g_sent)
    sent_x = x.advance(g_sums)
    sent_z = z.advance(g_sums)
    u02 = add_low(g_kept, after(g_got, sent_x, sent_z))
    u_other = flip_y(u02[rows:])
    gain_one_grad = jnp.sum(g_sums, axis=0) / gain_pair[0]
    state_part = t_mm(after(a1, x_sent), g_bc).reshape(peers, 2, 2, own_rows, n2)
    f_other = after(f_other, u02)

    g_taps, g_shared, g_vec, g_skip = lax.optimization_barrier(
        (g_taps, g_shared, g_vec, g_skip, g_sums)
    )[:4]
    conv_taps_grad = g_taps[: conv_mamba.shape[0]]
    conv_shared_grad = g_shared[: conv_state.shape[0]]
    bias_grad = jnp.sum(g_vec[:heads], axis=1)
    decay_grad = jnp.sum(g_vec[8 : 8 + heads], axis=1)
    skip_grad = jnp.sum(g_skip.reshape(8, heads, HEAD), axis=(0, 2))
    gain_grads = take_blocks(jnp.stack([gain_one_grad, gain_two_grad]), me, peers, True)

    def rows_of(items):
        flat = jnp.concatenate([item.reshape(-1) for item in items])
        return jnp.pad(flat, (0, -flat.shape[0] % (8 * n2))).reshape(-1, n2)

    both = rows_of([conv_shared_grad, gain_grads])
    only = rows_of([conv_taps_grad, bias_grad, decay_grad, skip_grad])

    def exchange(kept, sent, shared, axis, mask, *others):
        got = flip(jnp.concatenate([sent.reshape(-1, n2), shared], axis=0), axis, mask)
        got = after(got, *others)
        count = got.shape[0] - shared.shape[0]
        return kept + got[:count].reshape(kept.shape), shared + got[count:]

    by_core = pick(core, state_part[:, :, ::-1], state_part)
    state, both = exchange(by_core[:, :, 0], by_core[:, :, 1], both, "tensor", 1, u02)
    by_y = pick(y, state[:, ::-1], state)
    sent_x = x.advance(by_y)
    state, both = exchange(by_y[:, 0], by_y[:, 1], both, "tensor", 2, sent_x, sent_z)
    state = state.reshape(peers * own_rows, n2)
    shared = jnp.concatenate([both, only], axis=0)
    tie = (u_other,)
    for bit in range(bits_of(peers)):
        half = state.shape[0] // 2
        state, shared = exchange(state[:half], state[half:], shared, "dp", 1 << bit, *tie)
        if bit == 0:
            both_sum = z.finish(state)
            tie = (both_sum,)
        elif bit == 1:
            tie = ()
    state_proj_grad = state
    both_rows = both.shape[0]
    both = shared[:both_rows].reshape(-1)
    only = shared[both_rows:].reshape(-1)

    f_sum = f02[:rows].astype(f32) + f_other.astype(f32)
    layer_out = masked(r1_0 + f_sum, 0).astype(bf16)
    layer_out = move_blocks(layer_out, me, peers, True)[:, None]
    x_sum = x.finish()
    out_sum, z_sum = both_sum[:, : chans + q_cols], both_sum[:, chans + q_cols :]
    in_grad = final_gradient(after(me, both_sum), peers, u02, u_other, gain_pair[0], x02, g_r1_0)[:, None]

    conv_state_sum = both[: conv_state.size * peers * ranks].reshape(conv_shared.shape)
    gain_sum = both[conv_shared.size : conv_shared.size + 2 * width].reshape(2, width)
    member = me * ranks + rank
    conv_state_grad = lax.dynamic_slice_in_dim(conv_state_sum, member * taps_own, taps_own, 1)
    norm_gains_grad = lax.dynamic_slice_in_dim(gain_sum, member * gains_own, gains_own, 1)
    cut = conv_taps_grad.size
    conv_mamba_grad = only[:cut].reshape(conv_taps_grad.shape)
    step_bias_grad = only[cut : cut + heads]
    decay_log_grad = only[cut + heads : cut + 2 * heads]
    skip_gain_grad = only[cut + 2 * heads : cut + 3 * heads]

    return (
        layer_out,
        in_grad,
        x_sum[:, :chans],
        z_sum[:, :chans],
        x_sum[:, chans : chans + heads],
        z_sum[:, chans : chans + q_cols],
        z_sum[:, chans + q_cols : chans + q_cols + k_cols],
        z_sum[:, chans + q_cols + k_cols :],
        out_sum[:, :chans].T,
        out_sum[:, chans:].T,
        gu_sum[:, :ff],
        gu_sum[:, ff:],
        dn_sum.T,
        state_proj_grad,
        conv_state_grad,
        norm_gains_grad,
        conv_mamba_grad,
        step_bias_grad,
        decay_log_grad,
        skip_gain_grad,
    )


def solution(mesh):
    in_specs = (
        P("tensor", "dp", None),
        P("tensor", "dp", None),
        P("dp"),
        P("dp", "tensor"),
        P("dp", "tensor"),
        P("dp", "tensor"),
        P("dp", "tensor"),
        P("dp", "tensor"),
        P("dp", "tensor"),
        P("tensor", "dp"),
        P("tensor", "dp"),
        P("dp", "tensor"),
        P("dp", "tensor"),
        P("tensor", "dp"),
        P(("dp", "tensor"), None),
        P(None, ("dp", "tensor")),
        P(None, ("dp", "tensor")),
        P(None, "tensor"),
        P("tensor"),
        P("tensor"),
        P("tensor"),
    )
    out_specs = (
        P("tensor", "dp", None),
        P("tensor", "dp", None),
        P("dp", "tensor"),
        P("dp", "tensor"),
        P("dp", "tensor"),
        P("dp", "tensor"),
        P("dp", "tensor"),
        P("dp", "tensor"),
        P("tensor", "dp"),
        P("tensor", "dp"),
        P("dp", "tensor"),
        P("dp", "tensor"),
        P("tensor", "dp"),
        P(("dp", "tensor"), None),
        P(None, ("dp", "tensor")),
        P(None, ("dp", "tensor")),
        P(None, "tensor"),
        P("tensor"),
        P("tensor"),
        P("tensor"),
    )
    return jax.shard_map(body, mesh=mesh, in_specs=in_specs, out_specs=out_specs, check_vma=False)
```

profile of v0, /device:TPU:0, one launch (start us, length us, event | category | flops | bytes accessed | tf_op | source)
XLA Modules:
  0.0 355.5 jit_solution(766120731234612925)
XLA Ops:
  5.2 1.9 pack_weights.1
  7.1 4.1 %collective-permute-start.5 = (bf16[128,512]{1,0:T(8,128)(2,1)}, bf16[128,512]{1,0:T(8,128)(2,1)S(1)}, u32[]{:S(2)}, u32[]{:S(2)}) collective-permute-start(bf16[128,512]{1,0:T(8,128)(2,1)} %get-tuple-element.108), channel_id=1, source_target_pairs={{0,16},{4,20},{8,24},{12,28},{16,0},{20,4},{24,8},{28,12},{1,17},{... | collective-permute-start | bytes 393224 | tf_op jit(solution)/shard_map/ppermute | solution.py:19
  20.2 2.0 fusion.50
  22.2 1.9 pad_maximum_fusion.9
  27.5 2.7 collective-permute-start.4
  35.4 4.7 %collective-permute-done.8.refs_1_ = bf16[256,512]{1,0:T(8,128)(2,1)S(1)} collective-permute-done((bf16[256,512]{1,0:T(8,128)(2,1)S(1)}, bf16[256,512]{1,0:T(8,128)(2,1)S(1)}, u32[]{:S(2)}, u32[]{:S(2)}) %collective-permute-start.8) | collective-permute-done | bytes 262176 | tf_op jit(solution)/shard_map/ppermute | solution.py:19
  47.8 2.0 move_blocks.2
  52.1 8.1 %collective-permute-done.10 = bf16[544,256]{1,0:T(8,128)(2,1)} collective-permute-done((bf16[544,256]{1,0:T(8,128)(2,1)}, bf16[544,256]{1,0:T(8,128)(2,1)}, u32[]{:S(2)}, u32[]{:S(2)}) %collective-permute-start.10) | collective-permute-done | bytes 278560 | tf_op jit(solution)/shard_map/ppermute | solution.py:19
  65.5 2.6 collective-permute-done.12.refs_5_.refs_7_
  68.1 9.2 %norm_project.1 = (bf16[1024,1024]{1,0:T(8,128)(2,1)}, bf16[512,1024]{1,0:T(8,128)(2,1)}, f32[1024,384]{1,0:T(8,128)}, f32[1024,384]{1,0:T(8,128)}, f32[1024,256...) custom-call(s32[1]{0:T(128)} %bitcast.scalars.me, bf16[512,1024]{1,0:T(8,128)(2,1)} %pad_maximum_fusion.3.even, ...), custom_call_target="tpu_custom_call" | custom-call | flops 3000000000 | bytes 14000000 | tf_op jit(solution)/shard_map/norm_project/pallas_call | solution.py:945
  83.3 2.0 constant_dynamic-update-slice_fusion.20
  85.9 6.8 %attend_forward.1.oa.refs_2_.refs_5_.refs_8_.refs_11_ = bf16[1024,128]{1,0:T(8,128)(2,1)} custom-call(s32[1]{0:T(128)} %bitcast.9.rank, f32[1024,256]{1,0:T(8,128)} %get-tuple-element.119.qkv, f32[1024,128]{1,0:T(8,128)} %get-tuple-element.352.cosine, f32[1024,128]{1,0:T(8,128)} %get-tuple-element.353.sine), custom_call_target="tpu_custom_call" | custom-call | flops 2000000000 | bytes 4000000 | tf_op jit(solution)/shard_map/attend_forward/pallas_call | solution.py:845
  93.4 2.0 collective-permute-start.20
  96.1 12.3 %mamba_forward.1 = (bf16[1024,384]{1,0:T(8,128)(2,1)}, bf16[1024,384]{1,0:T(8,128)(2,1)}, f32[8,128,384]{2,1,0:T(8,128)}) custom-call(s32[1]{0:T(128)} %bitcast.9.rank, f32[1024,384]{1,0:T(8,128)} %get-tuple-element.126.px.px_tail, f32[1024,384]{1,0:T(8,128)} %get-tuple-element.126.px.px_tail, f32[1024,384]{1,0:T(8,128)} %get-tuple-element.127.pz.refs_4_, ...), custom_call_target="tpu_custom_call" | custom-call | flops 4000000000 | bytes 8000000 | tf_op jit(solution)/shard_map/mamba_forward/pallas_call | solution.py:662
  108.4 8.1 %collective-permute-done.20.refs_1_.refs_3_ = bf16[512,512]{1,0:T(8,128)(2,1)S(1)} collective-permute-done((bf16[512,512]{1,0:T(8,128)(2,1)}, bf16[512,512]{1,0:T(8,128)(2,1)S(1)}, u32[]{:S(2)}, u32[]{:S(2)}) %collective-permute-start.20) | collective-permute-done | bytes 524320 | tf_op jit(solution)/shard_map/ppermute | solution.py:19
  117.3 6.2 %mixer_out.1 = (f32[512,1024]{1,0:T(8,128)}, bf16[512,1024]{1,0:T(8,128)(2,1)}) custom-call(s32[1]{0:T(128)} %bitcast.9.rank, bf16[1024,384]{1,0:T(8,128)(2,1)} %get-tuple-element.129.om.refs_1_.refs_4_.refs_7_.refs_10_, bf16[1024,128]{1,0:T(8,128)(2,1)} %attend_forward.1.oa.refs_2_.refs_5_.refs_8_.refs_11_, bf16[256,512]{1,0:T(8,128)(2,1)} %copy-done.42, ...), custom_call_target="tpu_custom_call" | custom-call | flops 1000000000 | bytes 7000000 | tf_op jit(solution)/shard_map/mixer_out/pallas_call | solution.py:1000
  124.2 2.3 collective-permute-done.21
  126.4 2.0 add_convert_fusion.1
  131.6 2.1 constant_dynamic-update-slice_fusion.19
  133.7 10.1 %collective-permute-done.23 = bf16[256,1536]{0,1:T(8,128)(2,1)} collective-permute-done((bf16[256,1536]{0,1:T(8,128)(2,1)}, bf16[256,1536]{0,1:T(8,128)(2,1)}, u32[]{:S(2)}, u32[]{:S(2)}) %collective-permute-start.23) | collective-permute-done | bytes 786464 | tf_op jit(solution)/shard_map/ppermute | solution.py:19
  144.5 10.4 %collective-permute-done.25 = bf16[256,1024]{1,0:T(8,128)(2,1)S(1)} collective-permute-done((bf16[256,1024]{1,0:T(8,128)(2,1)}, bf16[256,1024]{1,0:T(8,128)(2,1)S(1)}, u32[]{:S(2)}, u32[]{:S(2)}) %collective-permute-start.25) | collective-permute-done | bytes 524320 | tf_op jit(solution)/shard_map/ppermute | solution.py:19
  155.7 1.8 multiply_reduce_fusion.4
  162.5 2.0 fusion.12
  167.7 2.0 fusion.15
  176.9 2.3 pad_maximum_fusion.4.refs_1_.refs_3_
  179.2 5.2 %weight_product.4 = (f32[512,512]{1,0:T(8,128)}, bf16[512,512]{1,0:T(8,128)(2,1)}) custom-call(s32[1]{0:T(128)} %bitcast.9.rank, bf16[256,1024]{1,0:T(8,128)(2,1)} %copy-done.15, bf16[512,512]{1,0:T(8,128)(2,1)} %get-tuple-element.142.refs_1_.refs_3_, bf16[256,1024]{1,0:T(8,128)(2,1)} %copy-done.28, bf16[512,512]{1,0:T(8,128)(2,1)} %get-tuple-element.142.refs_1_.refs_3_, ...), custom_call_target="tpu_custom_call" | custom-call | flops 1073741824 | bytes 4194304 | tf_op jit(solution)/shard_map/weight_product/pallas_call | solution.py:162
  184.7 6.9 %weight_product.5 = (f32[512,1024]{1,0:T(8,128)}, bf16[512,1024]{1,0:T(8,128)(2,1)}) custom-call(s32[1]{0:T(128)} %bitcast.9.rank, bf16[256,1024]{1,0:T(8,128)(2,1)} %copy-done.47, bf16[512,1024]{1,0:T(8,128)(2,1)} %pad_maximum_fusion.4.refs_1_.refs_3_, bf16[256,1024]{1,0:T(8,128)(2,1)} %copy-done.72, bf16[512,1024]{1,0:T(8,128)(2,1)} %pad_maximum_fusion.4.refs_1_.refs_3_, ...), custom_call_target="tpu_custom_call" | custom-call | flops 2147483648 | bytes 8388608 | tf_op jit(solution)/shard_map/weight_product/pallas_call | solution.py:162
  192.3 6.0 %collective-permute-done.29 = bf16[256,1024]{1,0:T(8,128)(2,1)} collective-permute-done((bf16[256,1024]{1,0:T(8,128)(2,1)}, bf16[256,1024]{1,0:T(8,128)(2,1)}, u32[]{:S(2)}, u32[]{:S(2)}) %collective-permute-start.29) | collective-permute-done | bytes 524320 | tf_op jit(solution)/shard_map/ppermute | solution.py:19
  198.3 2.5 multiply_reduce_fusion
  200.8 3.6 %fusion.64 = (bf16[256,1024]{1,0:T(8,128)(2,1)S(1)}, f32[256,1024]{1,0:T(8,128)}, bf16[256,1024]{1,0:T(8,128)(2,1)S(1)}) fusion(f32[256]{0:T(256)S(1)} %broadcast_multiply_fusion.1, f32[256,1024]{1,0:T(8,128)S(1)} %get-tuple-element.284, f32[1024]{0:T(1024)S(1)} %mul.230, bf16[256,1024]{1,0:T(8,128)(2,1)} %collective-permute-done.29, ...), kind=kLoop, calls=%fused_computation.216 | loop fusion | flops 7340032 | bytes 7872768 | tf_op jit(solution)/shard_map/convert_element_type | solution.py:1343
  211.2 6.0 %mixer_back.1 = (f32[1024,384]{1,0:T(8,128)}, bf16[1024,128]{1,0:T(8,128)(2,1)}, bf16[1024,384]{1,0:T(8,128)(2,1)}) custom-call(s32[1]{0:T(128)} %bitcast.9.rank, bf16[256,1024]{1,0:T(8,128)(2,1)} %copy-done.9, bf16[256,1024]{1,0:T(8,128)(2,1)} %copy-done.24, bf16[256,1024]{1,0:T(8,128)(2,1)} %copy-done.10, bf16[256,1024]{1,0:T(8,128)(2,1)} %copy-done.25, ...), custom_call_target="tpu_custom_call" | custom-call | flops 1000000000 | bytes 9000000 | tf_op jit(solution)/shard_map/mixer_back/pallas_call | solution.py:1046
  219.0 10.0 %attend_backward.1.refs_14_.g_qkv = bf16[1024,256]{1,0:T(8,128)(2,1)} custom-call(s32[1]{0:T(128)} %bitcast.9.rank, f32[1024,256]{1,0:T(8,128)} %get-tuple-element.119.qkv, f32[1024,128]{1,0:T(8,128)} %get-tuple-element.352.cosine, f32[1024,128]{1,0:T(8,128)} %get-tuple-element.353.sine, bf16[1024,128]{1,0:T(8,128)(2,1)} %get-tuple-element.148.go), custom_call_target="tpu_custom_call" | custom-call | flops 4000000000 | bytes 6000000 | tf_op jit(solution)/shard_map/attend_backward/pallas_call | solution.py:863
  229.0 2.3 convert_add_fusion.1
  233.2 2.0 collective-permute-start.37
  238.7 10.9 %weight_product.6 = (f32[512,1152]{1,0:T(8,128)}, bf16[512,1152]{1,0:T(8,128)(2,1)}) custom-call(s32[1]{0:T(128)} %bitcast.9.rank, bf16[256,1024]{1,0:T(8,128)(2,1)} %copy-done.9, bf16[1024,384]{1,0:T(8,128)(2,1)} %get-tuple-element.129.om.refs_1_.refs_4_.refs_7_.refs_10_, bf16[1024,128]{1,0:T(8,128)(2,1)} %attend_forward.1.oa.refs_2_.refs_5_.refs_8_.refs_11_, ...), custom_call_target="tpu_custom_call" | custom-call | flops 2415919104 | bytes 9437184 | tf_op jit(solution)/shard_map/weight_product/pallas_call | solution.py:162
  254.7 20.8 %mamba_backward.1 = (bf16[1024,512]{1,0:T(8,128)(2,1)}, bf16[1024,256]{1,0:T(8,128)(2,1)}, f32[8,384]{1,0:T(8,128)}, f32[8,256]{1,0:T(8,128)}, f32[16,128]{1,0:T(8,128)}, /*index=5*/f32[8,384]{1,0:T(8,128)}) custom-call(s32[1]{0:T(128)} %bitcast.9.rank, f32[1024,384]{1,0:T(8,128)} %get-tuple-element.126.px.px_tail, ...), custom_call_target="tpu_custom_call" | custom-call | flops 8999999488 | bytes 10000000 | tf_op jit(solution)/shard_map/mamba_backward/pallas_call | solution.py:700
  277.3 1.8 fusion.41
  279.1 5.2 %weight_product.7 = (f32[512,512]{1,0:T(8,128)}, bf16[512,512]{1,0:T(8,128)(2,1)}) custom-call(s32[1]{0:T(128)} %bitcast.9.rank, bf16[1024,1024]{1,0:T(8,128)(2,1)} %get-tuple-element.180.refs_12_.refs_0_.a1, bf16[1024,512]{1,0:T(8,128)(2,1)} %get-tuple-element.163.refs_1_.g_pxs), custom_call_target="tpu_custom_call" | custom-call | flops 1073741824 | bytes 4194304 | tf_op jit(solution)/shard_map/weight_product/pallas_call | solution.py:162
  289.1 2.4 convert_add_fusion
  293.3 9.0 %project_back.1 = (f32[512,1024]{1,0:T(8,128)}, bf16[512,1024]{1,0:T(8,128)(2,1)}, f32[8,1024]{1,0:T(8,128)}) custom-call(s32[1]{0:T(128)} %bitcast.9.rank, bf16[1024,1024]{1,0:T(8,128)(2,1)} %get-tuple-element.180.refs_12_.refs_0_.a1, bf16[1024,384]{1,0:T(8,128)(2,1)} %get-tuple-element.157.refs_13_.g_pz, bf16[1024,256]{1,0:T(8,128)(2,1)} %attend_backward.1.refs_14_.g_qkv, ...), custom_call_target="tpu_custom_call" | custom-call | flops 3000000000 | bytes 11000000 | tf_op jit(solution)/shard_map/project_back/pallas_call | solution.py:1106
  305.3 2.4 convert_add_fusion.3
  310.8 2.0 collective-permute-start.45
  312.8 2.3 add_convert_fusion.u_own
  319.0 2.1 select_convert_fusion.source
  321.9 2.1 move_blocks.3
  329.8 4.4 %collective-permute-done.51 = bf16[128,512]{1,0:T(8,128)(2,1)S(1)} collective-permute-done((bf16[128,512]{1,0:T(8,128)(2,1)S(1)}, bf16[128,512]{1,0:T(8,128)(2,1)S(1)}, u32[]{:S(2)}, u32[]{:S(2)}) %collective-permute-start.51) | collective-permute-done | bytes 131104 | tf_op jit(solution)/shard_map/ppermute | solution.py:19
  341.5 3.6 %collective-permute-done.52 = f32[88,256]{1,0:T(8,128)S(1)} collective-permute-done((f32[88,256]{1,0:T(8,128)S(1)}, f32[88,256]{1,0:T(8,128)S(1)}, u32[]{:S(2)}, u32[]{:S(2)}) %collective-permute-start.52) | collective-permute-done | bytes 90144 | tf_op jit(solution)/shard_map/ppermute | solution.py:19
  349.1 3.1 input_gradient.1
  (420 shorter events, 124.5 us)
Async XLA Ops:
  7.1 23.1 %collective-permute-start.5 = (bf16[128,512]{1,0:T(8,128)(2,1)}, bf16[128,512]{1,0:T(8,128)(2,1)S(1)}, u32[]{:S(2)}, u32[]{:S(2)}) collective-permute-start(bf16[128,512]{1,0:T(8,128)(2,1)} %get-tuple-element.108), channel_id=1, source_target_pairs={{0,16},{4,20},{8,24},{12,28},{16,0},{20,4},{24,8},{28,12},{1,17},{... | collective-permute-start | bytes 393224 | tf_op jit(solution)/shard_map/ppermute | solution.py:19
  11.1 21.3 %collective-permute-start.6 = (bf16[128,640]{1,0:T(8,128)(2,1)}, bf16[128,640]{1,0:T(8,128)(2,1)S(1)}, u32[]{:S(2)}, u32[]{:S(2)}) collective-permute-start(bf16[128,640]{1,0:T(8,128)(2,1)} %get-tuple-element.109), channel_id=1, source_target_pairs={{0,16},{4,20},{8,24},{12,28},{16,0},{20,4},{24,8},{28,12},{1,17},{... | collective-permute-start | bytes 491528 | tf_op jit(solution)/shard_map/ppermute | solution.py:19
  11.1 39.8 %collective-permute-start = (bf16[256,1024]{1,0:T(8,128)(2,1)}, bf16[256,1024]{1,0:T(8,128)(2,1)S(1)}, u32[]{:S(2)}, u32[]{:S(2)}) collective-permute-start(bf16[256,1024]{1,0:T(8,128)(2,1)} %bitcast.97), channel_id=1, source_target_pairs={{0,2},{1,3},{2,0},{3,1},{4,6},{5,7},{6,4},{7,5},{8,10},{9,11},{10,... | collective-permute-start | bytes 1572872 | tf_op jit(solution)/shard_map/ppermute | solution.py:19
  15.5 9.7 %collective-permute-start.2 = (bf16[34,256]{1,0:T(8,128)(2,1)S(1)}, bf16[34,256]{1,0:T(8,128)(2,1)S(1)}, u32[]{:S(2)}, u32[]{:S(2)}) collective-permute-start(bf16[34,256]{1,0:T(8,128)(2,1)S(1)} %pad_maximum_fusion.21), channel_id=1, source_target_pairs={{0,2},{1,3},{2,0},{3,1},{4,6},{5,7},{6,4},{7,5},{8,10},{9,11},{10,... | collective-permute-start | bytes 52232 | tf_op jit(solution)/shard_map/ppermute | solution.py:19
  27.5 7.2 %collective-permute-start.4 = (bf16[136,256]{1,0:T(8,128)(2,1)S(1)}, bf16[136,256]{1,0:T(8,128)(2,1)S(1)}, u32[]{:S(2)}, u32[]{:S(2)}) collective-permute-start(bf16[136,256]{1,0:T(8,128)(2,1)S(1)} %reshape_reshape.7), channel_id=1, source_target_pairs={{0,16},{4,20},{8,24},{12,28},{16,0},{20,4},{24,8},{28,12},{1,17},{... | collective-permute-start | bytes 208904 | tf_op jit(solution)/shard_map/ppermute | solution.py:19
  30.8 9.2 %collective-permute-start.8 = (bf16[256,512]{1,0:T(8,128)(2,1)S(1)}, bf16[256,512]{1,0:T(8,128)(2,1)S(1)}, u32[]{:S(2)}, u32[]{:S(2)}) collective-permute-start(bf16[256,512]{1,0:T(8,128)(2,1)S(1)} %get-tuple-element.328.refs_0_), channel_id=1, source_target_pairs={{0,8},{4,12},{8,0},{12,4},{16,24},{20,28},{24,16},{28,20},{1,9},{5... | collective-permute-start | bytes 786440 | tf_op jit(solution)/shard_map/ppermute | solution.py:19
  33.1 9.6 %collective-permute-start.9 = (bf16[256,640]{1,0:T(8,128)(2,1)S(1)}, bf16[256,640]{1,0:T(8,128)(2,1)S(1)}, u32[]{:S(2)}, u32[]{:S(2)}) collective-permute-start(bf16[256,640]{1,0:T(8,128)(2,1)S(1)} %get-tuple-element.320.refs_4_), channel_id=1, source_target_pairs={{0,4},{4,0},{8,12},{12,8},{16,20},{20,16},{24,28},{28,24},{1,5},{5... | collective-permute-start | bytes 983048 | tf_op jit(solution)/shard_map/ppermute | solution.py:19
  34.6 11.8 %collective-permute-start.7 = (bf16[272,256]{1,0:T(8,128)(2,1)S(1)}, bf16[272,256]{1,0:T(8,128)(2,1)S(1)}, u32[]{:S(2)}, u32[]{:S(2)}) collective-permute-start(bf16[272,256]{1,0:T(8,128)(2,1)S(1)} %pad_maximum_fusion.15), channel_id=1, source_target_pairs={{0,8},{4,12},{8,0},{12,4},{16,24},{20,28},{24,16},{28,20},{1,9},{5... | collective-permute-start | bytes 417800 | tf_op jit(solution)/shard_map/ppermute | solution.py:19
  40.8 24.0 %collective-permute-start.11 = (bf16[512,512]{1,0:T(8,128)(2,1)}, bf16[512,512]{1,0:T(8,128)(2,1)}, u32[]{:S(2)}, u32[]{:S(2)}) collective-permute-start(bf16[512,512]{1,0:T(8,128)(2,1)} %constant_dynamic-update-slice_fusion.4), channel_id=1, source_target_pairs={{0,4},{4,0},{8,12},{12,8},{16,20},{20,16},{24,28},{28,24},{1,5},{5... | collective-permute-start | bytes 1572872 | tf_op jit(solution)/shard_map/ppermute | solution.py:19
  43.5 24.6 %collective-permute-start.12 = (bf16[512,640]{1,0:T(8,128)(2,1)}, bf16[512,640]{1,0:T(8,128)(2,1)}, u32[]{:S(2)}, u32[]{:S(2)}) collective-permute-start(bf16[512,640]{1,0:T(8,128)(2,1)} %constant_dynamic-update-slice_fusion.7), channel_id=1, source_target_pairs={{0,8},{4,12},{8,0},{12,4},{16,24},{20,28},{24,16},{28,20},{1,9},{5... | collective-permute-start | bytes 1966088 | tf_op jit(solution)/shard_map/ppermute | solution.py:19
  44.7 36.3 %collective-permute-start.13 = (bf16[128,1536]{0,1:T(8,128)(2,1)S(1)}, bf16[128,1536]{0,1:T(8,128)(2,1)S(1)}, u32[]{:S(2)}, u32[]{:S(2)}) collective-permute-start(bf16[128,1536]{0,1:T(8,128)(2,1)S(1)} %pad_maximum_fusion.11), channel_id=1, source_target_pairs={{0,16},{4,20},{8,24},{12,28},{16,0},{20,4},{24,8},{28,12},{1,17},{... | collective-permute-start | bytes 1179656 | tf_op jit(solution)/shard_map/ppermute | solution.py:19
  47.2 13.0 %collective-permute-start.10 = (bf16[544,256]{1,0:T(8,128)(2,1)}, bf16[544,256]{1,0:T(8,128)(2,1)}, u32[]{:S(2)}, u32[]{:S(2)}) collective-permute-start(bf16[544,256]{1,0:T(8,128)(2,1)} %pad_maximum_fusion.12), channel_id=1, source_target_pairs={{0,4},{4,0},{8,12},{12,8},{16,20},{20,16},{24,28},{28,24},{1,5},{5... | collective-permute-start | bytes 835592 | tf_op jit(solution)/shard_map/ppermute | solution.py:19
  52.1 16.0 %collective-permute-start.1 = (bf16[512,1024]{1,0:T(8,128)(2,1)}, bf16[512,1024]{1,0:T(8,128)(2,1)}, u32[]{:S(2)}, u32[]{:S(2)}) collective-permute-start(bf16[512,1024]{1,0:T(8,128)(2,1)} %pad_maximum_fusion.3.even), channel_id=1, source_target_pairs={{0,1},{1,0},{2,3},{3,2},{4,5},{5,4},{6,7},{7,6},{8,9},{9,8},{10,11... | collective-permute-start | bytes 3145736 | tf_op jit(solution)/shard_map/ppermute | solution.py:19
  60.2 17.1 %collective-permute-start.17 = (bf16[256,1024]{1,0:T(8,128)(2,1)S(1)}, bf16[256,1024]{1,0:T(8,128)(2,1)S(1)}, u32[]{:S(2)}, u32[]{:S(2)}) collective-permute-start(bf16[256,1024]{1,0:T(8,128)(2,1)S(1)} %broadcast_select_fusion.refs_0_), channel_id=1, source_target_pairs={{0,2},{1,3},{2,0},{3,1},{4,6},{5,7},{6,4},{7,5},{8,10},{9,11},{10,... | collective-permute-start | bytes 1572872 | tf_op jit(solution)/shard_map/ppermute | solution.py:19
  64.9 16.2 %collective-permute-start.15 = (bf16[128,512]{1,0:T(8,128)(2,1)S(1)}, bf16[128,512]{1,0:T(8,128)(2,1)S(1)}, u32[]{:S(2)}, u32[]{:S(2)}) collective-permute-start(bf16[128,512]{1,0:T(8,128)(2,1)S(1)} %pad_maximum_fusion.16), channel_id=1, source_target_pairs={{0,16},{4,20},{8,24},{12,28},{16,0},{20,4},{24,8},{28,12},{1,17},{... | collective-permute-start | bytes 393224 | tf_op jit(solution)/shard_map/ppermute | solution.py:19
  78.4 17.7 %collective-permute-start.18 = (bf16[512,1024]{1,0:T(8,128)(2,1)}, bf16[512,1024]{1,0:T(8,128)(2,1)S(1)}, u32[]{:S(2)}, u32[]{:S(2)}) collective-permute-start(bf16[512,1024]{1,0:T(8,128)(2,1)} %pad_maximum_fusion.1), channel_id=1, source_target_pairs={{0,1},{1,0},{2,3},{3,2},{4,5},{5,4},{6,7},{7,6},{8,9},{9,8},{10,11... | collective-permute-start | bytes 3145736 | tf_op jit(solution)/shard_map/ppermute | solution.py:19
  81.8 10.8 %collective-permute-start.16 = (bf16[256,512]{1,0:T(8,128)(2,1)S(1)}, bf16[256,512]{1,0:T(8,128)(2,1)S(1)}, u32[]{:S(2)}, u32[]{:S(2)}) collective-permute-start(bf16[256,512]{1,0:T(8,128)(2,1)S(1)} %get-tuple-element.324.refs_0_), channel_id=1, source_target_pairs={{0,4},{4,0},{8,12},{12,8},{16,20},{20,16},{24,28},{28,24},{1,5},{5... | collective-permute-start | bytes 786440 | tf_op jit(solution)/shard_map/ppermute | solution.py:19
  85.4 23.0 %collective-permute-start.14 = (bf16[256,1536]{0,1:T(8,128)(2,1)}, bf16[256,1536]{0,1:T(8,128)(2,1)}, u32[]{:S(2)}, u32[]{:S(2)}) collective-permute-start(bf16[256,1536]{0,1:T(8,128)(2,1)} %get-tuple-element.315), channel_id=1, source_target_pairs={{0,8},{4,12},{8,0},{12,4},{16,24},{20,28},{24,16},{28,20},{1,9},{5... | collective-permute-start | bytes 2359304 | tf_op jit(solution)/shard_map/ppermute | solution.py:19
  85.4 23.0 %collective-permute-start.19 = (bf16[256,1536]{0,1:T(8,128)(2,1)}, bf16[256,1536]{0,1:T(8,128)(2,1)S(1)}, u32[]{:S(2)}, u32[]{:S(2)}) collective-permute-start(bf16[256,1536]{0,1:T(8,128)(2,1)} %get-tuple-element.315), channel_id=1, source_target_pairs={{0,4},{4,0},{8,12},{12,8},{16,20},{20,16},{24,28},{28,24},{1,5},{5... | collective-permute-start | bytes 2359304 | tf_op jit(solution)/shard_map/ppermute | solution.py:19
  93.4 23.0 %collective-permute-start.20 = (bf16[512,512]{1,0:T(8,128)(2,1)}, bf16[512,512]{1,0:T(8,128)(2,1)S(1)}, u32[]{:S(2)}, u32[]{:S(2)}) collective-permute-start(bf16[512,512]{1,0:T(8,128)(2,1)} %constant_dynamic-update-slice_fusion.14), channel_id=1, source_target_pairs={{0,8},{4,12},{8,0},{12,4},{16,24},{20,28},{24,16},{28,20},{1,9},{5... | collective-permute-start | bytes 1572872 | tf_op jit(solution)/shard_map/ppermute | solution.py:19
  123.6 20.3 %collective-permute-start.23 = (bf16[256,1536]{0,1:T(8,128)(2,1)}, bf16[256,1536]{0,1:T(8,128)(2,1)}, u32[]{:S(2)}, u32[]{:S(2)}) collective-permute-start(bf16[256,1536]{0,1:T(8,128)(2,1)} %collective-permute-done.14), channel_id=1, source_target_pairs={{0,4},{4,0},{8,12},{12,8},{16,20},{20,16},{24,28},{28,24},{1,5},{5... | collective-permute-start | bytes 2359304 | tf_op jit(solution)/shard_map/ppermute | solution.py:19
  129.5 15.0 %collective-permute-start.22 = (bf16[256,1024]{1,0:T(8,128)(2,1)}, bf16[256,1024]{1,0:T(8,128)(2,1)S(1)}, u32[]{:S(2)}, u32[]{:S(2)}) collective-permute-start(bf16[256,1024]{1,0:T(8,128)(2,1)} %get-tuple-element.305), channel_id=1, source_target_pairs={{0,2},{1,3},{2,0},{3,1},{4,6},{5,7},{6,4},{7,5},{8,10},{9,11},{10,... | collective-permute-start | bytes 1572872 | tf_op jit(solution)/shard_map/ppermute | solution.py:19
  131.0 23.9 %collective-permute-start.25 = (bf16[256,1024]{1,0:T(8,128)(2,1)}, bf16[256,1024]{1,0:T(8,128)(2,1)S(1)}, u32[]{:S(2)}, u32[]{:S(2)}) collective-permute-start(bf16[256,1024]{1,0:T(8,128)(2,1)} %get-tuple-element.304), channel_id=1, source_target_pairs={{0,2},{1,3},{2,0},{3,1},{4,6},{5,7},{6,4},{7,5},{8,10},{9,11},{10,... | collective-permute-start | bytes 1572872 | tf_op jit(solution)/shard_map/ppermute | solution.py:19
  161.0 5.4 %collective-permute-start.26 = (bf16[256,1024]{1,0:T(8,128)(2,1)S(1)}, bf16[256,1024]{1,0:T(8,128)(2,1)S(1)}, u32[]{:S(2)}, u32[]{:S(2)}) collective-permute-start(bf16[256,1024]{1,0:T(8,128)(2,1)S(1)} %get-tuple-element.297.refs_4_), channel_id=1, source_target_pairs={{0,1},{1,0},{2,3},{3,2},{4,5},{5,4},{6,7},{7,6},{8,9},{9,8},{10,11... | collective-permute-start | bytes 1572872 | tf_op jit(solution)/shard_map/ppermute | solution.py:19
  172.4 19.8 %collective-permute-start.33 = (bf16[256,1024]{1,0:T(8,128)(2,1)}, bf16[256,1024]{1,0:T(8,128)(2,1)}, u32[]{:S(2)}, u32[]{:S(2)}) collective-permute-start(bf16[256,1024]{1,0:T(8,128)(2,1)} %fusion.17), channel_id=1, source_target_pairs={{0,2},{1,3},{2,0},{3,1},{4,6},{5,7},{6,4},{7,5},{8,10},{9,11},{10,... | collective-permute-start | bytes 1572872 | tf_op jit(solution)/shard_map/ppermute | solution.py:19
  175.3 23.0 %collective-permute-start.29 = (bf16[256,1024]{1,0:T(8,128)(2,1)}, bf16[256,1024]{1,0:T(8,128)(2,1)}, u32[]{:S(2)}, u32[]{:S(2)}) collective-permute-start(bf16[256,1024]{1,0:T(8,128)(2,1)} %fusion.16), channel_id=1, source_target_pairs={{0,2},{1,3},{2,0},{3,1},{4,6},{5,7},{6,4},{7,5},{8,10},{9,11},{10,... | collective-permute-start | bytes 1572872 | tf_op jit(solution)/shard_map/ppermute | solution.py:19
  184.4 32.8 %collective-permute-start.31 = (bf16[512,512]{1,0:T(8,128)(2,1)}, bf16[512,512]{1,0:T(8,128)(2,1)}, u32[]{:S(2)}, u32[]{:S(2)}) collective-permute-start(bf16[512,512]{1,0:T(8,128)(2,1)} %get-tuple-element.138), channel_id=1, source_target_pairs={{0,8},{4,12},{8,0},{12,4},{16,24},{20,28},{24,16},{28,20},{1,9},{5... | collective-permute-start | bytes 1572872 | tf_op jit(solution)/shard_map/ppermute | solution.py:19
  191.7 37.3 %collective-permute-start.38 = (bf16[512,1024]{1,0:T(8,128)(2,1)}, bf16[512,1024]{1,0:T(8,128)(2,1)}, u32[]{:S(2)}, u32[]{:S(2)}) collective-permute-start(bf16[512,1024]{1,0:T(8,128)(2,1)} %get-tuple-element.140), channel_id=1, source_target_pairs={{0,4},{4,0},{8,12},{12,8},{16,20},{20,16},{24,28},{28,24},{1,5},{5... | collective-permute-start | bytes 3145736 | tf_op jit(solution)/shard_map/ppermute | solution.py:19
  204.4 5.2 %collective-permute-start.32 = (bf16[256,1024]{1,0:T(8,128)(2,1)S(1)}, bf16[256,1024]{1,0:T(8,128)(2,1)S(1)}, u32[]{:S(2)}, u32[]{:S(2)}) collective-permute-start(bf16[256,1024]{1,0:T(8,128)(2,1)S(1)} %get-tuple-element.281.g0.refs_0_), channel_id=1, source_target_pairs={{0,1},{1,0},{2,3},{3,2},{4,5},{5,4},{6,7},{7,6},{8,9},{9,8},{10,11... | collective-permute-start | bytes 1572872 | tf_op jit(solution)/shard_map/ppermute | solution.py:19
  204.4 5.2 %collective-permute-start.34 = (bf16[256,1024]{1,0:T(8,128)(2,1)S(1)}, bf16[256,1024]{1,0:T(8,128)(2,1)S(1)}, u32[]{:S(2)}, u32[]{:S(2)}) collective-permute-start(bf16[256,1024]{1,0:T(8,128)(2,1)S(1)} %get-tuple-element.346.g2.refs_6_), channel_id=1, source_target_pairs={{0,1},{1,0},{2,3},{3,2},{4,5},{5,4},{6,7},{7,6},{8,9},{9,8},{10,11... | collective-permute-start | bytes 1572872 | tf_op jit(solution)/shard_map/ppermute | solution.py:19
  209.5 25.7 %collective-permute-start.30 = (bf16[512,1024]{1,0:T(8,128)(2,1)}, bf16[512,1024]{1,0:T(8,128)(2,1)}, u32[]{:S(2)}, u32[]{:S(2)}) collective-permute-start(bf16[512,1024]{1,0:T(8,128)(2,1)} %pad_maximum_fusion.6), channel_id=1, source_target_pairs={{0,1},{1,0},{2,3},{3,2},{4,5},{5,4},{6,7},{7,6},{8,9},{9,8},{10,11... | collective-permute-start | bytes 3145736 | tf_op jit(solution)/shard_map/ppermute | solution.py:19
  218.4 13.2 %collective-permute-start.36 = (bf16[256,512]{1,0:T(8,128)(2,1)S(1)}, bf16[256,512]{1,0:T(8,128)(2,1)}, u32[]{:S(2)}, u32[]{:S(2)}) collective-permute-start(bf16[256,512]{1,0:T(8,128)(2,1)S(1)} %get-tuple-element.301), channel_id=1, source_target_pairs={{0,4},{4,0},{8,12},{12,8},{16,20},{20,16},{24,28},{28,24},{1,5},{5... | collective-permute-start | bytes 786440 | tf_op jit(solution)/shard_map/ppermute | solution.py:19
  231.3 18.4 %collective-permute-start.39 = (bf16[256,1024]{1,0:T(8,128)(2,1)S(1)}, bf16[256,1024]{1,0:T(8,128)(2,1)}, u32[]{:S(2)}, u32[]{:S(2)}) collective-permute-start(bf16[256,1024]{1,0:T(8,128)(2,1)S(1)} %get-tuple-element.290), channel_id=1, source_target_pairs={{0,8},{4,12},{8,0},{12,4},{16,24},{20,28},{24,16},{28,20},{1,9},{5... | collective-permute-start | bytes 1572872 | tf_op jit(solution)/shard_map/ppermute | solution.py:19
  233.2 42.2 %collective-permute-start.37 = (bf16[128,512]{1,0:T(8,128)(2,1)}, bf16[128,512]{1,0:T(8,128)(2,1)S(1)}, u32[]{:S(2)}, u32[]{:S(2)}) collective-permute-start(bf16[128,512]{1,0:T(8,128)(2,1)} %fusion.48), channel_id=1, source_target_pairs={{0,16},{4,20},{8,24},{12,28},{16,0},{20,4},{24,8},{28,12},{1,17},{... | collective-permute-start | bytes 393224 | tf_op jit(solution)/shard_map/ppermute | solution.py:19
  250.7 26.6 %collective-permute-start.40 = (bf16[128,1024]{1,0:T(8,128)(2,1)S(1)}, bf16[128,1024]{1,0:T(8,128)(2,1)S(1)}, u32[]{:S(2)}, u32[]{:S(2)}) collective-permute-start(bf16[128,1024]{1,0:T(8,128)(2,1)S(1)} %fusion.42), channel_id=1, source_target_pairs={{0,16},{4,20},{8,24},{12,28},{16,0},{20,4},{24,8},{28,12},{1,17},{... | collective-permute-start | bytes 786440 | tf_op jit(solution)/shard_map/ppermute | solution.py:19
  251.6 37.0 %collective-permute-start.41 = (bf16[512,1152]{1,0:T(8,128)(2,1)}, bf16[512,1152]{1,0:T(8,128)(2,1)}, u32[]{:S(2)}, u32[]{:S(2)}) collective-permute-start(bf16[512,1152]{1,0:T(8,128)(2,1)} %get-tuple-element.158), channel_id=1, source_target_pairs={{0,4},{4,0},{8,12},{12,8},{16,20},{20,16},{24,28},{28,24},{1,5},{5... | collective-permute-start | bytes 3538952 | tf_op jit(solution)/shard_map/ppermute | solution.py:19
  253.1 64.3 %collective-permute-start.35 = (bf16[256,1024]{1,0:T(8,128)(2,1)}, bf16[256,1024]{1,0:T(8,128)(2,1)}, u32[]{:S(2)}, u32[]{:S(2)}) collective-permute-start(bf16[256,1024]{1,0:T(8,128)(2,1)} %slice.490), channel_id=1, source_target_pairs={{0,2},{1,3},{2,0},{3,1},{4,6},{5,7},{6,4},{7,5},{8,10},{9,11},{10,... | collective-permute-start | bytes 1572872 | tf_op jit(solution)/shard_map/ppermute | solution.py:19
  284.3 19.6 %collective-permute-start.43 = (bf16[512,512]{1,0:T(8,128)(2,1)}, bf16[512,512]{1,0:T(8,128)(2,1)}, u32[]{:S(2)}, u32[]{:S(2)}) collective-permute-start(bf16[512,512]{1,0:T(8,128)(2,1)} %get-tuple-element.167), channel_id=1, source_target_pairs={{0,4},{4,0},{8,12},{12,8},{16,20},{20,16},{24,28},{28,24},{1,5},{5... | collective-permute-start | bytes 1572872 | tf_op jit(solution)/shard_map/ppermute | solution.py:19
  291.5 17.6 %collective-permute-start.44 = (bf16[256,1152]{1,0:T(8,128)(2,1)}, bf16[256,1152]{1,0:T(8,128)(2,1)}, u32[]{:S(2)}, u32[]{:S(2)}) collective-permute-start(bf16[256,1152]{1,0:T(8,128)(2,1)} %get-tuple-element.288), channel_id=1, source_target_pairs={{0,8},{4,12},{8,0},{12,4},{16,24},{20,28},{24,16},{28,20},{1,9},{5... | collective-permute-start | bytes 1769480 | tf_op jit(solution)/shard_map/ppermute | solution.py:19
  302.4 10.5 %collective-permute-start.42 = (bf16[512,1024]{1,0:T(8,128)(2,1)}, bf16[512,1024]{1,0:T(8,128)(2,1)}, u32[]{:S(2)}, u32[]{:S(2)}) collective-permute-start(bf16[512,1024]{1,0:T(8,128)(2,1)} %get-tuple-element.173), channel_id=1, source_target_pairs={{0,1},{1,0},{2,3},{3,2},{4,5},{5,4},{6,7},{7,6},{8,9},{9,8},{10,11... | collective-permute-start | bytes 3145736 | tf_op jit(solution)/shard_map/ppermute | solution.py:19
  304.8 10.3 %collective-permute-start.46 = (f32[528,256]{1,0:T(8,128)}, f32[528,256]{1,0:T(8,128)}, u32[]{:S(2)}, u32[]{:S(2)}) collective-permute-start(f32[528,256]{1,0:T(8,128)} %pad_maximum_fusion.8), channel_id=1, source_target_pairs={{0,1},{1,0},{2,3},{3,2},{4,5},{5,4},{6,7},{7,6},{8,9},{9,8},{10,11... | collective-permute-start | bytes 1622024 | tf_op jit(solution)/shard_map/ppermute | solution.py:19
  307.7 16.2 %collective-permute-start.48 = (bf16[256,512]{1,0:T(8,128)(2,1)}, bf16[256,512]{1,0:T(8,128)(2,1)}, u32[]{:S(2)}, u32[]{:S(2)}) collective-permute-start(bf16[256,512]{1,0:T(8,128)(2,1)} %get-tuple-element.299), channel_id=1, source_target_pairs={{0,8},{4,12},{8,0},{12,4},{16,24},{20,28},{24,16},{28,20},{1,9},{5... | collective-permute-start | bytes 786440 | tf_op jit(solution)/shard_map/ppermute | solution.py:19
  310.8 27.9 %collective-permute-start.45 = (bf16[128,1152]{1,0:T(8,128)(2,1)}, bf16[128,1152]{1,0:T(8,128)(2,1)}, u32[]{:S(2)}, u32[]{:S(2)}) collective-permute-start(bf16[128,1152]{1,0:T(8,128)(2,1)} %fusion.39), channel_id=1, source_target_pairs={{0,16},{4,20},{8,24},{12,28},{16,0},{20,4},{24,8},{28,12},{1,17},{... | collective-permute-start | bytes 884744 | tf_op jit(solution)/shard_map/ppermute | solution.py:19
  318.4 9.0 %collective-permute-start.47 = (f32[272,256]{1,0:T(8,128)}, f32[272,256]{1,0:T(8,128)S(1)}, u32[]{:S(2)}, u32[]{:S(2)}) collective-permute-start(f32[272,256]{1,0:T(8,128)} %pad_maximum_fusion.13), channel_id=1, source_target_pairs={{0,2},{1,3},{2,0},{3,1},{4,6},{5,7},{6,4},{7,5},{8,10},{9,11},{10,... | collective-permute-start | bytes 835592 | tf_op jit(solution)/shard_map/ppermute | solution.py:19
  323.9 14.0 %collective-permute-start.50 = (bf16[256,1024]{1,0:T(8,128)(2,1)}, bf16[256,1024]{1,0:T(8,128)(2,1)S(1)}, u32[]{:S(2)}, u32[]{:S(2)}) collective-permute-start(bf16[256,1024]{1,0:T(8,128)(2,1)} %slice.504), channel_id=1, source_target_pairs={{0,2},{1,3},{2,0},{3,1},{4,6},{5,7},{6,4},{7,5},{8,10},{9,11},{10,... | collective-permute-start | bytes 1572872 | tf_op jit(solution)/shard_map/ppermute | solution.py:19
  326.4 7.8 %collective-permute-start.51 = (bf16[128,512]{1,0:T(8,128)(2,1)S(1)}, bf16[128,512]{1,0:T(8,128)(2,1)S(1)}, u32[]{:S(2)}, u32[]{:S(2)}) collective-permute-start(bf16[128,512]{1,0:T(8,128)(2,1)S(1)} %fusion.46), channel_id=1, source_target_pairs={{0,16},{4,20},{8,24},{12,28},{16,0},{20,4},{24,8},{28,12},{1,17},{... | collective-permute-start | bytes 393224 | tf_op jit(solution)/shard_map/ppermute | solution.py:19
  328.3 8.3 %collective-permute-start.49 = (f32[152,256]{1,0:T(8,128)S(1)}, f32[152,256]{1,0:T(8,128)S(1)}, u32[]{:S(2)}, u32[]{:S(2)}) collective-permute-start(f32[152,256]{1,0:T(8,128)S(1)} %pad_maximum_fusion.14), channel_id=1, source_target_pairs={{0,4},{4,0},{8,12},{12,8},{16,20},{20,16},{24,28},{28,24},{1,5},{5... | collective-permute-start | bytes 466952 | tf_op jit(solution)/shard_map/ppermute | solution.py:19
  345.1 7.1 %collective-permute-start.53 = (f32[56,256]{1,0:T(8,128)S(1)}, f32[56,256]{1,0:T(8,128)S(1)}, u32[]{:S(2)}, u32[]{:S(2)}) collective-permute-start(f32[56,256]{1,0:T(8,128)S(1)} %pad_maximum_fusion.19), channel_id=1, source_target_pairs={{0,16},{4,20},{8,24},{12,28},{16,0},{20,4},{24,8},{28,12},{1,17},{... | collective-permute-start | bytes 172040 | tf_op jit(solution)/shard_map/ppermute | solution.py:19
  (83 other events, 726.4 us)
where the time goes:
time: 362 us; the launch traced here: 356 us
  Pallas kernels  117 us (32%)
  waiting for transfers between devices  63.9 us (18%)
  other arithmetic  57.3 us (16%)
  local copies, waits for them, and re-layouts  51.7 us (14%)
  starting transfers between devices  49.9 us (14%)
  matrix products  12.3 us (3%)
    ppermute x54, waiting for transfers between devices, flip(): return lax.ppermute(value, axis, [(i, i ^ mask) for i in range(size)])  63.9 us
    ppermute x54, starting transfers between devices, flip(): return lax.ppermute(value, axis, [(i, i ^ mask) for i in range(size)])  49.9 us
    pallas_call x4, Pallas kernels, product(): pl.pallas_call(functools.partial(product_kernel, shapes), grid_spec=pltpu...  28.3 us
    unnamed x170, local copies, waits for them, and re-layouts  27.3 us
    pallas_call x1, Pallas kernels, mamba_bwd(): pl.pallas_call(functools.partial(mamba_bwd_kernel, heads), grid_spec=pltp...  20.8 us
    pallas_call x1, Pallas kernels, mamba_fwd(): pl.pallas_call(functools.partial(mamba_fwd_kernel, heads), grid_spec=pltp...  12.3 us
    pallas_call x1, Pallas kernels, attend_bwd(): pl.pallas_call(functools.partial(attend_bwd_kernel, HEAD ** (-0.5)), grid...  9.97 us
    pallas_call x1, Pallas kernels, project(): pl.pallas_call(functools.partial(project_kernel, order, chans), grid_spec...  9.16 us
  transfers between devices with their start and end apart: 54, of which 15 were waited for; matrix products, arithmetic and copies ran while one was open for 28% of the time, Pallas kernels for 31%

commit v1 on v0

--- a/solution.py
+++ b/solution.py
@@ -179,25 +179,27 @@
     )(token, *operands)
 
 
-def pack_kernel(chans, x, step, z, q, k, v, pack_x, pack_z):
+def pack_kernel(chans, x, step, z, q, k, v, pack_x, pack_z, turned):
     pack_x[:, :chans] = x[...].astype(bf16)
-    pack_x[:, chans:] = jnp.zeros((x.shape[0], 128), bf16)
-    pack_x[:, chans : chans + step.shape[1]] = step[...].astype(bf16)
+    turned[...] = jnp.zeros_like(turned)
+    turned[: step.shape[0]] = step[...]
+    pack_x[:, chans:] = jnp.transpose(turned[...]).astype(bf16)
     pack_z[:, :chans] = z[...].astype(bf16)
     pack_z[:, chans : chans + q.shape[1]] = q[...].astype(bf16)
-    both = jnp.concatenate([k[...], v[...]], axis=1)
-    pack_z[:, chans + q.shape[1] :] = both.astype(bf16)
+    both = jnp.concatenate([k[...], v[...]], axis=0)
+    pack_z[:, chans + q.shape[1] :] = jnp.transpose(both).astype(bf16)
 
 
 def pack_early(x, step, z, q, k, v):
     lines, chans = x.shape
-    cols = chans + q.shape[1] + k.shape[1] + v.shape[1]
+    cols = chans + q.shape[1] + k.shape[0] + v.shape[0]
     return pl.pallas_call(
         functools.partial(pack_kernel, chans),
         out_shape=[
             jax.ShapeDtypeStruct((lines, chans + 128), bf16),
             jax.ShapeDtypeStruct((lines, cols), bf16),
         ],
+        scratch_shapes=[pltpu.VMEM((128, lines), f32)],
         cost_estimate=cost(0, lines * 7000, 0),
         name="pack_weights",
     )(x, step, z, q, k, v)
@@ -1189,15 +1191,17 @@
     ff = mlp_gate.shape[1]
     own_rows, n2 = state_proj.shape
 
+    pack_x, pack_z = pack_early(
+        mamba_x, mamba_step.T, mamba_z, query_proj, key_proj.T, value_proj.T
+    )
+    first = Gather(pack_x, "dp", False)
+    second = Gather(pack_z, "dp", True)
+    layer_in, conv_state, norm_gains, state_proj = lax.optimization_barrier(
+        (layer_in, conv_state, norm_gains, state_proj, pack_x, pack_z)
+    )[:4]
     raw_0 = layer_in[:, 0]
     raw_even = jnp.concatenate([raw_0, flip_y(raw_0)], axis=0)
     raw_odd = flip_core(raw_even)
-
-    pack_x, pack_z = pack_early(
-        mamba_x, mamba_step, mamba_z, query_proj, key_proj, value_proj
-    )
-    first = Gather(pack_x, "dp", False)
-    second = Gather(pack_z, "dp", True)
     small = jnp.concatenate([conv_state.reshape(-1), norm_gains.reshape(-1)])
     parts = []
     rest = small
@@ -1289,7 +1293,8 @@
     r1_0, rho_0, a2_0 = second_norm(x0, s0.astype(f32) + m_got.astype(f32))
     a2_1 = flip_core(a2_0)
     a2_a = jnp.concatenate([a2_0, a2_1], axis=0)
-    r1_2, rho_2, a2_2 = second_norm(x2, y_sum(s2, s0))
+    m_other = after(flip_y(s0), a2_0)
+    r1_2, rho_2, a2_2 = second_norm(x2, s2.astype(f32) + m_other.astype(f32))
     a2_3 = flip_core(a2_2)
     a2_b = jnp.concatenate([a2_2, a2_3], axis=0)
 

time: 362 us -> 357 us (0.986)
  local copies, waits for them, and re-layouts: 51.7 us -> 46 us
    unnamed x170 -> x173, local copies, waits for them, and re-layouts: 27.3 us -> 22.1 us
  transfers between devices with their start and end apart: 54 -> 54, of which waited for: 15 -> 14; matrix products, arithmetic and copies ran while one was open for 28% -> 28% of each run, Pallas kernels for 31% -> 31%
where the time goes in v1:
time: 357 us; the launch traced here: 350 us
  Pallas kernels  118 us (33%)
  waiting for transfers between devices  63 us (18%)
  other arithmetic  56.7 us (16%)
  starting transfers between devices  51.5 us (14%)
  local copies, waits for them, and re-layouts  46 us (13%)
  matrix products  12.3 us (3%)
    ppermute x54, waiting for transfers between devices, flip(): return lax.ppermute(value, axis, [(i, i ^ mask) for i in range(size)])  63 us
    ppermute x54, starting transfers between devices, flip(): return lax.ppermute(value, axis, [(i, i ^ mask) for i in range(size)])  51.5 us
    pallas_call x4, Pallas kernels, product(): pl.pallas_call(functools.partial(product_kernel, shapes), grid_spec=pltpu...  28.4 us
    unnamed x173, local copies, waits for them, and re-layouts  22.1 us
    pallas_call x1, Pallas kernels, mamba_bwd(): pl.pallas_call(functools.partial(mamba_bwd_kernel, heads), grid_spec=pltp...  20.8 us
    pallas_call x1, Pallas kernels, mamba_fwd(): pl.pallas_call(functools.partial(mamba_fwd_kernel, heads), grid_spec=pltp...  12.2 us
    pallas_call x1, Pallas kernels, attend_bwd(): pl.pallas_call(functools.partial(attend_bwd_kernel, HEAD ** (-0.5)), grid...  9.95 us
    pallas_call x1, Pallas kernels, project(): pl.pallas_call(functools.partial(project_kernel, order, chans), grid_spec...  9.17 us
  transfers between devices with their start and end apart: 54, of which 14 were waited for; matrix products, arithmetic and copies ran while one was open for 28% of the time, Pallas kernels for 31%

profile of v1, /device:TPU:0, one launch (start us, length us, event | category | flops | bytes accessed | tf_op | source)
XLA Modules:
  0.0 350.1 jit_solution(15263544208413041234)
XLA Ops:
  0.7 2.0 pack_weights.1
  2.7 4.1 %collective-permute-start.5 = (bf16[128,512]{1,0:T(8,128)(2,1)}, bf16[128,512]{1,0:T(8,128)(2,1)S(1)}, u32[]{:S(2)}, u32[]{:S(2)}) collective-permute-start(bf16[128,512]{1,0:T(8,128)(2,1)} %get-tuple-element.113), channel_id=1, source_target_pairs={{0,16},{4,20},{8,24},{12,28},{16,0},{20,4},{24,8},{28,12},{1,17},{... | collective-permute-start | bytes 393224 | tf_op jit(solution)/shard_map/ppermute | solution.py:19
  6.8 1.8 collective-permute-start
  16.5 2.0 fusion.50
  18.6 1.9 pad_maximum_fusion.9
  24.1 3.0 collective-permute-start.4
  32.3 4.7 %collective-permute-done.8.refs_1_ = bf16[256,512]{1,0:T(8,128)(2,1)S(1)} collective-permute-done((bf16[256,512]{1,0:T(8,128)(2,1)S(1)}, bf16[256,512]{1,0:T(8,128)(2,1)S(1)}, u32[]{:S(2)}, u32[]{:S(2)}) %collective-permute-start.8) | collective-permute-done | bytes 262176 | tf_op jit(solution)/shard_map/ppermute | solution.py:19
  44.7 2.0 move_blocks.2
  48.9 8.0 %collective-permute-done.10 = bf16[544,256]{1,0:T(8,128)(2,1)S(1)} collective-permute-done((bf16[544,256]{1,0:T(8,128)(2,1)}, bf16[544,256]{1,0:T(8,128)(2,1)S(1)}, u32[]{:S(2)}, u32[]{:S(2)}) %collective-permute-start.10) | collective-permute-done | bytes 278560 | tf_op jit(solution)/shard_map/ppermute | solution.py:19
  63.0 2.0 collective-permute-done.12.refs_5_.refs_7_
  64.9 9.2 %norm_project.1 = (bf16[1024,1024]{1,0:T(8,128)(2,1)}, bf16[512,1024]{1,0:T(8,128)(2,1)}, f32[1024,384]{1,0:T(8,128)}, f32[1024,384]{1,0:T(8,128)}, f32[1024,256...) custom-call(s32[1]{0:T(128)} %bitcast.scalars.me, bf16[512,1024]{1,0:T(8,128)(2,1)} %pad_maximum_fusion.3.even, ...), custom_call_target="tpu_custom_call" | custom-call | flops 3000000000 | bytes 14000000 | tf_op jit(solution)/shard_map/norm_project/pallas_call | solution.py:947
  80.3 2.0 constant_dynamic-update-slice_fusion.20
  83.1 6.8 %attend_forward.1.oa.refs_2_.refs_5_.refs_8_.refs_11_ = bf16[1024,128]{1,0:T(8,128)(2,1)} custom-call(s32[1]{0:T(128)} %bitcast.12.rank, f32[1024,256]{1,0:T(8,128)} %get-tuple-element.128.qkv, f32[1024,128]{1,0:T(8,128)} %get-tuple-element.361.cosine, f32[1024,128]{1,0:T(8,128)} %get-tuple-element.362.sine), custom_call_target="tpu_custom_call" | custom-call | flops 2000000000 | bytes 4000000 | tf_op jit(solution)/shard_map/attend_forward/pallas_call | solution.py:847
  90.6 1.8 collective-permute-start.20
  93.1 12.2 %mamba_forward.1 = (bf16[1024,384]{1,0:T(8,128)(2,1)}, bf16[1024,384]{1,0:T(8,128)(2,1)}, f32[8,128,384]{2,1,0:T(8,128)}) custom-call(s32[1]{0:T(128)} %bitcast.12.rank, f32[1024,384]{1,0:T(8,128)} %get-tuple-element.135.px.px_tail, f32[1024,384]{1,0:T(8,128)} %get-tuple-element.135.px.px_tail, f32[1024,384]{1,0:T(8,128)} %get-tuple-element.136.pz.refs_4_, ...), custom_call_target="tpu_custom_call" | custom-call | flops 4000000000 | bytes 8000000 | tf_op jit(solution)/shard_map/mamba_forward/pallas_call | solution.py:664
  105.4 8.1 %collective-permute-done.20.refs_1_.refs_3_ = bf16[512,512]{1,0:T(8,128)(2,1)S(1)} collective-permute-done((bf16[512,512]{1,0:T(8,128)(2,1)}, bf16[512,512]{1,0:T(8,128)(2,1)S(1)}, u32[]{:S(2)}, u32[]{:S(2)}) %collective-permute-start.20) | collective-permute-done | bytes 524320 | tf_op jit(solution)/shard_map/ppermute | solution.py:19
  114.2 6.2 %mixer_out.1 = (f32[512,1024]{1,0:T(8,128)}, bf16[512,1024]{1,0:T(8,128)(2,1)}) custom-call(s32[1]{0:T(128)} %bitcast.12.rank, bf16[1024,384]{1,0:T(8,128)(2,1)} %get-tuple-element.138.om.refs_1_.refs_4_.refs_7_.refs_10_, bf16[1024,128]{1,0:T(8,128)(2,1)} %attend_forward.1.oa.refs_2_.refs_5_.refs_8_.refs_11_, bf16[256,512]{1,0:T(8,128)(2,1)} %copy-done.39, ...), custom_call_target="tpu_custom_call" | custom-call | flops 1000000000 | bytes 7000000 | tf_op jit(solution)/shard_map/mixer_out/pallas_call | solution.py:1002
  121.2 2.1 constant_dynamic-update-slice_fusion.19
  123.4 2.1 add_convert_fusion.1
  127.4 13.4 %collective-permute-done.23 = bf16[256,1536]{0,1:T(8,128)(2,1)S(1)} collective-permute-done((bf16[256,1536]{0,1:T(8,128)(2,1)}, bf16[256,1536]{0,1:T(8,128)(2,1)S(1)}, u32[]{:S(2)}, u32[]{:S(2)}) %collective-permute-start.23) | collective-permute-done | bytes 786464 | tf_op jit(solution)/shard_map/ppermute | solution.py:19
  143.1 11.3 %collective-permute-done.25 = bf16[256,1024]{1,0:T(8,128)(2,1)S(1)} collective-permute-done((bf16[256,1024]{1,0:T(8,128)(2,1)S(1)}, bf16[256,1024]{1,0:T(8,128)(2,1)S(1)}, u32[]{:S(2)}, u32[]{:S(2)}) %collective-permute-start.25) | collective-permute-done | bytes 524320 | tf_op jit(solution)/shard_map/ppermute | solution.py:19
  157.0 2.0 fusion.12
  162.2 2.0 fusion.15
  172.0 2.3 pad_maximum_fusion.4.refs_1_.refs_3_
  174.3 5.2 %weight_product.4 = (f32[512,512]{1,0:T(8,128)}, bf16[512,512]{1,0:T(8,128)(2,1)}) custom-call(s32[1]{0:T(128)} %bitcast.12.rank, bf16[256,1024]{1,0:T(8,128)(2,1)} %copy-done.14, bf16[512,512]{1,0:T(8,128)(2,1)} %get-tuple-element.152.refs_1_.refs_3_, bf16[256,1024]{1,0:T(8,128)(2,1)} %copy-done.26, bf16[512,512]{1,0:T(8,128)(2,1)} %get-tuple-element.152.refs_1_.refs_3_, ...), custom_call_target="tpu_custom_call" | custom-call | flops 1073741824 | bytes 4194304 | tf_op jit(solution)/shard_map/weight_product/pallas_call | solution.py:162
  179.8 7.0 %weight_product.5 = (f32[512,1024]{1,0:T(8,128)}, bf16[512,1024]{1,0:T(8,128)(2,1)}) custom-call(s32[1]{0:T(128)} %bitcast.12.rank, bf16[256,1024]{1,0:T(8,128)(2,1)} %copy-done.42, bf16[512,1024]{1,0:T(8,128)(2,1)} %pad_maximum_fusion.4.refs_1_.refs_3_, bf16[256,1024]{1,0:T(8,128)(2,1)} %copy-done.75, bf16[512,1024]{1,0:T(8,128)(2,1)} %pad_maximum_fusion.4.refs_1_.refs_3_, ...), custom_call_target="tpu_custom_call" | custom-call | flops 2147483648 | bytes 8388608 | tf_op jit(solution)/shard_map/weight_product/pallas_call | solution.py:162
  187.4 5.3 %collective-permute-done.29 = bf16[256,1024]{1,0:T(8,128)(2,1)} collective-permute-done((bf16[256,1024]{1,0:T(8,128)(2,1)}, bf16[256,1024]{1,0:T(8,128)(2,1)}, u32[]{:S(2)}, u32[]{:S(2)}) %collective-permute-start.29) | collective-permute-done | bytes 524320 | tf_op jit(solution)/shard_map/ppermute | solution.py:19
  192.8 2.5 multiply_reduce_fusion
  195.3 3.6 %fusion.64 = (bf16[256,1024]{1,0:T(8,128)(2,1)S(1)}, f32[256,1024]{1,0:T(8,128)}, bf16[256,1024]{1,0:T(8,128)(2,1)S(1)}) fusion(f32[256]{0:T(256)S(1)} %broadcast_multiply_fusion.1, f32[256,1024]{1,0:T(8,128)S(1)} %get-tuple-element.294, f32[1024]{0:T(1024)S(1)} %mul.230, bf16[256,1024]{1,0:T(8,128)(2,1)} %collective-permute-done.29, ...), kind=kLoop, calls=%fused_computation.216 | loop fusion | flops 7340032 | bytes 7872768 | tf_op jit(solution)/shard_map/convert_element_type | solution.py:1348
  205.7 6.0 %mixer_back.1 = (f32[1024,384]{1,0:T(8,128)}, bf16[1024,128]{1,0:T(8,128)(2,1)}, bf16[1024,384]{1,0:T(8,128)(2,1)}) custom-call(s32[1]{0:T(128)} %bitcast.12.rank, bf16[256,1024]{1,0:T(8,128)(2,1)} %copy-done.8, bf16[256,1024]{1,0:T(8,128)(2,1)} %copy-done.23, bf16[256,1024]{1,0:T(8,128)(2,1)} %copy-done.9, bf16[256,1024]{1,0:T(8,128)(2,1)} %copy-done.24, ...), custom_call_target="tpu_custom_call" | custom-call | flops 1000000000 | bytes 9000000 | tf_op jit(solution)/shard_map/mixer_back/pallas_call | solution.py:1048
  213.5 9.9 %attend_backward.1.refs_14_.g_qkv = bf16[1024,256]{1,0:T(8,128)(2,1)} custom-call(s32[1]{0:T(128)} %bitcast.12.rank, f32[1024,256]{1,0:T(8,128)} %get-tuple-element.128.qkv, f32[1024,128]{1,0:T(8,128)} %get-tuple-element.361.cosine, f32[1024,128]{1,0:T(8,128)} %get-tuple-element.362.sine, bf16[1024,128]{1,0:T(8,128)(2,1)} %get-tuple-element.158.go), custom_call_target="tpu_custom_call" | custom-call | flops 4000000000 | bytes 6000000 | tf_op jit(solution)/shard_map/attend_backward/pallas_call | solution.py:865
  223.5 2.3 convert_add_fusion.1
  227.7 2.1 collective-permute-start.37
  233.2 10.9 %weight_product.6 = (f32[512,1152]{1,0:T(8,128)}, bf16[512,1152]{1,0:T(8,128)(2,1)}) custom-call(s32[1]{0:T(128)} %bitcast.12.rank, bf16[256,1024]{1,0:T(8,128)(2,1)} %copy-done.8, bf16[1024,384]{1,0:T(8,128)(2,1)} %get-tuple-element.138.om.refs_1_.refs_4_.refs_7_.refs_10_, bf16[1024,128]{1,0:T(8,128)(2,1)} %attend_forward.1.oa.refs_2_.refs_5_.refs_8_.refs_11_, ...), custom_call_target="tpu_custom_call" | custom-call | flops 2415919104 | bytes 9437184 | tf_op jit(solution)/shard_map/weight_product/pallas_call | solution.py:162
  249.2 20.8 %mamba_backward.1 = (bf16[1024,512]{1,0:T(8,128)(2,1)}, bf16[1024,256]{1,0:T(8,128)(2,1)}, f32[8,384]{1,0:T(8,128)}, f32[8,256]{1,0:T(8,128)}, f32[16,128]{1,0:T(8,128)}, /*index=5*/f32[8,384]{1,0:T(8,128)}) custom-call(s32[1]{0:T(128)} %bitcast.12.rank, f32[1024,384]{1,0:T(8,128)} %get-tuple-element.135.px.px_tail, ...), custom_call_target="tpu_custom_call" | custom-call | flops 8999999488 | bytes 10000000 | tf_op jit(solution)/shard_map/mamba_backward/pallas_call | solution.py:702
  271.8 1.8 fusion.41
  273.6 5.2 %weight_product.7 = (f32[512,512]{1,0:T(8,128)}, bf16[512,512]{1,0:T(8,128)(2,1)}) custom-call(s32[1]{0:T(128)} %bitcast.12.rank, bf16[1024,1024]{1,0:T(8,128)(2,1)} %get-tuple-element.190.refs_12_.refs_0_.a1, bf16[1024,512]{1,0:T(8,128)(2,1)} %get-tuple-element.173.refs_1_.g_pxs), custom_call_target="tpu_custom_call" | custom-call | flops 1073741824 | bytes 4194304 | tf_op jit(solution)/shard_map/weight_product/pallas_call | solution.py:162
  283.5 2.4 convert_add_fusion
  285.9 1.8 collective-permute-start.44
  287.7 9.0 %project_back.1 = (f32[512,1024]{1,0:T(8,128)}, bf16[512,1024]{1,0:T(8,128)(2,1)}, f32[8,1024]{1,0:T(8,128)}) custom-call(s32[1]{0:T(128)} %bitcast.12.rank, bf16[1024,1024]{1,0:T(8,128)(2,1)} %get-tuple-element.190.refs_12_.refs_0_.a1, bf16[1024,384]{1,0:T(8,128)(2,1)} %get-tuple-element.167.refs_13_.g_pz, bf16[1024,256]{1,0:T(8,128)(2,1)} %attend_backward.1.refs_14_.g_qkv, ...), custom_call_target="tpu_custom_call" | custom-call | flops 3000000000 | bytes 11000000 | tf_op jit(solution)/shard_map/project_back/pallas_call | solution.py:1108
  299.9 2.4 convert_add_fusion.3
  305.4 2.0 collective-permute-start.45
  307.4 2.3 add_convert_fusion.u_own
  313.5 2.1 select_convert_fusion.source
  316.4 2.1 move_blocks.3
  324.4 4.4 %collective-permute-done.51 = bf16[128,512]{1,0:T(8,128)(2,1)S(1)} collective-permute-done((bf16[128,512]{1,0:T(8,128)(2,1)S(1)}, bf16[128,512]{1,0:T(8,128)(2,1)S(1)}, u32[]{:S(2)}, u32[]{:S(2)}) %collective-permute-start.51) | collective-permute-done | bytes 131104 | tf_op jit(solution)/shard_map/ppermute | solution.py:19
  336.1 3.6 %collective-permute-done.52 = f32[88,256]{1,0:T(8,128)S(1)} collective-permute-done((f32[88,256]{1,0:T(8,128)S(1)}, f32[88,256]{1,0:T(8,128)S(1)}, u32[]{:S(2)}, u32[]{:S(2)}) %collective-permute-start.52) | collective-permute-done | bytes 90144 | tf_op jit(solution)/shard_map/ppermute | solution.py:19
  343.7 3.1 input_gradient.1
  (424 shorter events, 116.5 us)
Async XLA Ops:
  2.7 24.4 %collective-permute-start.5 = (bf16[128,512]{1,0:T(8,128)(2,1)}, bf16[128,512]{1,0:T(8,128)(2,1)S(1)}, u32[]{:S(2)}, u32[]{:S(2)}) collective-permute-start(bf16[128,512]{1,0:T(8,128)(2,1)} %get-tuple-element.113), channel_id=1, source_target_pairs={{0,16},{4,20},{8,24},{12,28},{16,0},{20,4},{24,8},{28,12},{1,17},{... | collective-permute-start | bytes 393224 | tf_op jit(solution)/shard_map/ppermute | solution.py:19
  6.7 22.6 %collective-permute-start.6 = (bf16[128,640]{1,0:T(8,128)(2,1)}, bf16[128,640]{1,0:T(8,128)(2,1)S(1)}, u32[]{:S(2)}, u32[]{:S(2)}) collective-permute-start(bf16[128,640]{1,0:T(8,128)(2,1)} %get-tuple-element.114), channel_id=1, source_target_pairs={{0,16},{4,20},{8,24},{12,28},{16,0},{20,4},{24,8},{28,12},{1,17},{... | collective-permute-start | bytes 491528 | tf_op jit(solution)/shard_map/ppermute | solution.py:19
  6.8 41.0 %collective-permute-start = (bf16[256,1024]{1,0:T(8,128)(2,1)}, bf16[256,1024]{1,0:T(8,128)(2,1)S(1)}, u32[]{:S(2)}, u32[]{:S(2)}) collective-permute-start(bf16[256,1024]{1,0:T(8,128)(2,1)} %bitcast.100), channel_id=1, source_target_pairs={{0,2},{1,3},{2,0},{3,1},{4,6},{5,7},{6,4},{7,5},{8,10},{9,11},{10,... | collective-permute-start | bytes 1572872 | tf_op jit(solution)/shard_map/ppermute | solution.py:19
  11.1 10.2 %collective-permute-start.2 = (bf16[34,256]{1,0:T(8,128)(2,1)S(1)}, bf16[34,256]{1,0:T(8,128)(2,1)S(1)}, u32[]{:S(2)}, u32[]{:S(2)}) collective-permute-start(bf16[34,256]{1,0:T(8,128)(2,1)S(1)} %pad_maximum_fusion.21), channel_id=1, source_target_pairs={{0,2},{1,3},{2,0},{3,1},{4,6},{5,7},{6,4},{7,5},{8,10},{9,11},{10,... | collective-permute-start | bytes 52232 | tf_op jit(solution)/shard_map/ppermute | solution.py:19
  24.1 7.4 %collective-permute-start.4 = (bf16[136,256]{1,0:T(8,128)(2,1)S(1)}, bf16[136,256]{1,0:T(8,128)(2,1)S(1)}, u32[]{:S(2)}, u32[]{:S(2)}) collective-permute-start(bf16[136,256]{1,0:T(8,128)(2,1)S(1)} %reshape_reshape.7), channel_id=1, source_target_pairs={{0,16},{4,20},{8,24},{12,28},{16,0},{20,4},{24,8},{28,12},{1,17},{... | collective-permute-start | bytes 208904 | tf_op jit(solution)/shard_map/ppermute | solution.py:19
  27.8 9.2 %collective-permute-start.8 = (bf16[256,512]{1,0:T(8,128)(2,1)S(1)}, bf16[256,512]{1,0:T(8,128)(2,1)S(1)}, u32[]{:S(2)}, u32[]{:S(2)}) collective-permute-start(bf16[256,512]{1,0:T(8,128)(2,1)S(1)} %get-tuple-element.337.refs_0_), channel_id=1, source_target_pairs={{0,8},{4,12},{8,0},{12,4},{16,24},{20,28},{24,16},{28,20},{1,9},{5... | collective-permute-start | bytes 786440 | tf_op jit(solution)/shard_map/ppermute | solution.py:19
  30.1 9.6 %collective-permute-start.9 = (bf16[256,640]{1,0:T(8,128)(2,1)S(1)}, bf16[256,640]{1,0:T(8,128)(2,1)S(1)}, u32[]{:S(2)}, u32[]{:S(2)}) collective-permute-start(bf16[256,640]{1,0:T(8,128)(2,1)S(1)} %get-tuple-element.329.refs_4_), channel_id=1, source_target_pairs={{0,4},{4,0},{8,12},{12,8},{16,20},{20,16},{24,28},{28,24},{1,5},{5... | collective-permute-start | bytes 983048 | tf_op jit(solution)/shard_map/ppermute | solution.py:19
  31.6 11.8 %collective-permute-start.7 = (bf16[272,256]{1,0:T(8,128)(2,1)S(1)}, bf16[272,256]{1,0:T(8,128)(2,1)S(1)}, u32[]{:S(2)}, u32[]{:S(2)}) collective-permute-start(bf16[272,256]{1,0:T(8,128)(2,1)S(1)} %pad_maximum_fusion.15), channel_id=1, source_target_pairs={{0,8},{4,12},{8,0},{12,4},{16,24},{20,28},{24,16},{28,20},{1,9},{5... | collective-permute-start | bytes 417800 | tf_op jit(solution)/shard_map/ppermute | solution.py:19
  37.7 24.7 %collective-permute-start.11 = (bf16[512,512]{1,0:T(8,128)(2,1)}, bf16[512,512]{1,0:T(8,128)(2,1)}, u32[]{:S(2)}, u32[]{:S(2)}) collective-permute-start(bf16[512,512]{1,0:T(8,128)(2,1)} %constant_dynamic-update-slice_fusion.4), channel_id=1, source_target_pairs={{0,4},{4,0},{8,12},{12,8},{16,20},{20,16},{24,28},{28,24},{1,5},{5... | collective-permute-start | bytes 1572872 | tf_op jit(solution)/shard_map/ppermute | solution.py:19
  40.4 24.5 %collective-permute-start.12 = (bf16[512,640]{1,0:T(8,128)(2,1)}, bf16[512,640]{1,0:T(8,128)(2,1)}, u32[]{:S(2)}, u32[]{:S(2)}) collective-permute-start(bf16[512,640]{1,0:T(8,128)(2,1)} %constant_dynamic-update-slice_fusion.7), channel_id=1, source_target_pairs={{0,8},{4,12},{8,0},{12,4},{16,24},{20,28},{24,16},{28,20},{1,9},{5... | collective-permute-start | bytes 1966088 | tf_op jit(solution)/shard_map/ppermute | solution.py:19
  41.6 36.4 %collective-permute-start.13 = (bf16[128,1536]{0,1:T(8,128)(2,1)S(1)}, bf16[128,1536]{0,1:T(8,128)(2,1)S(1)}, u32[]{:S(2)}, u32[]{:S(2)}) collective-permute-start(bf16[128,1536]{0,1:T(8,128)(2,1)S(1)} %pad_maximum_fusion.11), channel_id=1, source_target_pairs={{0,16},{4,20},{8,24},{12,28},{16,0},{20,4},{24,8},{28,12},{1,17},{... | collective-permute-start | bytes 1179656 | tf_op jit(solution)/shard_map/ppermute | solution.py:19
  44.1 12.9 %collective-permute-start.10 = (bf16[544,256]{1,0:T(8,128)(2,1)}, bf16[544,256]{1,0:T(8,128)(2,1)S(1)}, u32[]{:S(2)}, u32[]{:S(2)}) collective-permute-start(bf16[544,256]{1,0:T(8,128)(2,1)} %pad_maximum_fusion.12), channel_id=1, source_target_pairs={{0,4},{4,0},{8,12},{12,8},{16,20},{20,16},{24,28},{28,24},{1,5},{5... | collective-permute-start | bytes 835592 | tf_op jit(solution)/shard_map/ppermute | solution.py:19
  48.9 16.0 %collective-permute-start.1 = (bf16[512,1024]{1,0:T(8,128)(2,1)}, bf16[512,1024]{1,0:T(8,128)(2,1)}, u32[]{:S(2)}, u32[]{:S(2)}) collective-permute-start(bf16[512,1024]{1,0:T(8,128)(2,1)} %pad_maximum_fusion.3.even), channel_id=1, source_target_pairs={{0,1},{1,0},{2,3},{3,2},{4,5},{5,4},{6,7},{7,6},{8,9},{9,8},{10,11... | collective-permute-start | bytes 3145736 | tf_op jit(solution)/shard_map/ppermute | solution.py:19
  57.7 16.4 %collective-permute-start.17 = (bf16[256,1024]{1,0:T(8,128)(2,1)S(1)}, bf16[256,1024]{1,0:T(8,128)(2,1)S(1)}, u32[]{:S(2)}, u32[]{:S(2)}) collective-permute-start(bf16[256,1024]{1,0:T(8,128)(2,1)S(1)} %broadcast_select_fusion.refs_0_), channel_id=1, source_target_pairs={{0,2},{1,3},{2,0},{3,1},{4,6},{5,7},{6,4},{7,5},{8,10},{9,11},{10,... | collective-permute-start | bytes 1572872 | tf_op jit(solution)/shard_map/ppermute | solution.py:19
  62.4 15.6 %collective-permute-start.15 = (bf16[128,512]{1,0:T(8,128)(2,1)S(1)}, bf16[128,512]{1,0:T(8,128)(2,1)S(1)}, u32[]{:S(2)}, u32[]{:S(2)}) collective-permute-start(bf16[128,512]{1,0:T(8,128)(2,1)S(1)} %pad_maximum_fusion.16), channel_id=1, source_target_pairs={{0,16},{4,20},{8,24},{12,28},{16,0},{20,4},{24,8},{28,12},{1,17},{... | collective-permute-start | bytes 393224 | tf_op jit(solution)/shard_map/ppermute | solution.py:19
  75.3 17.8 %collective-permute-start.18 = (bf16[512,1024]{1,0:T(8,128)(2,1)}, bf16[512,1024]{1,0:T(8,128)(2,1)S(1)}, u32[]{:S(2)}, u32[]{:S(2)}) collective-permute-start(bf16[512,1024]{1,0:T(8,128)(2,1)} %pad_maximum_fusion.1), channel_id=1, source_target_pairs={{0,1},{1,0},{2,3},{3,2},{4,5},{5,4},{6,7},{7,6},{8,9},{9,8},{10,11... | collective-permute-start | bytes 3145736 | tf_op jit(solution)/shard_map/ppermute | solution.py:19
  78.8 11.1 %collective-permute-start.16 = (bf16[256,512]{1,0:T(8,128)(2,1)S(1)}, bf16[256,512]{1,0:T(8,128)(2,1)S(1)}, u32[]{:S(2)}, u32[]{:S(2)}) collective-permute-start(bf16[256,512]{1,0:T(8,128)(2,1)S(1)} %get-tuple-element.333.refs_0_), channel_id=1, source_target_pairs={{0,4},{4,0},{8,12},{12,8},{16,20},{20,16},{24,28},{28,24},{1,5},{5... | collective-permute-start | bytes 786440 | tf_op jit(solution)/shard_map/ppermute | solution.py:19
  82.3 23.0 %collective-permute-start.14 = (bf16[256,1536]{0,1:T(8,128)(2,1)}, bf16[256,1536]{0,1:T(8,128)(2,1)}, u32[]{:S(2)}, u32[]{:S(2)}) collective-permute-start(bf16[256,1536]{0,1:T(8,128)(2,1)} %get-tuple-element.324), channel_id=1, source_target_pairs={{0,8},{4,12},{8,0},{12,4},{16,24},{20,28},{24,16},{28,20},{1,9},{5... | collective-permute-start | bytes 2359304 | tf_op jit(solution)/shard_map/ppermute | solution.py:19
  82.5 22.8 %collective-permute-start.19 = (bf16[256,1536]{0,1:T(8,128)(2,1)}, bf16[256,1536]{0,1:T(8,128)(2,1)S(1)}, u32[]{:S(2)}, u32[]{:S(2)}) collective-permute-start(bf16[256,1536]{0,1:T(8,128)(2,1)} %get-tuple-element.324), channel_id=1, source_target_pairs={{0,4},{4,0},{8,12},{12,8},{16,20},{20,16},{24,28},{28,24},{1,5},{5... | collective-permute-start | bytes 2359304 | tf_op jit(solution)/shard_map/ppermute | solution.py:19
  90.6 22.8 %collective-permute-start.20 = (bf16[512,512]{1,0:T(8,128)(2,1)}, bf16[512,512]{1,0:T(8,128)(2,1)S(1)}, u32[]{:S(2)}, u32[]{:S(2)}) collective-permute-start(bf16[512,512]{1,0:T(8,128)(2,1)} %constant_dynamic-update-slice_fusion.14), channel_id=1, source_target_pairs={{0,8},{4,12},{8,0},{12,4},{16,24},{20,28},{24,16},{28,20},{1,9},{5... | collective-permute-start | bytes 1572872 | tf_op jit(solution)/shard_map/ppermute | solution.py:19
  120.6 20.1 %collective-permute-start.23 = (bf16[256,1536]{0,1:T(8,128)(2,1)}, bf16[256,1536]{0,1:T(8,128)(2,1)S(1)}, u32[]{:S(2)}, u32[]{:S(2)}) collective-permute-start(bf16[256,1536]{0,1:T(8,128)(2,1)} %collective-permute-done.14), channel_id=1, source_target_pairs={{0,4},{4,0},{8,12},{12,8},{16,20},{20,16},{24,28},{28,24},{1,5},{5... | collective-permute-start | bytes 2359304 | tf_op jit(solution)/shard_map/ppermute | solution.py:19
  125.6 16.9 %collective-permute-start.22 = (bf16[256,1024]{1,0:T(8,128)(2,1)S(1)}, bf16[256,1024]{1,0:T(8,128)(2,1)S(1)}, u32[]{:S(2)}, u32[]{:S(2)}) collective-permute-start(bf16[256,1024]{1,0:T(8,128)(2,1)S(1)} %get-tuple-element.314), channel_id=1, source_target_pairs={{0,2},{1,3},{2,0},{3,1},{4,6},{5,7},{6,4},{7,5},{8,10},{9,11},{10,... | collective-permute-start | bytes 1572872 | tf_op jit(solution)/shard_map/ppermute | solution.py:19
  140.9 13.5 %collective-permute-start.25 = (bf16[256,1024]{1,0:T(8,128)(2,1)S(1)}, bf16[256,1024]{1,0:T(8,128)(2,1)S(1)}, u32[]{:S(2)}, u32[]{:S(2)}) collective-permute-start(bf16[256,1024]{1,0:T(8,128)(2,1)S(1)} %get-tuple-element.313), channel_id=1, source_target_pairs={{0,2},{1,3},{2,0},{3,1},{4,6},{5,7},{6,4},{7,5},{8,10},{9,11},{10,... | collective-permute-start | bytes 1572872 | tf_op jit(solution)/shard_map/ppermute | solution.py:19
  143.0 12.6 %collective-permute-start.24 = (bf16[256,1024]{1,0:T(8,128)(2,1)S(1)}, bf16[256,1024]{1,0:T(8,128)(2,1)S(1)}, u32[]{:S(2)}, u32[]{:S(2)}) collective-permute-start(bf16[256,1024]{1,0:T(8,128)(2,1)S(1)} %multiply_convert_fusion.5.refs_0_), channel_id=1, source_target_pairs={{0,1},{1,0},{2,3},{3,2},{4,5},{5,4},{6,7},{7,6},{8,9},{9,8},{10,11... | collective-permute-start | bytes 1572872 | tf_op jit(solution)/shard_map/ppermute | solution.py:19
  155.5 5.4 %collective-permute-start.26 = (bf16[256,1024]{1,0:T(8,128)(2,1)S(1)}, bf16[256,1024]{1,0:T(8,128)(2,1)S(1)}, u32[]{:S(2)}, u32[]{:S(2)}) collective-permute-start(bf16[256,1024]{1,0:T(8,128)(2,1)S(1)} %multiply_convert_fusion.3.refs_4_), channel_id=1, source_target_pairs={{0,1},{1,0},{2,3},{3,2},{4,5},{5,4},{6,7},{7,6},{8,9},{9,8},{10,11... | collective-permute-start | bytes 1572872 | tf_op jit(solution)/shard_map/ppermute | solution.py:19
  166.9 20.5 %collective-permute-start.33 = (bf16[256,1024]{1,0:T(8,128)(2,1)}, bf16[256,1024]{1,0:T(8,128)(2,1)}, u32[]{:S(2)}, u32[]{:S(2)}) collective-permute-start(bf16[256,1024]{1,0:T(8,128)(2,1)} %fusion.17), channel_id=1, source_target_pairs={{0,2},{1,3},{2,0},{3,1},{4,6},{5,7},{6,4},{7,5},{8,10},{9,11},{10,... | collective-permute-start | bytes 1572872 | tf_op jit(solution)/shard_map/ppermute | solution.py:19
  169.8 23.0 %collective-permute-start.29 = (bf16[256,1024]{1,0:T(8,128)(2,1)}, bf16[256,1024]{1,0:T(8,128)(2,1)}, u32[]{:S(2)}, u32[]{:S(2)}) collective-permute-start(bf16[256,1024]{1,0:T(8,128)(2,1)} %fusion.16), channel_id=1, source_target_pairs={{0,2},{1,3},{2,0},{3,1},{4,6},{5,7},{6,4},{7,5},{8,10},{9,11},{10,... | collective-permute-start | bytes 1572872 | tf_op jit(solution)/shard_map/ppermute | solution.py:19
  179.5 32.2 %collective-permute-start.31 = (bf16[512,512]{1,0:T(8,128)(2,1)}, bf16[512,512]{1,0:T(8,128)(2,1)}, u32[]{:S(2)}, u32[]{:S(2)}) collective-permute-start(bf16[512,512]{1,0:T(8,128)(2,1)} %get-tuple-element.148), channel_id=1, source_target_pairs={{0,8},{4,12},{8,0},{12,4},{16,24},{20,28},{24,16},{28,20},{1,9},{5... | collective-permute-start | bytes 1572872 | tf_op jit(solution)/shard_map/ppermute | solution.py:19
  186.8 36.6 %collective-permute-start.38 = (bf16[512,1024]{1,0:T(8,128)(2,1)}, bf16[512,1024]{1,0:T(8,128)(2,1)}, u32[]{:S(2)}, u32[]{:S(2)}) collective-permute-start(bf16[512,1024]{1,0:T(8,128)(2,1)} %get-tuple-element.150), channel_id=1, source_target_pairs={{0,4},{4,0},{8,12},{12,8},{16,20},{20,16},{24,28},{28,24},{1,5},{5... | collective-permute-start | bytes 3145736 | tf_op jit(solution)/shard_map/ppermute | solution.py:19
  198.9 5.2 %collective-permute-start.32 = (bf16[256,1024]{1,0:T(8,128)(2,1)S(1)}, bf16[256,1024]{1,0:T(8,128)(2,1)S(1)}, u32[]{:S(2)}, u32[]{:S(2)}) collective-permute-start(bf16[256,1024]{1,0:T(8,128)(2,1)S(1)} %get-tuple-element.291.g0.refs_0_), channel_id=1, source_target_pairs={{0,1},{1,0},{2,3},{3,2},{4,5},{5,4},{6,7},{7,6},{8,9},{9,8},{10,11... | collective-permute-start | bytes 1572872 | tf_op jit(solution)/shard_map/ppermute | solution.py:19
  204.0 25.7 %collective-permute-start.30 = (bf16[512,1024]{1,0:T(8,128)(2,1)}, bf16[512,1024]{1,0:T(8,128)(2,1)}, u32[]{:S(2)}, u32[]{:S(2)}) collective-permute-start(bf16[512,1024]{1,0:T(8,128)(2,1)} %pad_maximum_fusion.6), channel_id=1, source_target_pairs={{0,1},{1,0},{2,3},{3,2},{4,5},{5,4},{6,7},{7,6},{8,9},{9,8},{10,11... | collective-permute-start | bytes 3145736 | tf_op jit(solution)/shard_map/ppermute | solution.py:19
  212.9 13.2 %collective-permute-start.36 = (bf16[256,512]{1,0:T(8,128)(2,1)S(1)}, bf16[256,512]{1,0:T(8,128)(2,1)}, u32[]{:S(2)}, u32[]{:S(2)}) collective-permute-start(bf16[256,512]{1,0:T(8,128)(2,1)S(1)} %get-tuple-element.310), channel_id=1, source_target_pairs={{0,4},{4,0},{8,12},{12,8},{16,20},{20,16},{24,28},{28,24},{1,5},{5... | collective-permute-start | bytes 786440 | tf_op jit(solution)/shard_map/ppermute | solution.py:19
  225.8 18.4 %collective-permute-start.39 = (bf16[256,1024]{1,0:T(8,128)(2,1)S(1)}, bf16[256,1024]{1,0:T(8,128)(2,1)}, u32[]{:S(2)}, u32[]{:S(2)}) collective-permute-start(bf16[256,1024]{1,0:T(8,128)(2,1)S(1)} %get-tuple-element.300), channel_id=1, source_target_pairs={{0,8},{4,12},{8,0},{12,4},{16,24},{20,28},{24,16},{28,20},{1,9},{5... | collective-permute-start | bytes 1572872 | tf_op jit(solution)/shard_map/ppermute | solution.py:19
  227.7 42.3 %collective-permute-start.37 = (bf16[128,512]{1,0:T(8,128)(2,1)}, bf16[128,512]{1,0:T(8,128)(2,1)S(1)}, u32[]{:S(2)}, u32[]{:S(2)}) collective-permute-start(bf16[128,512]{1,0:T(8,128)(2,1)} %fusion.48), channel_id=1, source_target_pairs={{0,16},{4,20},{8,24},{12,28},{16,0},{20,4},{24,8},{28,12},{1,17},{... | collective-permute-start | bytes 393224 | tf_op jit(solution)/shard_map/ppermute | solution.py:19
  245.2 26.6 %collective-permute-start.40 = (bf16[128,1024]{1,0:T(8,128)(2,1)S(1)}, bf16[128,1024]{1,0:T(8,128)(2,1)S(1)}, u32[]{:S(2)}, u32[]{:S(2)}) collective-permute-start(bf16[128,1024]{1,0:T(8,128)(2,1)S(1)} %fusion.42), channel_id=1, source_target_pairs={{0,16},{4,20},{8,24},{12,28},{16,0},{20,4},{24,8},{28,12},{1,17},{... | collective-permute-start | bytes 786440 | tf_op jit(solution)/shard_map/ppermute | solution.py:19
  246.1 37.0 %collective-permute-start.41 = (bf16[512,1152]{1,0:T(8,128)(2,1)}, bf16[512,1152]{1,0:T(8,128)(2,1)}, u32[]{:S(2)}, u32[]{:S(2)}) collective-permute-start(bf16[512,1152]{1,0:T(8,128)(2,1)} %get-tuple-element.168), channel_id=1, source_target_pairs={{0,4},{4,0},{8,12},{12,8},{16,20},{20,16},{24,28},{28,24},{1,5},{5... | collective-permute-start | bytes 3538952 | tf_op jit(solution)/shard_map/ppermute | solution.py:19
  247.6 64.5 %collective-permute-start.35 = (bf16[256,1024]{1,0:T(8,128)(2,1)}, bf16[256,1024]{1,0:T(8,128)(2,1)}, u32[]{:S(2)}, u32[]{:S(2)}) collective-permute-start(bf16[256,1024]{1,0:T(8,128)(2,1)} %slice.490), channel_id=1, source_target_pairs={{0,2},{1,3},{2,0},{3,1},{4,6},{5,7},{6,4},{7,5},{8,10},{9,11},{10,... | collective-permute-start | bytes 1572872 | tf_op jit(solution)/shard_map/ppermute | solution.py:19
  278.8 19.8 %collective-permute-start.43 = (bf16[512,512]{1,0:T(8,128)(2,1)}, bf16[512,512]{1,0:T(8,128)(2,1)}, u32[]{:S(2)}, u32[]{:S(2)}) collective-permute-start(bf16[512,512]{1,0:T(8,128)(2,1)} %get-tuple-element.177), channel_id=1, source_target_pairs={{0,4},{4,0},{8,12},{12,8},{16,20},{20,16},{24,28},{28,24},{1,5},{5... | collective-permute-start | bytes 1572872 | tf_op jit(solution)/shard_map/ppermute | solution.py:19
  285.9 17.7 %collective-permute-start.44 = (bf16[256,1152]{1,0:T(8,128)(2,1)}, bf16[256,1152]{1,0:T(8,128)(2,1)}, u32[]{:S(2)}, u32[]{:S(2)}) collective-permute-start(bf16[256,1152]{1,0:T(8,128)(2,1)} %get-tuple-element.298), channel_id=1, source_target_pairs={{0,8},{4,12},{8,0},{12,4},{16,24},{20,28},{24,16},{28,20},{1,9},{5... | collective-permute-start | bytes 1769480 | tf_op jit(solution)/shard_map/ppermute | solution.py:19
  296.8 10.6 %collective-permute-start.42 = (bf16[512,1024]{1,0:T(8,128)(2,1)}, bf16[512,1024]{1,0:T(8,128)(2,1)}, u32[]{:S(2)}, u32[]{:S(2)}) collective-permute-start(bf16[512,1024]{1,0:T(8,128)(2,1)} %get-tuple-element.183), channel_id=1, source_target_pairs={{0,1},{1,0},{2,3},{3,2},{4,5},{5,4},{6,7},{7,6},{8,9},{9,8},{10,11... | collective-permute-start | bytes 3145736 | tf_op jit(solution)/shard_map/ppermute | solution.py:19
  299.4 10.3 %collective-permute-start.46 = (f32[528,256]{1,0:T(8,128)}, f32[528,256]{1,0:T(8,128)}, u32[]{:S(2)}, u32[]{:S(2)}) collective-permute-start(f32[528,256]{1,0:T(8,128)} %pad_maximum_fusion.8), channel_id=1, source_target_pairs={{0,1},{1,0},{2,3},{3,2},{4,5},{5,4},{6,7},{7,6},{8,9},{9,8},{10,11... | collective-permute-start | bytes 1622024 | tf_op jit(solution)/shard_map/ppermute | solution.py:19
  302.3 16.2 %collective-permute-start.48 = (bf16[256,512]{1,0:T(8,128)(2,1)}, bf16[256,512]{1,0:T(8,128)(2,1)}, u32[]{:S(2)}, u32[]{:S(2)}) collective-permute-start(bf16[256,512]{1,0:T(8,128)(2,1)} %get-tuple-element.308), channel_id=1, source_target_pairs={{0,8},{4,12},{8,0},{12,4},{16,24},{20,28},{24,16},{28,20},{1,9},{5... | collective-permute-start | bytes 786440 | tf_op jit(solution)/shard_map/ppermute | solution.py:19
  305.4 27.9 %collective-permute-start.45 = (bf16[128,1152]{1,0:T(8,128)(2,1)}, bf16[128,1152]{1,0:T(8,128)(2,1)}, u32[]{:S(2)}, u32[]{:S(2)}) collective-permute-start(bf16[128,1152]{1,0:T(8,128)(2,1)} %fusion.39), channel_id=1, source_target_pairs={{0,16},{4,20},{8,24},{12,28},{16,0},{20,4},{24,8},{28,12},{1,17},{... | collective-permute-start | bytes 884744 | tf_op jit(solution)/shard_map/ppermute | solution.py:19
  313.0 9.0 %collective-permute-start.47 = (f32[272,256]{1,0:T(8,128)}, f32[272,256]{1,0:T(8,128)S(1)}, u32[]{:S(2)}, u32[]{:S(2)}) collective-permute-start(f32[272,256]{1,0:T(8,128)} %pad_maximum_fusion.13), channel_id=1, source_target_pairs={{0,2},{1,3},{2,0},{3,1},{4,6},{5,7},{6,4},{7,5},{8,10},{9,11},{10,... | collective-permute-start | bytes 835592 | tf_op jit(solution)/shard_map/ppermute | solution.py:19
  318.5 14.0 %collective-permute-start.50 = (bf16[256,1024]{1,0:T(8,128)(2,1)}, bf16[256,1024]{1,0:T(8,128)(2,1)S(1)}, u32[]{:S(2)}, u32[]{:S(2)}) collective-permute-start(bf16[256,1024]{1,0:T(8,128)(2,1)} %slice.504), channel_id=1, source_target_pairs={{0,2},{1,3},{2,0},{3,1},{4,6},{5,7},{6,4},{7,5},{8,10},{9,11},{10,... | collective-permute-start | bytes 1572872 | tf_op jit(solution)/shard_map/ppermute | solution.py:19
  321.0 7.8 %collective-permute-start.51 = (bf16[128,512]{1,0:T(8,128)(2,1)S(1)}, bf16[128,512]{1,0:T(8,128)(2,1)S(1)}, u32[]{:S(2)}, u32[]{:S(2)}) collective-permute-start(bf16[128,512]{1,0:T(8,128)(2,1)S(1)} %fusion.46), channel_id=1, source_target_pairs={{0,16},{4,20},{8,24},{12,28},{16,0},{20,4},{24,8},{28,12},{1,17},{... | collective-permute-start | bytes 393224 | tf_op jit(solution)/shard_map/ppermute | solution.py:19
  322.9 8.3 %collective-permute-start.49 = (f32[152,256]{1,0:T(8,128)S(1)}, f32[152,256]{1,0:T(8,128)S(1)}, u32[]{:S(2)}, u32[]{:S(2)}) collective-permute-start(f32[152,256]{1,0:T(8,128)S(1)} %pad_maximum_fusion.14), channel_id=1, source_target_pairs={{0,4},{4,0},{8,12},{12,8},{16,20},{20,16},{24,28},{28,24},{1,5},{5... | collective-permute-start | bytes 466952 | tf_op jit(solution)/shard_map/ppermute | solution.py:19
  339.7 7.1 %collective-permute-start.53 = (f32[56,256]{1,0:T(8,128)S(1)}, f32[56,256]{1,0:T(8,128)S(1)}, u32[]{:S(2)}, u32[]{:S(2)}) collective-permute-start(f32[56,256]{1,0:T(8,128)S(1)} %pad_maximum_fusion.19), channel_id=1, source_target_pairs={{0,16},{4,20},{8,24},{12,28},{16,0},{20,4},{24,8},{28,12},{1,17},{... | collective-permute-start | bytes 172040 | tf_op jit(solution)/shard_map/ppermute | solution.py:19
  (86 other events, 630.5 us)

commit v2 on v1

--- a/solution.py
+++ b/solution.py
@@ -1212,15 +1212,20 @@
     small_rows = -(-parts.shape[0] // n2)
     parts = jnp.pad(parts, (0, small_rows * n2 - parts.shape[0])).reshape(small_rows, n2)
     pack_s = jnp.concatenate([state_proj, parts], axis=0).astype(bf16)
-    pack_o = jnp.concatenate([mamba_out.T.astype(bf16), attend_out.T.astype(bf16)], axis=1)
-    pack_m = jnp.concatenate(
-        [mlp_gate.astype(bf16), mlp_up.astype(bf16), mlp_down.T.astype(bf16)], axis=1
-    )
     ranked = in_rank_order(pack_s, y, core)
     third = Gather(ranked.reshape(-1, n2), "dp", False)
     sent_x = first.until(2)
     sent_z = second.until(2)
     third.until(2, sent_x, sent_z)
+    late = (mamba_out, attend_out, mlp_gate, mlp_up, mlp_down, conv_mamba)
+    late = late + (step_bias, decay_log, skip_gain)
+    late = lax.optimization_barrier(late + (sent_x, sent_z))[: len(late)]
+    mamba_out, attend_out, mlp_gate, mlp_up, mlp_down, conv_mamba = late[:6]
+    step_bias, decay_log, skip_gain = late[6:]
+    pack_o = jnp.concatenate([mamba_out.T.astype(bf16), attend_out.T.astype(bf16)], axis=1)
+    pack_m = jnp.concatenate(
+        [mlp_gate.astype(bf16), mlp_up.astype(bf16), mlp_down.T.astype(bf16)], axis=1
+    )
     far_x = first.advance()
     far_z = second.advance()
     third.advance(far_x, far_z)

time: 357 us -> 354 us (level)
    unnamed x173 -> x167, local copies, waits for them, and re-layouts: 22.1 us -> 22.3 us
where the time goes in v2:
time: 354 us; the launch traced here: 348 us
  Pallas kernels  117 us (33%)
  waiting for transfers between devices  62.2 us (18%)
  other arithmetic  55.8 us (16%)
  starting transfers between devices  51.6 us (15%)
  local copies, waits for them, and re-layouts  45.3 us (13%)
  matrix products  12.3 us (3%)
    ppermute x54, waiting for transfers between devices, flip(): return lax.ppermute(value, axis, [(i, i ^ mask) for i in range(size)])  62.2 us
    ppermute x54, starting transfers between devices, flip(): return lax.ppermute(value, axis, [(i, i ^ mask) for i in range(size)])  51.6 us
    pallas_call x4, Pallas kernels, product(): pl.pallas_call(functools.partial(product_kernel, shapes), grid_spec=pltpu...  28.3 us
    unnamed x167, local copies, waits for them, and re-layouts  22.3 us
    pallas_call x1, Pallas kernels, mamba_bwd(): pl.pallas_call(functools.partial(mamba_bwd_kernel, heads), grid_spec=pltp...  20.8 us
    pallas_call x1, Pallas kernels, mamba_fwd(): pl.pallas_call(functools.partial(mamba_fwd_kernel, heads), grid_spec=pltp...  12.2 us
    pallas_call x1, Pallas kernels, attend_bwd(): pl.pallas_call(functools.partial(attend_bwd_kernel, HEAD ** (-0.5)), grid...  9.96 us
    pallas_call x1, Pallas kernels, project(): pl.pallas_call(functools.partial(project_kernel, order, chans), grid_spec...  9.17 us
  transfers between devices with their start and end apart: 54, of which 14 were waited for; matrix products, arithmetic and copies ran while one was open for 28% of the time, Pallas kernels for 31%

profile of v2, /device:TPU:0, one launch (start us, length us, event | category | flops | bytes accessed | tf_op | source)
XLA Modules:
  0.0 347.6 jit_solution(14795009268875114558)
XLA Ops:
  0.7 1.9 pack_weights.1
  2.6 4.1 %collective-permute-start.5 = (bf16[128,512]{1,0:T(8,128)(2,1)}, bf16[128,512]{1,0:T(8,128)(2,1)S(1)}, u32[]{:S(2)}, u32[]{:S(2)}) collective-permute-start(bf16[128,512]{1,0:T(8,128)(2,1)} %get-tuple-element.122), channel_id=1, source_target_pairs={{0,16},{4,20},{8,24},{12,28},{16,0},{20,4},{24,8},{28,12},{1,17},{... | collective-permute-start | bytes 393224 | tf_op jit(solution)/shard_map/ppermute | solution.py:19
  6.6 1.8 collective-permute-start
  15.8 2.0 fusion.50
  17.8 1.9 pad_maximum_fusion.9
  22.3 3.0 collective-permute-start.4
  32.4 2.9 collective-permute-done.8.refs_1_
  43.0 2.0 move_blocks.2
  47.3 7.4 %collective-permute-done.10 = bf16[544,256]{1,0:T(8,128)(2,1)S(1)} collective-permute-done((bf16[544,256]{1,0:T(8,128)(2,1)}, bf16[544,256]{1,0:T(8,128)(2,1)S(1)}, u32[]{:S(2)}, u32[]{:S(2)}) %collective-permute-start.10) | collective-permute-done | bytes 278560 | tf_op jit(solution)/shard_map/ppermute | solution.py:19
  59.7 2.8 collective-permute-done.12.refs_5_.refs_7_
  62.5 9.2 %norm_project.1 = (bf16[1024,1024]{1,0:T(8,128)(2,1)}, bf16[512,1024]{1,0:T(8,128)(2,1)}, f32[1024,384]{1,0:T(8,128)}, f32[1024,384]{1,0:T(8,128)}, f32[1024,256...) custom-call(s32[1]{0:T(128)} %bitcast.scalars.me, bf16[512,1024]{1,0:T(8,128)(2,1)} %pad_maximum_fusion.3.even, ...), custom_call_target="tpu_custom_call" | custom-call | flops 3000000000 | bytes 14000000 | tf_op jit(solution)/shard_map/norm_project/pallas_call | solution.py:947
  77.8 2.0 constant_dynamic-update-slice_fusion.20
  80.4 6.8 %attend_forward.1.oa.refs_2_.refs_5_.refs_8_.refs_11_ = bf16[1024,128]{1,0:T(8,128)(2,1)} custom-call(s32[1]{0:T(128)} %bitcast.12.rank, f32[1024,256]{1,0:T(8,128)} %get-tuple-element.142.qkv, f32[1024,128]{1,0:T(8,128)} %get-tuple-element.379.cosine, f32[1024,128]{1,0:T(8,128)} %get-tuple-element.380.sine), custom_call_target="tpu_custom_call" | custom-call | flops 2000000000 | bytes 4000000 | tf_op jit(solution)/shard_map/attend_forward/pallas_call | solution.py:847
  88.0 2.0 collective-permute-start.20
  90.6 12.2 %mamba_forward.1 = (bf16[1024,384]{1,0:T(8,128)(2,1)}, bf16[1024,384]{1,0:T(8,128)(2,1)}, f32[8,128,384]{2,1,0:T(8,128)}) custom-call(s32[1]{0:T(128)} %bitcast.12.rank, f32[1024,384]{1,0:T(8,128)} %get-tuple-element.149.px.px_tail, f32[1024,384]{1,0:T(8,128)} %get-tuple-element.149.px.px_tail, f32[1024,384]{1,0:T(8,128)} %get-tuple-element.150.pz.refs_4_, ...), custom_call_target="tpu_custom_call" | custom-call | flops 4000000000 | bytes 8000000 | tf_op jit(solution)/shard_map/mamba_forward/pallas_call | solution.py:664
  102.9 8.1 %collective-permute-done.20.refs_1_.refs_3_ = bf16[512,512]{1,0:T(8,128)(2,1)S(1)} collective-permute-done((bf16[512,512]{1,0:T(8,128)(2,1)}, bf16[512,512]{1,0:T(8,128)(2,1)S(1)}, u32[]{:S(2)}, u32[]{:S(2)}) %collective-permute-start.20) | collective-permute-done | bytes 524320 | tf_op jit(solution)/shard_map/ppermute | solution.py:19
  111.8 6.2 %mixer_out.1 = (f32[512,1024]{1,0:T(8,128)}, bf16[512,1024]{1,0:T(8,128)(2,1)}) custom-call(s32[1]{0:T(128)} %bitcast.12.rank, bf16[1024,384]{1,0:T(8,128)(2,1)} %get-tuple-element.156.om.refs_1_.refs_4_.refs_7_.refs_10_, bf16[1024,128]{1,0:T(8,128)(2,1)} %attend_forward.1.oa.refs_2_.refs_5_.refs_8_.refs_11_, bf16[256,512]{1,0:T(8,128)(2,1)} %copy-done.39, ...), custom_call_target="tpu_custom_call" | custom-call | flops 1000000000 | bytes 7000000 | tf_op jit(solution)/shard_map/mixer_out/pallas_call | solution.py:1002
  118.7 2.1 constant_dynamic-update-slice_fusion.19
  120.9 2.1 add_convert_fusion.1
  124.9 13.4 %collective-permute-done.23 = bf16[256,1536]{0,1:T(8,128)(2,1)S(1)} collective-permute-done((bf16[256,1536]{0,1:T(8,128)(2,1)}, bf16[256,1536]{0,1:T(8,128)(2,1)S(1)}, u32[]{:S(2)}, u32[]{:S(2)}) %collective-permute-start.23) | collective-permute-done | bytes 786464 | tf_op jit(solution)/shard_map/ppermute | solution.py:19
  140.6 11.4 %collective-permute-done.25 = bf16[256,1024]{1,0:T(8,128)(2,1)S(1)} collective-permute-done((bf16[256,1024]{1,0:T(8,128)(2,1)S(1)}, bf16[256,1024]{1,0:T(8,128)(2,1)S(1)}, u32[]{:S(2)}, u32[]{:S(2)}) %collective-permute-start.25) | collective-permute-done | bytes 524320 | tf_op jit(solution)/shard_map/ppermute | solution.py:19
  154.5 2.0 fusion.12
  159.7 2.0 fusion.15
  169.4 2.3 pad_maximum_fusion.4.refs_1_.refs_3_
  171.7 5.2 %weight_product.4 = (f32[512,512]{1,0:T(8,128)}, bf16[512,512]{1,0:T(8,128)(2,1)}) custom-call(s32[1]{0:T(128)} %bitcast.12.rank, bf16[256,1024]{1,0:T(8,128)(2,1)} %copy-done.14, bf16[512,512]{1,0:T(8,128)(2,1)} %get-tuple-element.170.refs_1_.refs_3_, bf16[256,1024]{1,0:T(8,128)(2,1)} %copy-done.26, bf16[512,512]{1,0:T(8,128)(2,1)} %get-tuple-element.170.refs_1_.refs_3_, ...), custom_call_target="tpu_custom_call" | custom-call | flops 1073741824 | bytes 4194304 | tf_op jit(solution)/shard_map/weight_product/pallas_call | solution.py:162
  177.3 6.9 %weight_product.5 = (f32[512,1024]{1,0:T(8,128)}, bf16[512,1024]{1,0:T(8,128)(2,1)}) custom-call(s32[1]{0:T(128)} %bitcast.12.rank, bf16[256,1024]{1,0:T(8,128)(2,1)} %copy-done.42, bf16[512,1024]{1,0:T(8,128)(2,1)} %pad_maximum_fusion.4.refs_1_.refs_3_, bf16[256,1024]{1,0:T(8,128)(2,1)} %copy-done.73, bf16[512,1024]{1,0:T(8,128)(2,1)} %pad_maximum_fusion.4.refs_1_.refs_3_, ...), custom_call_target="tpu_custom_call" | custom-call | flops 2147483648 | bytes 8388608 | tf_op jit(solution)/shard_map/weight_product/pallas_call | solution.py:162
  184.8 5.4 %collective-permute-done.29 = bf16[256,1024]{1,0:T(8,128)(2,1)} collective-permute-done((bf16[256,1024]{1,0:T(8,128)(2,1)}, bf16[256,1024]{1,0:T(8,128)(2,1)}, u32[]{:S(2)}, u32[]{:S(2)}) %collective-permute-start.29) | collective-permute-done | bytes 524320 | tf_op jit(solution)/shard_map/ppermute | solution.py:19
  190.2 2.5 multiply_reduce_fusion
  192.8 3.6 %fusion.64 = (bf16[256,1024]{1,0:T(8,128)(2,1)S(1)}, f32[256,1024]{1,0:T(8,128)}, bf16[256,1024]{1,0:T(8,128)(2,1)S(1)}) fusion(f32[256]{0:T(256)S(1)} %broadcast_multiply_fusion.1, f32[256,1024]{1,0:T(8,128)S(1)} %get-tuple-element.312, f32[1024]{0:T(1024)S(1)} %mul.230, bf16[256,1024]{1,0:T(8,128)(2,1)} %collective-permute-done.29, ...), kind=kLoop, calls=%fused_computation.216 | loop fusion | flops 7340032 | bytes 7872768 | tf_op jit(solution)/shard_map/convert_element_type | solution.py:1353
  203.2 6.0 %mixer_back.1 = (f32[1024,384]{1,0:T(8,128)}, bf16[1024,128]{1,0:T(8,128)(2,1)}, bf16[1024,384]{1,0:T(8,128)(2,1)}) custom-call(s32[1]{0:T(128)} %bitcast.12.rank, bf16[256,1024]{1,0:T(8,128)(2,1)} %copy-done.8, bf16[256,1024]{1,0:T(8,128)(2,1)} %copy-done.23, bf16[256,1024]{1,0:T(8,128)(2,1)} %copy-done.9, bf16[256,1024]{1,0:T(8,128)(2,1)} %copy-done.24, ...), custom_call_target="tpu_custom_call" | custom-call | flops 1000000000 | bytes 9000000 | tf_op jit(solution)/shard_map/mixer_back/pallas_call | solution.py:1048
  211.0 10.0 %attend_backward.1.refs_14_.g_qkv = bf16[1024,256]{1,0:T(8,128)(2,1)} custom-call(s32[1]{0:T(128)} %bitcast.12.rank, f32[1024,256]{1,0:T(8,128)} %get-tuple-element.142.qkv, f32[1024,128]{1,0:T(8,128)} %get-tuple-element.379.cosine, f32[1024,128]{1,0:T(8,128)} %get-tuple-element.380.sine, bf16[1024,128]{1,0:T(8,128)(2,1)} %get-tuple-element.176.go), custom_call_target="tpu_custom_call" | custom-call | flops 4000000000 | bytes 6000000 | tf_op jit(solution)/shard_map/attend_backward/pallas_call | solution.py:865
  221.0 2.3 convert_add_fusion.1
  225.2 2.3 collective-permute-start.37
  230.9 10.9 %weight_product.6 = (f32[512,1152]{1,0:T(8,128)}, bf16[512,1152]{1,0:T(8,128)(2,1)}) custom-call(s32[1]{0:T(128)} %bitcast.12.rank, bf16[256,1024]{1,0:T(8,128)(2,1)} %copy-done.8, bf16[1024,384]{1,0:T(8,128)(2,1)} %get-tuple-element.156.om.refs_1_.refs_4_.refs_7_.refs_10_, bf16[1024,128]{1,0:T(8,128)(2,1)} %attend_forward.1.oa.refs_2_.refs_5_.refs_8_.refs_11_, ...), custom_call_target="tpu_custom_call" | custom-call | flops 2415919104 | bytes 9437184 | tf_op jit(solution)/shard_map/weight_product/pallas_call | solution.py:162
  246.6 20.8 %mamba_backward.1 = (bf16[1024,512]{1,0:T(8,128)(2,1)}, bf16[1024,256]{1,0:T(8,128)(2,1)}, f32[8,384]{1,0:T(8,128)}, f32[8,256]{1,0:T(8,128)}, f32[16,128]{1,0:T(8,128)}, /*index=5*/f32[8,384]{1,0:T(8,128)}) custom-call(s32[1]{0:T(128)} %bitcast.12.rank, f32[1024,384]{1,0:T(8,128)} %get-tuple-element.149.px.px_tail, ...), custom_call_target="tpu_custom_call" | custom-call | flops 8999999488 | bytes 10000000 | tf_op jit(solution)/shard_map/mamba_backward/pallas_call | solution.py:702
  269.2 1.8 fusion.41
  271.1 5.2 %weight_product.7 = (f32[512,512]{1,0:T(8,128)}, bf16[512,512]{1,0:T(8,128)(2,1)}) custom-call(s32[1]{0:T(128)} %bitcast.12.rank, bf16[1024,1024]{1,0:T(8,128)(2,1)} %get-tuple-element.208.refs_12_.refs_0_.a1, bf16[1024,512]{1,0:T(8,128)(2,1)} %get-tuple-element.191.refs_1_.g_pxs), custom_call_target="tpu_custom_call" | custom-call | flops 1073741824 | bytes 4194304 | tf_op jit(solution)/shard_map/weight_product/pallas_call | solution.py:162
  281.0 2.4 convert_add_fusion
  283.4 1.8 collective-permute-start.44
  285.2 9.0 %project_back.1 = (f32[512,1024]{1,0:T(8,128)}, bf16[512,1024]{1,0:T(8,128)(2,1)}, f32[8,1024]{1,0:T(8,128)}) custom-call(s32[1]{0:T(128)} %bitcast.12.rank, bf16[1024,1024]{1,0:T(8,128)(2,1)} %get-tuple-element.208.refs_12_.refs_0_.a1, bf16[1024,384]{1,0:T(8,128)(2,1)} %get-tuple-element.185.refs_13_.g_pz, bf16[1024,256]{1,0:T(8,128)(2,1)} %attend_backward.1.refs_14_.g_qkv, ...), custom_call_target="tpu_custom_call" | custom-call | flops 3000000000 | bytes 11000000 | tf_op jit(solution)/shard_map/project_back/pallas_call | solution.py:1108
  297.4 2.4 convert_add_fusion.3
  302.9 2.3 collective-permute-start.45
  305.2 2.3 add_convert_fusion.u_own
  311.3 2.1 select_convert_fusion.source
  314.2 2.1 move_blocks.3
  321.9 4.7 %collective-permute-done.51 = bf16[128,512]{1,0:T(8,128)(2,1)S(1)} collective-permute-done((bf16[128,512]{1,0:T(8,128)(2,1)S(1)}, bf16[128,512]{1,0:T(8,128)(2,1)S(1)}, u32[]{:S(2)}, u32[]{:S(2)}) %collective-permute-start.51) | collective-permute-done | bytes 131104 | tf_op jit(solution)/shard_map/ppermute | solution.py:19
  333.8 3.6 %collective-permute-done.52 = f32[88,256]{1,0:T(8,128)S(1)} collective-permute-done((f32[88,256]{1,0:T(8,128)S(1)}, f32[88,256]{1,0:T(8,128)S(1)}, u32[]{:S(2)}, u32[]{:S(2)}) %collective-permute-start.52) | collective-permute-done | bytes 90144 | tf_op jit(solution)/shard_map/ppermute | solution.py:19
  341.2 3.1 input_gradient.1
  (420 shorter events, 114.7 us)
Async XLA Ops:
  2.6 22.7 %collective-permute-start.5 = (bf16[128,512]{1,0:T(8,128)(2,1)}, bf16[128,512]{1,0:T(8,128)(2,1)S(1)}, u32[]{:S(2)}, u32[]{:S(2)}) collective-permute-start(bf16[128,512]{1,0:T(8,128)(2,1)} %get-tuple-element.122), channel_id=1, source_target_pairs={{0,16},{4,20},{8,24},{12,28},{16,0},{20,4},{24,8},{28,12},{1,17},{... | collective-permute-start | bytes 393224 | tf_op jit(solution)/shard_map/ppermute | solution.py:19
  6.6 20.9 %collective-permute-start.6 = (bf16[128,640]{1,0:T(8,128)(2,1)}, bf16[128,640]{1,0:T(8,128)(2,1)S(1)}, u32[]{:S(2)}, u32[]{:S(2)}) collective-permute-start(bf16[128,640]{1,0:T(8,128)(2,1)} %get-tuple-element.123), channel_id=1, source_target_pairs={{0,16},{4,20},{8,24},{12,28},{16,0},{20,4},{24,8},{28,12},{1,17},{... | collective-permute-start | bytes 491528 | tf_op jit(solution)/shard_map/ppermute | solution.py:19
  6.6 39.5 %collective-permute-start = (bf16[256,1024]{1,0:T(8,128)(2,1)}, bf16[256,1024]{1,0:T(8,128)(2,1)S(1)}, u32[]{:S(2)}, u32[]{:S(2)}) collective-permute-start(bf16[256,1024]{1,0:T(8,128)(2,1)} %bitcast.100), channel_id=1, source_target_pairs={{0,2},{1,3},{2,0},{3,1},{4,6},{5,7},{6,4},{7,5},{8,10},{9,11},{10,... | collective-permute-start | bytes 1572872 | tf_op jit(solution)/shard_map/ppermute | solution.py:19
  11.0 9.9 %collective-permute-start.2 = (bf16[34,256]{1,0:T(8,128)(2,1)S(1)}, bf16[34,256]{1,0:T(8,128)(2,1)S(1)}, u32[]{:S(2)}, u32[]{:S(2)}) collective-permute-start(bf16[34,256]{1,0:T(8,128)(2,1)S(1)} %pad_maximum_fusion.21), channel_id=1, source_target_pairs={{0,2},{1,3},{2,0},{3,1},{4,6},{5,7},{6,4},{7,5},{8,10},{9,11},{10,... | collective-permute-start | bytes 52232 | tf_op jit(solution)/shard_map/ppermute | solution.py:19
  22.3 7.5 %collective-permute-start.4 = (bf16[136,256]{1,0:T(8,128)(2,1)S(1)}, bf16[136,256]{1,0:T(8,128)(2,1)S(1)}, u32[]{:S(2)}, u32[]{:S(2)}) collective-permute-start(bf16[136,256]{1,0:T(8,128)(2,1)S(1)} %reshape_reshape.7), channel_id=1, source_target_pairs={{0,16},{4,20},{8,24},{12,28},{16,0},{20,4},{24,8},{28,12},{1,17},{... | collective-permute-start | bytes 208904 | tf_op jit(solution)/shard_map/ppermute | solution.py:19
  25.9 9.4 %collective-permute-start.8 = (bf16[256,512]{1,0:T(8,128)(2,1)}, bf16[256,512]{1,0:T(8,128)(2,1)S(1)}, u32[]{:S(2)}, u32[]{:S(2)}) collective-permute-start(bf16[256,512]{1,0:T(8,128)(2,1)} %get-tuple-element.356.refs_0_), channel_id=1, source_target_pairs={{0,8},{4,12},{8,0},{12,4},{16,24},{20,28},{24,16},{28,20},{1,9},{5... | collective-permute-start | bytes 786440 | tf_op jit(solution)/shard_map/ppermute | solution.py:19
  28.2 9.4 %collective-permute-start.9 = (bf16[256,640]{1,0:T(8,128)(2,1)S(1)}, bf16[256,640]{1,0:T(8,128)(2,1)S(1)}, u32[]{:S(2)}, u32[]{:S(2)}) collective-permute-start(bf16[256,640]{1,0:T(8,128)(2,1)S(1)} %get-tuple-element.348.refs_4_), channel_id=1, source_target_pairs={{0,4},{4,0},{8,12},{12,8},{16,20},{20,16},{24,28},{28,24},{1,5},{5... | collective-permute-start | bytes 983048 | tf_op jit(solution)/shard_map/ppermute | solution.py:19
  29.9 11.8 %collective-permute-start.7 = (bf16[272,256]{1,0:T(8,128)(2,1)S(1)}, bf16[272,256]{1,0:T(8,128)(2,1)S(1)}, u32[]{:S(2)}, u32[]{:S(2)}) collective-permute-start(bf16[272,256]{1,0:T(8,128)(2,1)S(1)} %pad_maximum_fusion.15), channel_id=1, source_target_pairs={{0,8},{4,12},{8,0},{12,4},{16,24},{20,28},{24,16},{28,20},{1,9},{5... | collective-permute-start | bytes 417800 | tf_op jit(solution)/shard_map/ppermute | solution.py:19
  36.1 22.4 %collective-permute-start.11 = (bf16[512,512]{1,0:T(8,128)(2,1)}, bf16[512,512]{1,0:T(8,128)(2,1)}, u32[]{:S(2)}, u32[]{:S(2)}) collective-permute-start(bf16[512,512]{1,0:T(8,128)(2,1)} %constant_dynamic-update-slice_fusion.4), channel_id=1, source_target_pairs={{0,4},{4,0},{8,12},{12,8},{16,20},{20,16},{24,28},{28,24},{1,5},{5... | collective-permute-start | bytes 1572872 | tf_op jit(solution)/shard_map/ppermute | solution.py:19
  38.4 24.1 %collective-permute-start.12 = (bf16[512,640]{1,0:T(8,128)(2,1)}, bf16[512,640]{1,0:T(8,128)(2,1)}, u32[]{:S(2)}, u32[]{:S(2)}) collective-permute-start(bf16[512,640]{1,0:T(8,128)(2,1)} %constant_dynamic-update-slice_fusion.7), channel_id=1, source_target_pairs={{0,8},{4,12},{8,0},{12,4},{16,24},{20,28},{24,16},{28,20},{1,9},{5... | collective-permute-start | bytes 1966088 | tf_op jit(solution)/shard_map/ppermute | solution.py:19
  40.0 35.6 %collective-permute-start.13 = (bf16[128,1536]{0,1:T(8,128)(2,1)S(1)}, bf16[128,1536]{0,1:T(8,128)(2,1)S(1)}, u32[]{:S(2)}, u32[]{:S(2)}) collective-permute-start(bf16[128,1536]{0,1:T(8,128)(2,1)S(1)} %pad_maximum_fusion.11), channel_id=1, source_target_pairs={{0,16},{4,20},{8,24},{12,28},{16,0},{20,4},{24,8},{28,12},{1,17},{... | collective-permute-start | bytes 1179656 | tf_op jit(solution)/shard_map/ppermute | solution.py:19
  42.4 12.2 %collective-permute-start.10 = (bf16[544,256]{1,0:T(8,128)(2,1)}, bf16[544,256]{1,0:T(8,128)(2,1)S(1)}, u32[]{:S(2)}, u32[]{:S(2)}) collective-permute-start(bf16[544,256]{1,0:T(8,128)(2,1)} %pad_maximum_fusion.12), channel_id=1, source_target_pairs={{0,4},{4,0},{8,12},{12,8},{16,20},{20,16},{24,28},{28,24},{1,5},{5... | collective-permute-start | bytes 835592 | tf_op jit(solution)/shard_map/ppermute | solution.py:19
  47.3 15.2 %collective-permute-start.1 = (bf16[512,1024]{1,0:T(8,128)(2,1)}, bf16[512,1024]{1,0:T(8,128)(2,1)}, u32[]{:S(2)}, u32[]{:S(2)}) collective-permute-start(bf16[512,1024]{1,0:T(8,128)(2,1)} %pad_maximum_fusion.3.even), channel_id=1, source_target_pairs={{0,1},{1,0},{2,3},{3,2},{4,5},{5,4},{6,7},{7,6},{8,9},{9,8},{10,11... | collective-permute-start | bytes 3145736 | tf_op jit(solution)/shard_map/ppermute | solution.py:19
  54.6 17.0 %collective-permute-start.17 = (bf16[256,1024]{1,0:T(8,128)(2,1)S(1)}, bf16[256,1024]{1,0:T(8,128)(2,1)S(1)}, u32[]{:S(2)}, u32[]{:S(2)}) collective-permute-start(bf16[256,1024]{1,0:T(8,128)(2,1)S(1)} %broadcast_select_fusion.refs_0_), channel_id=1, source_target_pairs={{0,2},{1,3},{2,0},{3,1},{4,6},{5,7},{6,4},{7,5},{8,10},{9,11},{10,... | collective-permute-start | bytes 1572872 | tf_op jit(solution)/shard_map/ppermute | solution.py:19
  58.4 17.1 %collective-permute-start.15 = (bf16[128,512]{1,0:T(8,128)(2,1)S(1)}, bf16[128,512]{1,0:T(8,128)(2,1)S(1)}, u32[]{:S(2)}, u32[]{:S(2)}) collective-permute-start(bf16[128,512]{1,0:T(8,128)(2,1)S(1)} %pad_maximum_fusion.16), channel_id=1, source_target_pairs={{0,16},{4,20},{8,24},{12,28},{16,0},{20,4},{24,8},{28,12},{1,17},{... | collective-permute-start | bytes 393224 | tf_op jit(solution)/shard_map/ppermute | solution.py:19
  72.8 17.8 %collective-permute-start.18 = (bf16[512,1024]{1,0:T(8,128)(2,1)}, bf16[512,1024]{1,0:T(8,128)(2,1)S(1)}, u32[]{:S(2)}, u32[]{:S(2)}) collective-permute-start(bf16[512,1024]{1,0:T(8,128)(2,1)} %pad_maximum_fusion.1), channel_id=1, source_target_pairs={{0,1},{1,0},{2,3},{3,2},{4,5},{5,4},{6,7},{7,6},{8,9},{9,8},{10,11... | collective-permute-start | bytes 3145736 | tf_op jit(solution)/shard_map/ppermute | solution.py:19
  76.3 10.9 %collective-permute-start.16 = (bf16[256,512]{1,0:T(8,128)(2,1)S(1)}, bf16[256,512]{1,0:T(8,128)(2,1)S(1)}, u32[]{:S(2)}, u32[]{:S(2)}) collective-permute-start(bf16[256,512]{1,0:T(8,128)(2,1)S(1)} %get-tuple-element.351.refs_0_), channel_id=1, source_target_pairs={{0,4},{4,0},{8,12},{12,8},{16,20},{20,16},{24,28},{28,24},{1,5},{5... | collective-permute-start | bytes 786440 | tf_op jit(solution)/shard_map/ppermute | solution.py:19
  79.9 23.0 %collective-permute-start.14 = (bf16[256,1536]{0,1:T(8,128)(2,1)}, bf16[256,1536]{0,1:T(8,128)(2,1)}, u32[]{:S(2)}, u32[]{:S(2)}) collective-permute-start(bf16[256,1536]{0,1:T(8,128)(2,1)} %get-tuple-element.342), channel_id=1, source_target_pairs={{0,8},{4,12},{8,0},{12,4},{16,24},{20,28},{24,16},{28,20},{1,9},{5... | collective-permute-start | bytes 2359304 | tf_op jit(solution)/shard_map/ppermute | solution.py:19
  79.9 23.0 %collective-permute-start.19 = (bf16[256,1536]{0,1:T(8,128)(2,1)}, bf16[256,1536]{0,1:T(8,128)(2,1)S(1)}, u32[]{:S(2)}, u32[]{:S(2)}) collective-permute-start(bf16[256,1536]{0,1:T(8,128)(2,1)} %get-tuple-element.342), channel_id=1, source_target_pairs={{0,4},{4,0},{8,12},{12,8},{16,20},{20,16},{24,28},{28,24},{1,5},{5... | collective-permute-start | bytes 2359304 | tf_op jit(solution)/shard_map/ppermute | solution.py:19
  88.0 23.0 %collective-permute-start.20 = (bf16[512,512]{1,0:T(8,128)(2,1)}, bf16[512,512]{1,0:T(8,128)(2,1)S(1)}, u32[]{:S(2)}, u32[]{:S(2)}) collective-permute-start(bf16[512,512]{1,0:T(8,128)(2,1)} %constant_dynamic-update-slice_fusion.14), channel_id=1, source_target_pairs={{0,8},{4,12},{8,0},{12,4},{16,24},{20,28},{24,16},{28,20},{1,9},{5... | collective-permute-start | bytes 1572872 | tf_op jit(solution)/shard_map/ppermute | solution.py:19
  118.2 20.1 %collective-permute-start.23 = (bf16[256,1536]{0,1:T(8,128)(2,1)}, bf16[256,1536]{0,1:T(8,128)(2,1)S(1)}, u32[]{:S(2)}, u32[]{:S(2)}) collective-permute-start(bf16[256,1536]{0,1:T(8,128)(2,1)} %collective-permute-done.14), channel_id=1, source_target_pairs={{0,4},{4,0},{8,12},{12,8},{16,20},{20,16},{24,28},{28,24},{1,5},{5... | collective-permute-start | bytes 2359304 | tf_op jit(solution)/shard_map/ppermute | solution.py:19
  123.1 16.9 %collective-permute-start.22 = (bf16[256,1024]{1,0:T(8,128)(2,1)S(1)}, bf16[256,1024]{1,0:T(8,128)(2,1)S(1)}, u32[]{:S(2)}, u32[]{:S(2)}) collective-permute-start(bf16[256,1024]{1,0:T(8,128)(2,1)S(1)} %get-tuple-element.332), channel_id=1, source_target_pairs={{0,2},{1,3},{2,0},{3,1},{4,6},{5,7},{6,4},{7,5},{8,10},{9,11},{10,... | collective-permute-start | bytes 1572872 | tf_op jit(solution)/shard_map/ppermute | solution.py:19
  138.4 13.5 %collective-permute-start.25 = (bf16[256,1024]{1,0:T(8,128)(2,1)S(1)}, bf16[256,1024]{1,0:T(8,128)(2,1)S(1)}, u32[]{:S(2)}, u32[]{:S(2)}) collective-permute-start(bf16[256,1024]{1,0:T(8,128)(2,1)S(1)} %get-tuple-element.331), channel_id=1, source_target_pairs={{0,2},{1,3},{2,0},{3,1},{4,6},{5,7},{6,4},{7,5},{8,10},{9,11},{10,... | collective-permute-start | bytes 1572872 | tf_op jit(solution)/shard_map/ppermute | solution.py:19
  140.5 12.6 %collective-permute-start.24 = (bf16[256,1024]{1,0:T(8,128)(2,1)S(1)}, bf16[256,1024]{1,0:T(8,128)(2,1)S(1)}, u32[]{:S(2)}, u32[]{:S(2)}) collective-permute-start(bf16[256,1024]{1,0:T(8,128)(2,1)S(1)} %multiply_convert_fusion.5.refs_0_), channel_id=1, source_target_pairs={{0,1},{1,0},{2,3},{3,2},{4,5},{5,4},{6,7},{7,6},{8,9},{9,8},{10,11... | collective-permute-start | bytes 1572872 | tf_op jit(solution)/shard_map/ppermute | solution.py:19
  153.0 5.4 %collective-permute-start.26 = (bf16[256,1024]{1,0:T(8,128)(2,1)S(1)}, bf16[256,1024]{1,0:T(8,128)(2,1)S(1)}, u32[]{:S(2)}, u32[]{:S(2)}) collective-permute-start(bf16[256,1024]{1,0:T(8,128)(2,1)S(1)} %multiply_convert_fusion.3.refs_4_), channel_id=1, source_target_pairs={{0,1},{1,0},{2,3},{3,2},{4,5},{5,4},{6,7},{7,6},{8,9},{9,8},{10,11... | collective-permute-start | bytes 1572872 | tf_op jit(solution)/shard_map/ppermute | solution.py:19
  164.4 20.5 %collective-permute-start.33 = (bf16[256,1024]{1,0:T(8,128)(2,1)}, bf16[256,1024]{1,0:T(8,128)(2,1)}, u32[]{:S(2)}, u32[]{:S(2)}) collective-permute-start(bf16[256,1024]{1,0:T(8,128)(2,1)} %fusion.17), channel_id=1, source_target_pairs={{0,2},{1,3},{2,0},{3,1},{4,6},{5,7},{6,4},{7,5},{8,10},{9,11},{10,... | collective-permute-start | bytes 1572872 | tf_op jit(solution)/shard_map/ppermute | solution.py:19
  167.3 23.0 %collective-permute-start.29 = (bf16[256,1024]{1,0:T(8,128)(2,1)}, bf16[256,1024]{1,0:T(8,128)(2,1)}, u32[]{:S(2)}, u32[]{:S(2)}) collective-permute-start(bf16[256,1024]{1,0:T(8,128)(2,1)} %fusion.16), channel_id=1, source_target_pairs={{0,2},{1,3},{2,0},{3,1},{4,6},{5,7},{6,4},{7,5},{8,10},{9,11},{10,... | collective-permute-start | bytes 1572872 | tf_op jit(solution)/shard_map/ppermute | solution.py:19
  177.0 32.2 %collective-permute-start.31 = (bf16[512,512]{1,0:T(8,128)(2,1)}, bf16[512,512]{1,0:T(8,128)(2,1)}, u32[]{:S(2)}, u32[]{:S(2)}) collective-permute-start(bf16[512,512]{1,0:T(8,128)(2,1)} %get-tuple-element.166), channel_id=1, source_target_pairs={{0,8},{4,12},{8,0},{12,4},{16,24},{20,28},{24,16},{28,20},{1,9},{5... | collective-permute-start | bytes 1572872 | tf_op jit(solution)/shard_map/ppermute | solution.py:19
  184.2 36.7 %collective-permute-start.38 = (bf16[512,1024]{1,0:T(8,128)(2,1)}, bf16[512,1024]{1,0:T(8,128)(2,1)}, u32[]{:S(2)}, u32[]{:S(2)}) collective-permute-start(bf16[512,1024]{1,0:T(8,128)(2,1)} %get-tuple-element.168), channel_id=1, source_target_pairs={{0,4},{4,0},{8,12},{12,8},{16,20},{20,16},{24,28},{28,24},{1,5},{5... | collective-permute-start | bytes 3145736 | tf_op jit(solution)/shard_map/ppermute | solution.py:19
  196.4 5.2 %collective-permute-start.32 = (bf16[256,1024]{1,0:T(8,128)(2,1)S(1)}, bf16[256,1024]{1,0:T(8,128)(2,1)S(1)}, u32[]{:S(2)}, u32[]{:S(2)}) collective-permute-start(bf16[256,1024]{1,0:T(8,128)(2,1)S(1)} %get-tuple-element.309.g0.refs_0_), channel_id=1, source_target_pairs={{0,1},{1,0},{2,3},{3,2},{4,5},{5,4},{6,7},{7,6},{8,9},{9,8},{10,11... | collective-permute-start | bytes 1572872 | tf_op jit(solution)/shard_map/ppermute | solution.py:19
  201.5 26.0 %collective-permute-start.30 = (bf16[512,1024]{1,0:T(8,128)(2,1)}, bf16[512,1024]{1,0:T(8,128)(2,1)}, u32[]{:S(2)}, u32[]{:S(2)}) collective-permute-start(bf16[512,1024]{1,0:T(8,128)(2,1)} %pad_maximum_fusion.6), channel_id=1, source_target_pairs={{0,1},{1,0},{2,3},{3,2},{4,5},{5,4},{6,7},{7,6},{8,9},{9,8},{10,11... | collective-permute-start | bytes 3145736 | tf_op jit(solution)/shard_map/ppermute | solution.py:19
  210.4 13.2 %collective-permute-start.36 = (bf16[256,512]{1,0:T(8,128)(2,1)S(1)}, bf16[256,512]{1,0:T(8,128)(2,1)}, u32[]{:S(2)}, u32[]{:S(2)}) collective-permute-start(bf16[256,512]{1,0:T(8,128)(2,1)S(1)} %get-tuple-element.328), channel_id=1, source_target_pairs={{0,4},{4,0},{8,12},{12,8},{16,20},{20,16},{24,28},{28,24},{1,5},{5... | collective-permute-start | bytes 786440 | tf_op jit(solution)/shard_map/ppermute | solution.py:19
  223.3 18.6 %collective-permute-start.39 = (bf16[256,1024]{1,0:T(8,128)(2,1)S(1)}, bf16[256,1024]{1,0:T(8,128)(2,1)}, u32[]{:S(2)}, u32[]{:S(2)}) collective-permute-start(bf16[256,1024]{1,0:T(8,128)(2,1)S(1)} %get-tuple-element.318), channel_id=1, source_target_pairs={{0,8},{4,12},{8,0},{12,4},{16,24},{20,28},{24,16},{28,20},{1,9},{5... | collective-permute-start | bytes 1572872 | tf_op jit(solution)/shard_map/ppermute | solution.py:19
  225.2 42.2 %collective-permute-start.37 = (bf16[128,512]{1,0:T(8,128)(2,1)}, bf16[128,512]{1,0:T(8,128)(2,1)S(1)}, u32[]{:S(2)}, u32[]{:S(2)}) collective-permute-start(bf16[128,512]{1,0:T(8,128)(2,1)} %fusion.48), channel_id=1, source_target_pairs={{0,16},{4,20},{8,24},{12,28},{16,0},{20,4},{24,8},{28,12},{1,17},{... | collective-permute-start | bytes 393224 | tf_op jit(solution)/shard_map/ppermute | solution.py:19
  242.9 26.3 %collective-permute-start.40 = (bf16[128,1024]{1,0:T(8,128)(2,1)S(1)}, bf16[128,1024]{1,0:T(8,128)(2,1)S(1)}, u32[]{:S(2)}, u32[]{:S(2)}) collective-permute-start(bf16[128,1024]{1,0:T(8,128)(2,1)S(1)} %fusion.42), channel_id=1, source_target_pairs={{0,16},{4,20},{8,24},{12,28},{16,0},{20,4},{24,8},{28,12},{1,17},{... | collective-permute-start | bytes 786440 | tf_op jit(solution)/shard_map/ppermute | solution.py:19
  243.6 36.9 %collective-permute-start.41 = (bf16[512,1152]{1,0:T(8,128)(2,1)}, bf16[512,1152]{1,0:T(8,128)(2,1)}, u32[]{:S(2)}, u32[]{:S(2)}) collective-permute-start(bf16[512,1152]{1,0:T(8,128)(2,1)} %get-tuple-element.186), channel_id=1, source_target_pairs={{0,4},{4,0},{8,12},{12,8},{16,20},{20,16},{24,28},{28,24},{1,5},{5... | collective-permute-start | bytes 3538952 | tf_op jit(solution)/shard_map/ppermute | solution.py:19
  245.1 64.7 %collective-permute-start.35 = (bf16[256,1024]{1,0:T(8,128)(2,1)}, bf16[256,1024]{1,0:T(8,128)(2,1)}, u32[]{:S(2)}, u32[]{:S(2)}) collective-permute-start(bf16[256,1024]{1,0:T(8,128)(2,1)} %slice.490), channel_id=1, source_target_pairs={{0,2},{1,3},{2,0},{3,1},{4,6},{5,7},{6,4},{7,5},{8,10},{9,11},{10,... | collective-permute-start | bytes 1572872 | tf_op jit(solution)/shard_map/ppermute | solution.py:19
  276.3 19.7 %collective-permute-start.43 = (bf16[512,512]{1,0:T(8,128)(2,1)}, bf16[512,512]{1,0:T(8,128)(2,1)}, u32[]{:S(2)}, u32[]{:S(2)}) collective-permute-start(bf16[512,512]{1,0:T(8,128)(2,1)} %get-tuple-element.195), channel_id=1, source_target_pairs={{0,4},{4,0},{8,12},{12,8},{16,20},{20,16},{24,28},{28,24},{1,5},{5... | collective-permute-start | bytes 1572872 | tf_op jit(solution)/shard_map/ppermute | solution.py:19
  283.4 17.7 %collective-permute-start.44 = (bf16[256,1152]{1,0:T(8,128)(2,1)}, bf16[256,1152]{1,0:T(8,128)(2,1)}, u32[]{:S(2)}, u32[]{:S(2)}) collective-permute-start(bf16[256,1152]{1,0:T(8,128)(2,1)} %get-tuple-element.316), channel_id=1, source_target_pairs={{0,8},{4,12},{8,0},{12,4},{16,24},{20,28},{24,16},{28,20},{1,9},{5... | collective-permute-start | bytes 1769480 | tf_op jit(solution)/shard_map/ppermute | solution.py:19
  294.3 10.9 %collective-permute-start.42 = (bf16[512,1024]{1,0:T(8,128)(2,1)}, bf16[512,1024]{1,0:T(8,128)(2,1)}, u32[]{:S(2)}, u32[]{:S(2)}) collective-permute-start(bf16[512,1024]{1,0:T(8,128)(2,1)} %get-tuple-element.201), channel_id=1, source_target_pairs={{0,1},{1,0},{2,3},{3,2},{4,5},{5,4},{6,7},{7,6},{8,9},{9,8},{10,11... | collective-permute-start | bytes 3145736 | tf_op jit(solution)/shard_map/ppermute | solution.py:19
  296.9 10.6 %collective-permute-start.46 = (f32[528,256]{1,0:T(8,128)}, f32[528,256]{1,0:T(8,128)}, u32[]{:S(2)}, u32[]{:S(2)}) collective-permute-start(f32[528,256]{1,0:T(8,128)} %pad_maximum_fusion.8), channel_id=1, source_target_pairs={{0,1},{1,0},{2,3},{3,2},{4,5},{5,4},{6,7},{7,6},{8,9},{9,8},{10,11... | collective-permute-start | bytes 1622024 | tf_op jit(solution)/shard_map/ppermute | solution.py:19
  299.8 16.5 %collective-permute-start.48 = (bf16[256,512]{1,0:T(8,128)(2,1)}, bf16[256,512]{1,0:T(8,128)(2,1)}, u32[]{:S(2)}, u32[]{:S(2)}) collective-permute-start(bf16[256,512]{1,0:T(8,128)(2,1)} %get-tuple-element.326), channel_id=1, source_target_pairs={{0,8},{4,12},{8,0},{12,4},{16,24},{20,28},{24,16},{28,20},{1,9},{5... | collective-permute-start | bytes 786440 | tf_op jit(solution)/shard_map/ppermute | solution.py:19
  302.9 28.1 %collective-permute-start.45 = (bf16[128,1152]{1,0:T(8,128)(2,1)}, bf16[128,1152]{1,0:T(8,128)(2,1)}, u32[]{:S(2)}, u32[]{:S(2)}) collective-permute-start(bf16[128,1152]{1,0:T(8,128)(2,1)} %fusion.39), channel_id=1, source_target_pairs={{0,16},{4,20},{8,24},{12,28},{16,0},{20,4},{24,8},{28,12},{1,17},{... | collective-permute-start | bytes 884744 | tf_op jit(solution)/shard_map/ppermute | solution.py:19
  310.8 9.0 %collective-permute-start.47 = (f32[272,256]{1,0:T(8,128)}, f32[272,256]{1,0:T(8,128)S(1)}, u32[]{:S(2)}, u32[]{:S(2)}) collective-permute-start(f32[272,256]{1,0:T(8,128)} %pad_maximum_fusion.13), channel_id=1, source_target_pairs={{0,2},{1,3},{2,0},{3,1},{4,6},{5,7},{6,4},{7,5},{8,10},{9,11},{10,... | collective-permute-start | bytes 835592 | tf_op jit(solution)/shard_map/ppermute | solution.py:19
  316.3 14.0 %collective-permute-start.50 = (bf16[256,1024]{1,0:T(8,128)(2,1)}, bf16[256,1024]{1,0:T(8,128)(2,1)S(1)}, u32[]{:S(2)}, u32[]{:S(2)}) collective-permute-start(bf16[256,1024]{1,0:T(8,128)(2,1)} %slice.504), channel_id=1, source_target_pairs={{0,2},{1,3},{2,0},{3,1},{4,6},{5,7},{6,4},{7,5},{8,10},{9,11},{10,... | collective-permute-start | bytes 1572872 | tf_op jit(solution)/shard_map/ppermute | solution.py:19
  318.8 7.8 %collective-permute-start.51 = (bf16[128,512]{1,0:T(8,128)(2,1)S(1)}, bf16[128,512]{1,0:T(8,128)(2,1)S(1)}, u32[]{:S(2)}, u32[]{:S(2)}) collective-permute-start(bf16[128,512]{1,0:T(8,128)(2,1)S(1)} %fusion.46), channel_id=1, source_target_pairs={{0,16},{4,20},{8,24},{12,28},{16,0},{20,4},{24,8},{28,12},{1,17},{... | collective-permute-start | bytes 393224 | tf_op jit(solution)/shard_map/ppermute | solution.py:19
  320.6 8.3 %collective-permute-start.49 = (f32[152,256]{1,0:T(8,128)S(1)}, f32[152,256]{1,0:T(8,128)S(1)}, u32[]{:S(2)}, u32[]{:S(2)}) collective-permute-start(f32[152,256]{1,0:T(8,128)S(1)} %pad_maximum_fusion.14), channel_id=1, source_target_pairs={{0,4},{4,0},{8,12},{12,8},{16,20},{20,16},{24,28},{28,24},{1,5},{5... | collective-permute-start | bytes 466952 | tf_op jit(solution)/shard_map/ppermute | solution.py:19
  337.4 6.8 %collective-permute-start.53 = (f32[56,256]{1,0:T(8,128)S(1)}, f32[56,256]{1,0:T(8,128)S(1)}, u32[]{:S(2)}, u32[]{:S(2)}) collective-permute-start(f32[56,256]{1,0:T(8,128)S(1)} %pad_maximum_fusion.19), channel_id=1, source_target_pairs={{0,16},{4,20},{8,24},{12,28},{16,0},{20,4},{24,8},{28,12},{1,17},{... | collective-permute-start | bytes 172040 | tf_op jit(solution)/shard_map/ppermute | solution.py:19
  (84 other events, 622.4 us)
